TPU v7x, 32 devices: a whole 2x2x4 slice. The times are simulated.
32 devices in a mesh: fsdp: 2 (over x), context: 4 (over y, core), tensor: 4 (over z).
Axes of the slice: x: 2, y: 2, z: 4, core: 2. Of those that a mesh axis runs over, the one named last changes fastest.
Arguments:
- hidden_in: bfloat16 [2, 1024, 2048], P('fsdp', ('context', 'tensor')), may hold values from -6 to 6
- segment_ids: int32 [2, 1024], P('fsdp'), may hold values from 0 to 15, never falling along the last dimension, each value on 1 to 512 neighbouring positions
- pad_mask: int32 [2, 1024], P('fsdp'), may hold values from 0 to 1, as said below
- attn_gain: bfloat16 [2048], P(('fsdp', 'context')), may hold values from 0.5 to 1.5
- w_query: bfloat16 [2048, 2048], P(('fsdp', 'context'), 'tensor'), may hold values from -0.1875 to 0.1875
- w_key: bfloat16 [2048, 256], P(('fsdp', 'context'), 'tensor'), may hold values from -0.1875 to 0.1875
- w_value: bfloat16 [2048, 256], P(('fsdp', 'context'), 'tensor'), may hold values from -0.125 to 0.125
- w_out: bfloat16 [2048, 2048], P('tensor', ('fsdp', 'context')), may hold values from -0.5 to 0.5
- mlp_gain: bfloat16 [2048], P(('fsdp', 'context')), may hold values from 0.5 to 1.5
- w_gate: bfloat16 [2048, 5632], P(('fsdp', 'context'), 'tensor'), may hold values from -0.125 to 0.125
- w_up: bfloat16 [2048, 5632], P(('fsdp', 'context'), 'tensor'), may hold values from -0.125 to 0.125
- w_down: bfloat16 [5632, 2048], P('tensor', ('fsdp', 'context')), may hold values from -0.078125 to 0.078125
- cotangent: bfloat16 [2, 1024, 2048], P('fsdp', ('context', 'tensor')), may hold values from -6 to 6
Outputs:
- block_out: bfloat16 [2, 1024, 2048], P('fsdp', ('context', 'tensor'))
- grad_hidden: float32 [2, 1024, 2048], P('fsdp', ('context', 'tensor'))
- grad_attn_gain: float32 [2048], P(('fsdp', 'context'))
- grad_query: float32 [2048, 2048], P(('fsdp', 'context'), 'tensor')
- grad_key: float32 [2048, 256], P(('fsdp', 'context'), 'tensor')
- grad_value: float32 [2048, 256], P(('fsdp', 'context'), 'tensor')
- grad_out: float32 [2048, 2048], P('tensor', ('fsdp', 'context'))
- grad_mlp_gain: float32 [2048], P(('fsdp', 'context'))
- grad_gate: float32 [2048, 5632], P(('fsdp', 'context'), 'tensor')
- grad_up: float32 [2048, 5632], P(('fsdp', 'context'), 'tensor')
- grad_down: float32 [5632, 2048], P('tensor', ('fsdp', 'context'))
Inputs may be any that keep to these rules, and one draw needn't show every extreme that they name: `segment_ids`: ids never fall along a sequence; a document is a run of 1 to 512 consecutive tokens of one id. `pad_mask`: every sequence ends in one or more padding slots, and no other slot is padding.
All inputs are finite; a program needn't handle non-finite values.
Results may differ from a plain program's by a relative error of at most 0.013.
The roundings to bfloat16 on the way count: a program that leaves them out, or rounds other values in their place, can miss the bound.
Values may be sent and summed in bfloat16 or wider, within the bound.
A program may use at most 88 MiB of HBM per device.

v0:
```python
import math

import jax
import jax.numpy as jnp
from jax import lax
from jax.sharding import PartitionSpec as P

EPS = 1e-05
NEG = -1e30


def positions_of(segments):
    length = segments.shape[1]
    columns = jnp.arange(length, dtype=jnp.int32)[None, :]
    previous = jnp.concatenate(
        [jnp.full((segments.shape[0], 1), -1, jnp.int32), segments[:, :-1]], axis=1
    )
    starts = jnp.where(segments != previous, columns, jnp.zeros_like(columns))
    return columns - lax.cummax(starts, axis=1)


def rope_tables(positions, head_size):
    half_size = head_size // 2
    frequency = jnp.exp(
        -(jnp.arange(half_size, dtype=jnp.float32) * (2.0 / head_size)) * math.log(10000.0)
    )
    angles = positions.astype(jnp.float32)[..., None] * frequency
    return (jnp.cos(angles)[..., None, :], jnp.sin(angles)[..., None, :])


def rotate(vectors, cos_table, sin_table):
    half_size = vectors.shape[-1] // 2
    first_half = vectors[..., :half_size]
    second_half = vectors[..., half_size:]
    return jnp.concatenate(
        [
            first_half * cos_table - second_half * sin_table,
            second_half * cos_table + first_half * sin_table,
        ],
        axis=-1,
    )


def allowed_of(seg_row, pad_row):
    length = seg_row.shape[0]
    columns = jnp.arange(length, dtype=jnp.int32)
    same_doc = seg_row[:, None] == seg_row[None, :]
    causal = columns[None, :] <= columns[:, None]
    live_key = (pad_row[None, :] == 1) | (columns[:, None] == columns[None, :])
    return same_doc & causal & live_key


def matmul(left_side, right_side):
    return jnp.dot(left_side, right_side, preferred_element_type=jnp.float32)


def matmul_left_t(left_side, right_side):
    return lax.dot_general(
        left_side, right_side, (((0,), (0,)), ((), ())), preferred_element_type=jnp.float32
    )


def matmul_right_t(left_side, right_side):
    return lax.dot_general(
        left_side, right_side, (((1,), (1,)), ((), ())), preferred_element_type=jnp.float32
    )


def rows_gather(activations):
    return lax.all_gather(activations, "tensor", axis=1, tiled=True)


def rows_sum(partials):
    return lax.psum_scatter(partials, "tensor", scatter_dimension=1, tiled=True)


def to_heads(by_rows):
    return lax.all_to_all(by_rows, "context", split_axis=2, concat_axis=1, tiled=True)


def to_spans(by_heads):
    return lax.all_to_all(by_heads, "context", split_axis=1, concat_axis=2, tiled=True)


def norm_back(grad_normed, vectors, inv_scale, gain_row):
    unit_rows = vectors * inv_scale
    weighted = grad_normed * gain_row.astype(jnp.float32)
    grad_gain = jnp.sum(grad_normed * unit_rows, axis=(0, 1))
    grad_vectors = inv_scale * (
        weighted - unit_rows * jnp.mean(weighted * unit_rows, axis=-1, keepdims=True)
    )
    return (grad_vectors, grad_gain)


def attend_scores(query_rows, kv_rows, seg_row, pad_row):
    length = query_rows.shape[0]
    head_size = kv_rows.shape[1] // 2
    query_heads = query_rows.reshape(length, -1, head_size)
    key_rows = kv_rows[:, :head_size]
    value_rows = kv_rows[:, head_size:]
    scores = jnp.einsum(
        "qhd,td->hqt", query_heads, key_rows, preferred_element_type=jnp.float32
    ) * head_size ** (-0.5)
    scores = jnp.where(allowed_of(seg_row, pad_row)[None], scores, NEG)
    return (query_heads, key_rows, value_rows, scores)


def attend_forward(packed_item):
    query_rows, kv_rows, seg_row, pad_row = packed_item
    query_heads, key_rows, value_rows, scores = attend_scores(query_rows, kv_rows, seg_row, pad_row)
    row_max = jnp.max(scores, axis=-1, keepdims=True)
    exp_scores = jnp.exp(scores - row_max)
    row_total = jnp.sum(exp_scores, axis=-1, keepdims=True)
    weights = exp_scores / row_total
    output = jnp.einsum(
        "hqt,td->qhd", weights.astype(jnp.bfloat16), value_rows, preferred_element_type=jnp.float32
    )
    output = output.reshape(query_rows.shape[0], -1).astype(jnp.bfloat16)
    return (output, (row_max + jnp.log(row_total))[..., 0])


def attend_backward(packed_item):
    query_rows, kv_rows, grad_rows, log_total, seg_row, pad_row = packed_item
    query_heads, key_rows, value_rows, scores = attend_scores(query_rows, kv_rows, seg_row, pad_row)
    head_size = key_rows.shape[1]
    scale = head_size ** (-0.5)
    weights = jnp.exp(scores - log_total[..., None])
    grad_heads = grad_rows.reshape(query_heads.shape)
    grad_weights = jnp.einsum(
        "qhd,td->hqt", grad_heads, value_rows, preferred_element_type=jnp.float32
    )
    row_delta = jnp.sum(weights * grad_weights, axis=-1, keepdims=True)
    grad_scores = (weights * (grad_weights - row_delta)).astype(jnp.bfloat16)
    grad_queries = (
        jnp.einsum("hqt,td->qhd", grad_scores, key_rows, preferred_element_type=jnp.float32) * scale
    )
    grad_keys = (
        jnp.einsum("hqt,qhd->td", grad_scores, query_heads, preferred_element_type=jnp.float32)
        * scale
    )
    grad_values = jnp.einsum(
        "hqt,qhd->td", weights.astype(jnp.bfloat16), grad_heads, preferred_element_type=jnp.float32
    )
    return (grad_queries, jnp.concatenate([grad_keys, grad_values], axis=-1))


def forward_pass(params, tables):
    hidden_in, attn_gain, w_query, w_key, w_value, w_out, mlp_gain, w_gate, w_up, w_down = params
    cos_span, sin_span, segment_ids, pad_mask, keep_rows = tables
    gain_one, query_all, key_all, value_all, out_all = (
        lax.all_gather(attn_gain, ("fsdp", "context"), axis=0, tiled=True),
        lax.all_gather(w_query, ("fsdp", "context"), axis=0, tiled=True),
        lax.all_gather(w_key, ("fsdp", "context"), axis=0, tiled=True),
        lax.all_gather(w_value, ("fsdp", "context"), axis=0, tiled=True),
        lax.all_gather(w_out, ("fsdp", "context"), axis=1, tiled=True),
    )
    seq_count, row_count, model_width = hidden_in.shape
    head_size = key_all.shape[1]
    hidden_f = hidden_in.astype(jnp.float32)
    scale_one = lax.rsqrt(jnp.mean(hidden_f * hidden_f, axis=-1, keepdims=True) + EPS)
    normed_one = rows_gather(
        (hidden_f * scale_one * gain_one.astype(jnp.float32)).astype(jnp.bfloat16)
    )
    span_len = normed_one.shape[1]
    flat_one = normed_one.reshape(-1, model_width)
    query_pre = matmul(flat_one, query_all).reshape(seq_count, span_len, -1, head_size)
    queries = (
        rotate(query_pre, cos_span, sin_span).astype(jnp.bfloat16).reshape(seq_count, span_len, -1)
    )
    key_pre = matmul(flat_one, key_all).reshape(seq_count, span_len, 1, head_size)
    key_rows = (
        rotate(key_pre, cos_span, sin_span)
        .astype(jnp.bfloat16)
        .reshape(seq_count, span_len, head_size)
    )
    value_rows = (
        matmul(flat_one, value_all).astype(jnp.bfloat16).reshape(seq_count, span_len, head_size)
    )
    query_full = to_heads(queries)
    kv_full = lax.all_gather(
        jnp.concatenate([key_rows, value_rows], axis=-1), "context", axis=1, tiled=True
    )
    attn_full, log_total = lax.map(attend_forward, (query_full, kv_full, segment_ids, pad_mask))
    out_span = to_spans(attn_full)
    out_flat = out_span.reshape(-1, out_span.shape[2])
    branch_one = rows_sum(matmul(out_flat, out_all).reshape(seq_count, span_len, model_width))
    middle = hidden_f + branch_one
    gain_two, gate_all, up_all, down_all = (
        lax.all_gather(mlp_gain, ("fsdp", "context"), axis=0, tiled=True),
        lax.all_gather(w_gate, ("fsdp", "context"), axis=0, tiled=True),
        lax.all_gather(w_up, ("fsdp", "context"), axis=0, tiled=True),
        lax.all_gather(w_down, ("fsdp", "context"), axis=1, tiled=True),
    )
    scale_two = lax.rsqrt(jnp.mean(middle * middle, axis=-1, keepdims=True) + EPS)
    normed_two = rows_gather(
        (middle * scale_two * gain_two.astype(jnp.float32)).astype(jnp.bfloat16)
    )
    flat_two = normed_two.reshape(-1, model_width)
    gate_rows = matmul(flat_two, gate_all)
    up_rows = matmul(flat_two, up_all)
    inner_rows = (jax.nn.silu(gate_rows) * up_rows).astype(jnp.bfloat16)
    branch_two = rows_sum(matmul(inner_rows, down_all).reshape(seq_count, span_len, model_width))
    block_out = (keep_rows * (middle + branch_two)).astype(jnp.bfloat16)
    return dict(
        block_out=block_out,
        gain_one=gain_one,
        query_all=query_all,
        key_all=key_all,
        value_all=value_all,
        out_all=out_all,
        gain_two=gain_two,
        gate_all=gate_all,
        up_all=up_all,
        down_all=down_all,
        hidden_f=hidden_f,
        scale_one=scale_one,
        flat_one=flat_one,
        query_full=query_full,
        kv_full=kv_full,
        log_total=log_total,
        out_flat=out_flat,
        middle=middle,
        scale_two=scale_two,
        flat_two=flat_two,
        gate_rows=gate_rows,
        up_rows=up_rows,
        inner_rows=inner_rows,
    )


def body(
    hidden_in,
    segment_ids,
    pad_mask,
    attn_gain,
    w_query,
    w_key,
    w_value,
    w_out,
    mlp_gain,
    w_gate,
    w_up,
    w_down,
    cotangent,
):
    seq_count, row_count, model_width = hidden_in.shape
    context_count = lax.axis_size("context")
    tensor_count = lax.axis_size("tensor")
    context_index = lax.axis_index("context")
    tensor_index = lax.axis_index("tensor")
    seq_length = segment_ids.shape[1]
    span_len = seq_length // context_count
    head_size = w_key.shape[1]
    cos_full, sin_full = rope_tables(positions_of(segment_ids), head_size)
    cos_span = lax.dynamic_slice_in_dim(cos_full, context_index * span_len, span_len, 1)
    sin_span = lax.dynamic_slice_in_dim(sin_full, context_index * span_len, span_len, 1)
    row_start = (context_index * tensor_count + tensor_index) * row_count
    keep_rows = lax.dynamic_slice_in_dim(pad_mask, row_start, row_count, 1).astype(jnp.float32)[
        ..., None
    ]
    tables = (cos_span, sin_span, segment_ids, pad_mask, keep_rows)
    params = (hidden_in, attn_gain, w_query, w_key, w_value, w_out, mlp_gain, w_gate, w_up, w_down)
    first_pass = forward_pass(params, tables)
    saved_state = forward_pass(lax.optimization_barrier(params), tables)
    grad_rows = cotangent.astype(jnp.float32) * keep_rows
    grad_down_in = rows_gather(grad_rows.astype(jnp.bfloat16)).reshape(-1, model_width)
    grad_down = matmul_left_t(saved_state["inner_rows"], grad_down_in)
    grad_inner = matmul_right_t(grad_down_in, saved_state["down_all"])
    gate_rows = saved_state["gate_rows"]
    sigmoid_gate = jax.nn.sigmoid(gate_rows)
    grad_gate_rows = (
        grad_inner
        * saved_state["up_rows"]
        * sigmoid_gate
        * (1.0 + gate_rows * (1.0 - sigmoid_gate))
    ).astype(jnp.bfloat16)
    grad_up_rows = (grad_inner * gate_rows * sigmoid_gate).astype(jnp.bfloat16)
    grad_gate = matmul_left_t(saved_state["flat_two"], grad_gate_rows)
    grad_up = matmul_left_t(saved_state["flat_two"], grad_up_rows)
    grad_gate, grad_up, grad_down = (
        lax.psum_scatter(grad_gate, ("fsdp", "context"), scatter_dimension=0, tiled=True),
        lax.psum_scatter(grad_up, ("fsdp", "context"), scatter_dimension=0, tiled=True),
        lax.psum_scatter(grad_down, ("fsdp", "context"), scatter_dimension=1, tiled=True),
    )
    grad_normed_two = matmul_right_t(grad_gate_rows, saved_state["gate_all"]) + matmul_right_t(
        grad_up_rows, saved_state["up_all"]
    )
    grad_normed_two = rows_sum(grad_normed_two.reshape(seq_count, span_len, model_width))
    grad_middle_norm, grad_gain_two = norm_back(
        grad_normed_two, saved_state["middle"], saved_state["scale_two"], saved_state["gain_two"]
    )
    grad_middle = grad_rows + grad_middle_norm
    grad_attn_in = rows_gather(grad_middle.astype(jnp.bfloat16)).reshape(-1, model_width)
    grad_out = matmul_left_t(saved_state["out_flat"], grad_attn_in)
    grad_attn_rows = matmul_right_t(grad_attn_in, saved_state["out_all"]).astype(jnp.bfloat16)
    grad_heads = to_heads(grad_attn_rows.reshape(seq_count, span_len, -1))
    grad_query_full, grad_kv_full = lax.map(
        attend_backward,
        (
            saved_state["query_full"],
            saved_state["kv_full"],
            grad_heads,
            saved_state["log_total"],
            segment_ids,
            pad_mask,
        ),
    )
    grad_query_full = (
        rotate(grad_query_full, cos_full, -sin_full)
        .astype(jnp.bfloat16)
        .reshape(seq_count, seq_length, -1)
    )
    grad_query_rows = to_spans(grad_query_full).reshape(seq_count * span_len, -1)
    grad_kv_span = lax.psum_scatter(grad_kv_full, "context", scatter_dimension=1, tiled=True)
    grad_key_rows = rotate(
        grad_kv_span[..., :head_size].reshape(seq_count, span_len, 1, head_size),
        cos_span,
        -sin_span,
    )
    grad_key_rows = grad_key_rows.astype(jnp.bfloat16).reshape(-1, head_size)
    grad_value_rows = grad_kv_span[..., head_size:].astype(jnp.bfloat16).reshape(-1, head_size)
    flat_one = saved_state["flat_one"]
    grad_query = matmul_left_t(flat_one, grad_query_rows)
    grad_key = matmul_left_t(flat_one, grad_key_rows)
    grad_value = matmul_left_t(flat_one, grad_value_rows)
    grad_normed_one = (
        matmul_right_t(grad_query_rows, saved_state["query_all"])
        + matmul_right_t(grad_key_rows, saved_state["key_all"])
        + matmul_right_t(grad_value_rows, saved_state["value_all"])
    )
    grad_normed_one = rows_sum(grad_normed_one.reshape(seq_count, span_len, model_width))
    grad_input_norm, grad_gain_one = norm_back(
        grad_normed_one, saved_state["hidden_f"], saved_state["scale_one"], saved_state["gain_one"]
    )
    grad_hidden = grad_middle + grad_input_norm
    grad_gain_one, grad_gain_two = lax.psum((grad_gain_one, grad_gain_two), "tensor")
    grad_gain_one, grad_query, grad_key, grad_value, grad_out, grad_gain_two = (
        lax.psum_scatter(grad_gain_one, ("fsdp", "context"), scatter_dimension=0, tiled=True),
        lax.psum_scatter(grad_query, ("fsdp", "context"), scatter_dimension=0, tiled=True),
        lax.psum_scatter(grad_key, ("fsdp", "context"), scatter_dimension=0, tiled=True),
        lax.psum_scatter(grad_value, ("fsdp", "context"), scatter_dimension=0, tiled=True),
        lax.psum_scatter(grad_out, ("fsdp", "context"), scatter_dimension=1, tiled=True),
        lax.psum_scatter(grad_gain_two, ("fsdp", "context"), scatter_dimension=0, tiled=True),
    )
    return (
        first_pass["block_out"],
        grad_hidden,
        grad_gain_one,
        grad_query,
        grad_key,
        grad_value,
        grad_out,
        grad_gain_two,
        grad_gate,
        grad_up,
        grad_down,
    )


def solution(mesh):
    in_specs = (
        P("fsdp", ("context", "tensor"), None),
        P("fsdp", None),
        P("fsdp", None),
        P(("fsdp", "context")),
        P(("fsdp", "context"), "tensor"),
        P(("fsdp", "context"), "tensor"),
        P(("fsdp", "context"), "tensor"),
        P("tensor", ("fsdp", "context")),
        P(("fsdp", "context")),
        P(("fsdp", "context"), "tensor"),
        P(("fsdp", "context"), "tensor"),
        P("tensor", ("fsdp", "context")),
        P("fsdp", ("context", "tensor"), None),
    )
    out_specs = (
        P("fsdp", ("context", "tensor"), None),
        P("fsdp", ("context", "tensor"), None),
        P(("fsdp", "context")),
        P(("fsdp", "context"), "tensor"),
        P(("fsdp", "context"), "tensor"),
        P(("fsdp", "context"), "tensor"),
        P("tensor", ("fsdp", "context")),
        P(("fsdp", "context")),
        P(("fsdp", "context"), "tensor"),
        P(("fsdp", "context"), "tensor"),
        P("tensor", ("fsdp", "context")),
    )
    return jax.shard_map(body, mesh=mesh, in_specs=in_specs, out_specs=out_specs, check_vma=False)
```

profile of v0, /device:TPU:0, one launch (start us, length us, event | category | flops | bytes accessed | tf_op | source)
XLA Modules:
  0.0 1386.3 jit_solution(9212681209821931771)
XLA Ops:
  9.0 10.3 all-gather.2
  23.4 8.8 all-gather
  37.4 9.1 all_gather.92
  46.5 9.6 all_gather.93
  65.9 13.0 all-gather.37.cloned.1.call-done
  82.9 25.8 %all-gather.23.cloned.1.call-done = bf16[2048,512]{1,0:T(8,128)(2,1)} async-done(((bf16[256,512]{1,0:T(8,128)(2,1)}), bf16[2048,512]{1,0:T(8,128)(2,1)}) %all-gather.23.cloned.1.call-update) | async-done | bytes 2097168 | tf_op jit(solution)/shard_map/all_gather | solution.py:152
  114.8 23.8 %all-gather.21.cloned.1.call-done = bf16[1,256,2048]{2,1,0:T(8,128)(2,1)} async-done(((bf16[1,64,2048]{2,1,0:T(8,128)(2,1)}), bf16[1,256,2048]{2,1,0:T(8,128)(2,1)}) %all-gather.21.cloned.1.call-update) | async-done | bytes 1048592 | tf_op jit(solution)/shard_map/all_gather | solution.py:70
  148.4 9.6 all_gather.94
  169.3 8.4 all_to_all.90
  182.1 8.8 all-gather.3
  191.0 35.0 %reduce-scatter.18.cloned.1.call-done = f32[1,64,2048]{2,1,0:T(8,128)} async-done(((f32[1,256,2048]{2,1,0:T(8,128)}), f32[1,64,2048]{2,1,0:T(8,128)}) %reduce-scatter.18.cloned.1.call-update) | async-done | bytes 524304 | tf_op jit(solution)/shard_map/reduce_scatter | solution.py:74
  233.9 22.6 %all-gather.45.cloned.1.call-done = bf16[1,256,2048]{2,1,0:T(8,128)(2,1)} async-done(((bf16[1,64,2048]{2,1,0:T(8,128)(2,1)}), bf16[1,256,2048]{2,1,0:T(8,128)(2,1)}) %all-gather.45.cloned.1.call-update) | async-done | bytes 1048592 | tf_op jit(solution)/shard_map/all_gather | solution.py:70
  256.5 44.9 %all-gather.47.cloned.1.call-done = bf16[2048,1408]{1,0:T(8,128)(2,1)} async-done(((bf16[256,1408]{1,0:T(8,128)(2,1)}), bf16[2048,1408]{1,0:T(8,128)(2,1)}) %all-gather.47.cloned.1.call-update) | async-done | bytes 5767184 | tf_op jit(solution)/shard_map/all_gather | solution.py:191
  301.4 5.9 fusion.40
  307.3 39.5 %all-gather.49.cloned.1.call-done = bf16[2048,1408]{1,0:T(8,128)(2,1)} async-done(((bf16[256,1408]{1,0:T(8,128)(2,1)}), bf16[2048,1408]{1,0:T(8,128)(2,1)}) %all-gather.49.cloned.1.call-update) | async-done | bytes 5767184 | tf_op jit(solution)/shard_map/all_gather | solution.py:190
  352.3 24.5 %all-gather.41.cloned.1.call-done = bf16[1,256,2048]{2,1,0:T(8,128)(2,1)} async-done(((bf16[1,64,2048]{2,1,0:T(8,128)(2,1)}), bf16[1,256,2048]{2,1,0:T(8,128)(2,1)}) %all-gather.41.cloned.1.call-update) | async-done | bytes 1048592 | tf_op jit(solution)/shard_map/all_gather | solution.py:70
  376.8 45.9 %all-gather.43.cloned.1.call-done = bf16[1408,2048]{1,0:T(8,128)(2,1)} async-done(((bf16[1408,256]{1,0:T(8,128)(2,1)}), bf16[1408,2048]{1,0:T(8,128)(2,1)}) %all-gather.43.cloned.1.call-update) | async-done | bytes 5767184 | tf_op jit(solution)/shard_map/all_gather | solution.py:192
  422.7 6.1 multiply_convert_fusion.1
  436.7 44.0 %reduce-scatter.20.cloned.1.call-done = f32[1,64,2048]{2,1,0:T(8,128)} async-done(((f32[1,256,2048]{2,1,0:T(8,128)}), f32[1,64,2048]{2,1,0:T(8,128)}) %reduce-scatter.20.cloned.1.call-update) | async-done | bytes 524304 | tf_op jit(solution)/shard_map/reduce_scatter | solution.py:74
  484.6 27.4 %all-gather.51.cloned.1.call-done = bf16[1,256,2048]{2,1,0:T(8,128)(2,1)} async-done(((bf16[1,64,2048]{2,1,0:T(8,128)(2,1)}), bf16[1,256,2048]{2,1,0:T(8,128)(2,1)}) %all-gather.51.cloned.1.call-update) | async-done | bytes 1048592 | tf_op jit(solution)/shard_map/all_gather | solution.py:70
  547.6 10.8 all_gather.80
  558.4 10.7 all_gather.81
  578.8 5.9 all-to-all-done
  587.1 7.3 all_gather.82
  594.4 6.5 fusion.117
  607.8 8.4 all_to_all.91
  621.1 9.3 all-gather.1
  630.5 33.1 %reduce-scatter.14.cloned.1.call-done = f32[1,64,2048]{2,1,0:T(8,128)} async-done(((f32[1,256,2048]{2,1,0:T(8,128)}), f32[1,64,2048]{2,1,0:T(8,128)}) %reduce-scatter.14.cloned.1.call-update) | async-done | bytes 524304 | tf_op jit(solution)/shard_map/reduce_scatter | solution.py:74
  680.1 10.2 all_to_all.92
  700.8 7.2 all-gather.29.cloned.1.call-done
  708.0 30.0 %all-gather.27.cloned.1.call-done = bf16[1,256,2048]{2,1,0:T(8,128)(2,1)} async-done(((bf16[1,64,2048]{2,1,0:T(8,128)(2,1)}), bf16[1,256,2048]{2,1,0:T(8,128)(2,1)}) %all-gather.27.cloned.1.call-update) | async-done | bytes 1048592 | tf_op jit(solution)/shard_map/all_gather | solution.py:70
  738.0 5.9 fusion.56
  743.9 38.8 %all-gather.31.cloned.1.call-done = bf16[2048,1408]{1,0:T(8,128)(2,1)} async-done(((bf16[256,1408]{1,0:T(8,128)(2,1)}), bf16[2048,1408]{1,0:T(8,128)(2,1)}) %all-gather.31.cloned.1.call-update) | async-done | bytes 5767184 | tf_op jit(solution)/shard_map/all_gather | solution.py:191
  782.7 46.1 %all-gather.33.cloned.1.call-done = bf16[1408,2048]{1,0:T(8,128)(2,1)} async-done(((bf16[1408,256]{1,0:T(8,128)(2,1)}), bf16[1408,2048]{1,0:T(8,128)(2,1)}) %all-gather.33.cloned.1.call-update) | async-done | bytes 5767184 | tf_op jit(solution)/shard_map/all_gather | solution.py:192
  828.8 9.5 convolution_bitcast_fusion.1
  847.7 6.1 fusion.36
  854.9 6.1 fusion.34
  862.6 7.3 fusion.42
  876.3 24.0 %all-reduce.2 = (f32[2048]{0:T(1024)S(1)}, f32[2048]{0:T(1024)S(1)}) all-reduce(f32[2048]{0:T(1024)S(1)} %get-tuple-element.99, f32[2048]{0:T(1024)S(1)} %copy-done.37), channel_id=8, replica_groups=mesh['fsdp'=2,'context'=4,'tensor'=4] {'fsdp','context'}, use_global_device_ids=true, to_apply=%region_21.22.clone | all-reduce | flops 4096 | bytes 32768
  900.5 11.3 all-reduce.3
  913.9 6.9 reduce-scatter.16.cloned.1.call-done
  922.7 35.3 %reduce-scatter.28.cloned.1.call-done = f32[256,64]{0,1:T(8,128)} async-done(((f32[2048,64]{0,1:T(8,128)}), f32[256,64]{0,1:T(8,128)}) %reduce-scatter.28.cloned.1.call-update) | async-done | bytes 65552 | tf_op jit(solution)/shard_map/reduce_scatter | solution.py:340
  958.0 38.0 %reduce-scatter.30.cloned.1.call-done = f32[256,64]{0,1:T(8,128)} async-done(((f32[2048,64]{0,1:T(8,128)}), f32[256,64]{0,1:T(8,128)}) %reduce-scatter.30.cloned.1.call-update) | async-done | bytes 65552 | tf_op jit(solution)/shard_map/reduce_scatter | solution.py:341
  996.0 55.3 %reduce-scatter.32.cloned.1.call-done = f32[512,256]{1,0:T(8,128)} async-done(((f32[512,2048]{1,0:T(8,128)}), f32[512,256]{1,0:T(8,128)}) %reduce-scatter.32.cloned.1.call-update) | async-done | bytes 524304 | tf_op jit(solution)/shard_map/reduce_scatter | solution.py:342
  1051.3 55.5 %reduce-scatter.26.cloned.1.call-done = f32[256,512]{1,0:T(8,128)} async-done(((f32[2048,512]{1,0:T(8,128)}), f32[256,512]{1,0:T(8,128)}) %reduce-scatter.26.cloned.1.call-update) | async-done | bytes 524304 | tf_op jit(solution)/shard_map/reduce_scatter | solution.py:339
  1106.8 90.7 %reduce-scatter.34.cloned.1.call-done = f32[256,1408]{1,0:T(8,128)} async-done(((f32[2048,1408]{1,0:T(8,128)}), f32[256,1408]{1,0:T(8,128)}) %reduce-scatter.34.cloned.1.call-update) | async-done | bytes 1441808 | tf_op jit(solution)/shard_map/reduce_scatter | solution.py:281
  1197.5 90.9 %reduce-scatter.36.cloned.1.call-done = f32[256,1408]{1,0:T(8,128)} async-done(((f32[2048,1408]{1,0:T(8,128)}), f32[256,1408]{1,0:T(8,128)}) %reduce-scatter.36.cloned.1.call-update) | async-done | bytes 1441808 | tf_op jit(solution)/shard_map/reduce_scatter | solution.py:282
  1288.4 90.9 %reduce-scatter.38.cloned.1.call-done = f32[1408,256]{1,0:T(8,128)} async-done(((f32[1408,2048]{1,0:T(8,128)}), f32[1408,256]{1,0:T(8,128)}) %reduce-scatter.38.cloned.1.call-update) | async-done | bytes 1441808 | tf_op jit(solution)/shard_map/reduce_scatter | solution.py:283
  (302 shorter events, 188.7 us)
Async XLA Ops:
  7.2 54.0 %all-gather.35.cloned.1.call-start = ((), (), s32[]{:S(2)}) async-start(), calls=%async_computation.28 | async-start | bytes 1310720 | tf_op jit(solution)/shard_map/all_gather | solution.py:70
  21.2 57.7 %all-gather.37.cloned.1.call-start = ((), (), s32[]{:S(2)}) async-start(), calls=%async_computation.29 | async-start | bytes 2359296 | tf_op jit(solution)/shard_map/all_gather | solution.py:152
  21.9 86.8 %all-gather.23.cloned.1.call-start = ((), (), s32[]{:S(2)}) async-start(), calls=%async_computation.20 | async-start | bytes 2359296 | tf_op jit(solution)/shard_map/all_gather | solution.py:152
  22.7 116.0 %all-gather.21.cloned.1.call-start = ((), (), s32[]{:S(2)}) async-start(), calls=%async_computation.19 | async-start | bytes 1310720 | tf_op jit(solution)/shard_map/all_gather | solution.py:70
  35.2 143.1 %all-gather.39.cloned.1.call-start = ((), (), s32[]{:S(2)}) async-start(), calls=%async_computation.30 | async-start | bytes 2359296 | tf_op jit(solution)/shard_map/all_gather | solution.py:155
  56.1 55.6 %copy-start.13 = (bf16[2048,64]{0,1:T(8,128)(2,1)}, bf16[2048,64]{0,1:T(8,128)(2,1)S(1)}, u32[]{:S(2)}) copy-start(bf16[2048,64]{0,1:T(8,128)(2,1)S(1)} %all_gather.93) | copy-start | bytes 786436
  144.9 13.1 all-to-all-start.2
  148.3 77.7 %reduce-scatter.18.cloned.1.call-start = ((), (), s32[]{:S(2)}) async-start(), calls=%async_computation.31 | async-start | bytes 2621440 | tf_op jit(solution)/shard_map/reduce_scatter | solution.py:74
  177.8 48.2 %copy-start.2 = (bf16[1,64,2048]{2,1,0:T(8,128)(2,1)S(1)}, bf16[1,64,2048]{2,1,0:T(8,128)(2,1)}, u32[]{:S(2)}) copy-start(bf16[1,64,2048]{2,1,0:T(8,128)(2,1)} %param.13) | copy-start | bytes 786436
  178.2 50.8 %copy-start.10 = (bf16[1,256,4,128]{1,3,2,0:T(8,128)(2,1)}, bf16[1,256,4,128]{1,3,2,0:T(8,128)(2,1)S(1)}, u32[]{:S(2)}) copy-start(bf16[1,256,4,128]{1,3,2,0:T(8,128)(2,1)S(1)} %copy.90) | copy-start | bytes 786436
  178.3 53.6 %copy-start.20 = (bf16[1,64,2048]{2,1,0:T(8,128)(2,1)S(1)}, bf16[1,64,2048]{2,1,0:T(8,128)(2,1)}, u32[]{:S(2)}) copy-start(bf16[1,64,2048]{2,1,0:T(8,128)(2,1)} %param.25) | copy-start | bytes 786436
  182.0 74.5 %all-gather.45.cloned.1.call-start = ((), (), s32[]{:S(2)}) async-start(), calls=%async_computation.34 | async-start | bytes 1310720 | tf_op jit(solution)/shard_map/all_gather | solution.py:70
  229.1 72.3 %all-gather.47.cloned.1.call-start = ((), (), s32[]{:S(2)}) async-start(), calls=%async_computation.35 | async-start | bytes 6488064 | tf_op jit(solution)/shard_map/all_gather | solution.py:191
  229.8 116.9 %all-gather.49.cloned.1.call-start = ((), (), s32[]{:S(2)}) async-start(), calls=%async_computation.36 | async-start | bytes 6488064 | tf_op jit(solution)/shard_map/all_gather | solution.py:190
  230.6 146.2 %all-gather.41.cloned.1.call-start = ((), (), s32[]{:S(2)}) async-start(), calls=%async_computation.32 | async-start | bytes 1310720 | tf_op jit(solution)/shard_map/all_gather | solution.py:70
  232.7 190.1 %all-gather.43.cloned.1.call-start = ((), (), s32[]{:S(2)}) async-start(), calls=%async_computation.33 | async-start | bytes 6488064 | tf_op jit(solution)/shard_map/all_gather | solution.py:192
  233.4 247.2 %reduce-scatter.20.cloned.1.call-start = ((), (), s32[]{:S(2)}) async-start(), calls=%async_computation.37 | async-start | bytes 2621440 | tf_op jit(solution)/shard_map/reduce_scatter | solution.py:74
  256.5 90.3 %copy-start.6 = (bf16[1,256,2048]{2,1,0:T(8,128)(2,1)S(1)}, bf16[1,256,2048]{2,1,0:T(8,128)(2,1)}, u32[]{:S(2)}) copy-start(bf16[1,256,2048]{2,1,0:T(8,128)(2,1)} %all-gather.45.cloned.1.call-done) | copy-start | bytes 3145732
  430.7 49.9 %copy-start.4 = (f32[1,64,2048]{2,1,0:T(8,128)S(1)}, f32[1,64,2048]{2,1,0:T(8,128)}, u32[]{:S(2)}) copy-start(f32[1,64,2048]{2,1,0:T(8,128)} %reduce-scatter.18.cloned.1.call-done) | copy-start | bytes 1572868
  430.7 49.9 %copy-start.46 = (f32[64]{0:T(128)S(1)}, f32[64]{0:T(128)}, u32[]{:S(2)}) copy-start(f32[64]{0:T(128)} %copy-done.45) | copy-start | bytes 772
  430.7 51.7 %copy-start.43 = (f32[64]{0:T(128)S(1)}, f32[64]{0:T(128)}, u32[]{:S(2)}) copy-start(f32[64]{0:T(128)} %copy-done.42) | copy-start | bytes 772
  436.6 75.5 %all-gather.51.cloned.1.call-start = ((), (), s32[]{:S(2)}) async-start(), calls=%async_computation.38 | async-start | bytes 1310720 | tf_op jit(solution)/shard_map/all_gather | solution.py:70
  482.5 39.3 %copy-start.39 = (f32[2,1024]{1,0:T(2,128)S(1)}, f32[2,1024]{1,0:T(2,128)}, u32[]{:S(2)}) copy-start(f32[2,1024]{1,0:T(2,128)} %copy-done.38) | copy-start | bytes 24580
  518.2 9.4 all-to-all-start.4
  521.6 63.9 %reduce-scatter.22.cloned.1.call-start = ((), (), s32[]{:S(2)}) async-start(), calls=%async_computation.39 | async-start | bytes 655360 | tf_op jit(solution)/shard_map/reduce_scatter | solution.py:314
  547.0 69.7 %all-gather.25.cloned.1.call-start = ((), (), s32[]{:S(2)}) async-start(), calls=%async_computation.21 | async-start | bytes 2359296 | tf_op jit(solution)/shard_map/all_gather | solution.py:155
  572.6 12.2 all-to-all-start
  576.0 87.6 %reduce-scatter.14.cloned.1.call-start = ((), (), s32[]{:S(2)}) async-start(), calls=%async_computation.22 | async-start | bytes 2621440 | tf_op jit(solution)/shard_map/reduce_scatter | solution.py:74
  620.5 47.6 %copy-start.36 = (f32[1024]{0:T(1024)S(1)}, f32[1024]{0:T(1024)}, u32[]{:S(2)}) copy-start(f32[1024]{0:T(1024)} %copy-done.35) | copy-start | bytes 12292
  620.5 47.6 %copy-start.48 = (f32[32]{0:T(128)S(1)}, f32[32]{0:T(128)}, u32[]{:S(2)}) copy-start(f32[32]{0:T(128)} %copy-done.47) | copy-start | bytes 388
  620.5 87.5 %all-gather.29.cloned.1.call-start = ((), (), s32[]{:S(2)}) async-start(), calls=%async_computation.24 | async-start | bytes 6488064 | tf_op jit(solution)/shard_map/all_gather | solution.py:190
  621.1 116.9 %all-gather.27.cloned.1.call-start = ((), (), s32[]{:S(2)}) async-start(), calls=%async_computation.23 | async-start | bytes 1310720 | tf_op jit(solution)/shard_map/all_gather | solution.py:70
  666.7 116.0 %all-gather.31.cloned.1.call-start = ((), (), s32[]{:S(2)}) async-start(), calls=%async_computation.25 | async-start | bytes 6488064 | tf_op jit(solution)/shard_map/all_gather | solution.py:191
  667.5 161.3 %all-gather.33.cloned.1.call-start = ((), (), s32[]{:S(2)}) async-start(), calls=%async_computation.26 | async-start | bytes 6488064 | tf_op jit(solution)/shard_map/all_gather | solution.py:192
  668.1 206.9 %reduce-scatter.24.cloned.1.call-start = ((), (), s32[]{:S(2)}) async-start(), calls=%async_computation.40 | async-start | bytes 2621440 | tf_op jit(solution)/shard_map/reduce_scatter | solution.py:74
  700.5 220.3 %reduce-scatter.16.cloned.1.call-start = ((), (), s32[]{:S(2)}) async-start(), calls=%async_computation.27 | async-start | bytes 2621440 | tf_op jit(solution)/shard_map/reduce_scatter | solution.py:74
  738.0 90.8 %copy-start.50 = (bf16[1,256,2048]{2,1,0:T(8,128)(2,1)S(1)}, bf16[1,256,2048]{2,1,0:T(8,128)(2,1)}, u32[]{:S(2)}) copy-start(bf16[1,256,2048]{2,1,0:T(8,128)(2,1)} %all-gather.27.cloned.1.call-done) | copy-start | bytes 3145732
  743.9 94.5 %copy-start.28 = (bf16[256,32]{0,1:T(8,128)(2,1)S(1)}, bf16[256,32]{0,1:T(8,128)(2,1)}, u32[]{:S(2)}) copy-start(bf16[256,32]{0,1:T(8,128)(2,1)} %get-tuple-element.116) | copy-start | bytes 49156
  838.3 119.7 %reduce-scatter.28.cloned.1.call-start = ((), (), s32[]{:S(2)}) async-start(), calls=%async_computation.42 | async-start | bytes 589824 | tf_op jit(solution)/shard_map/reduce_scatter | solution.py:340
  839.5 156.5 %reduce-scatter.30.cloned.1.call-start = ((), (), s32[]{:S(2)}) async-start(), calls=%async_computation.43 | async-start | bytes 589824 | tf_op jit(solution)/shard_map/reduce_scatter | solution.py:341
  840.7 210.6 %reduce-scatter.32.cloned.1.call-start = ((), (), s32[]{:S(2)}) async-start(), calls=%async_computation.44 | async-start | bytes 4718592 | tf_op jit(solution)/shard_map/reduce_scatter | solution.py:342
  843.5 263.3 %reduce-scatter.26.cloned.1.call-start = ((), (), s32[]{:S(2)}) async-start(), calls=%async_computation.41 | async-start | bytes 4718592 | tf_op jit(solution)/shard_map/reduce_scatter | solution.py:339
  846.3 351.3 %reduce-scatter.34.cloned.1.call-start = ((), (), s32[]{:S(2)}) async-start(), calls=%async_computation.45 | async-start | bytes 12976128 | tf_op jit(solution)/shard_map/reduce_scatter | solution.py:281
  853.8 434.6 %reduce-scatter.36.cloned.1.call-start = ((), (), s32[]{:S(2)}) async-start(), calls=%async_computation.46 | async-start | bytes 12976128 | tf_op jit(solution)/shard_map/reduce_scatter | solution.py:282
  861.0 518.3 %reduce-scatter.38.cloned.1.call-start = ((), (), s32[]{:S(2)}) async-start(), calls=%async_computation.47 | async-start | bytes 12976128 | tf_op jit(solution)/shard_map/reduce_scatter | solution.py:283
  869.9 41.9 %copy-start.17 = (f32[1,64,2048]{2,1,0:T(8,128)S(1)}, f32[1,64,2048]{2,1,0:T(8,128)}, u32[]{:S(2)}) copy-start(f32[1,64,2048]{2,1,0:T(8,128)} %get-tuple-element.106) | copy-start | bytes 1572868
  869.9 50.9 %copy-start.8 = (f32[1,64,2048]{2,1,0:T(8,128)S(1)}, f32[1,64,2048]{2,1,0:T(8,128)}, u32[]{:S(2)}) copy-start(f32[1,64,2048]{2,1,0:T(8,128)} %reduce-scatter.14.cloned.1.call-done) | copy-start | bytes 1572868
  870.0 50.9 %copy-start.44 = (f32[64]{0:T(128)S(1)}, f32[64]{0:T(128)}, u32[]{:S(2)}) copy-start(f32[64]{0:T(128)} %copy-done.42) | copy-start | bytes 772
  (38 other events, 349.6 us)
Sparse Core Ops, SparseCore 0:
  21.3 28.2 all-gather.34
  51.5 27.3 all-gather.36
  80.8 27.8 all-gather.22
  110.7 27.9 all-gather.20
  140.4 30.5 all-gather.38
  182.2 43.7 reduce-scatter.17
  229.2 27.2 all-gather.44
  258.5 42.7 all-gather.46
  303.4 43.3 all-gather.48
  348.8 27.9 all-gather.40
  378.9 43.8 all-gather.42
  436.7 43.8 reduce-scatter.19
  484.8 27.2 all-gather.50
  547.2 20.9 reduce-scatter.21
  570.0 29.6 all-gather.24
  620.6 42.9 reduce-scatter.13
  665.3 42.6 all-gather.28
  710.0 27.9 all-gather.26
  739.8 42.8 all-gather.30
  784.4 44.3 all-gather.32
  831.1 43.8 reduce-scatter.23
  877.4 43.4 reduce-scatter.15
  924.5 33.4 reduce-scatter.27
  961.8 34.1 reduce-scatter.29
  999.9 51.3 reduce-scatter.31
  1055.4 51.3 reduce-scatter.25
  1110.7 86.7 reduce-scatter.33
  1201.6 86.7 reduce-scatter.35
  1292.5 86.7 reduce-scatter.37
where the time goes:
time: 1400 us; the launch traced here: 1390 us
  waiting for transfers between devices  987 us (70%)
  blocking collectives  157 us (11%)
  matrix products  124 us (9%)
  other arithmetic  52.9 us (4%)
  local copies, waits for them, and re-layouts  37.4 us (3%)
  between operations  16.3 us (1%)
    all_gather x6, waiting for transfers between devices, rows_gather(): return lax.all_gather(activations, 'tensor', axis=1, tiled=True)  128 us
    reduce_scatter x5, waiting for transfers between devices, rows_sum(): return lax.psum_scatter(partials, 'tensor', scatter_dimension=1, tiled=True)  122 us
    all_gather x2, waiting for transfers between devices, forward_pass(): lax.all_gather(w_down, ('fsdp', 'context'), axis=1, tiled=True)  92 us
    reduce_scatter x1, waiting for transfers between devices, body(): lax.psum_scatter(grad_down, ('fsdp', 'context'), scatter_dimension=1, til...  90.9 us
    reduce_scatter x1, waiting for transfers between devices, body(): lax.psum_scatter(grad_up, ('fsdp', 'context'), scatter_dimension=0, tiled...  90.9 us
    reduce_scatter x1, waiting for transfers between devices, body(): lax.psum_scatter(grad_gate, ('fsdp', 'context'), scatter_dimension=0, til...  90.7 us
    all_gather x2, waiting for transfers between devices, forward_pass(): lax.all_gather(w_up, ('fsdp', 'context'), axis=0, tiled=True)  83.7 us
    reduce_scatter x1, waiting for transfers between devices, body(): lax.psum_scatter(grad_query, ('fsdp', 'context'), scatter_dimension=0, ti...  55.5 us
  transfers between devices with their start and end apart: 32, of which 27 were waited for; matrix products, arithmetic and copies ran while one was open for 11% of the time, Pallas kernels for 0%

commit v1 on v0

v1 whole, which is shorter than its diff:
```python
import math

import jax
import jax.numpy as jnp
from jax import lax
from jax.sharding import PartitionSpec as P

EPS = 1e-05
NEG = -1e30
BF = jnp.bfloat16
F32 = jnp.float32


def rope_tables(positions, head_size):
    half_size = head_size // 2
    frequency = jnp.exp(
        -(jnp.arange(half_size, dtype=F32) * (2.0 / head_size)) * math.log(10000.0)
    )
    angles = positions.astype(F32)[..., None] * frequency
    return (jnp.cos(angles)[..., None, :], jnp.sin(angles)[..., None, :])


def rotate(vectors, cos_table, sin_table):
    half_size = vectors.shape[-1] // 2
    first_half = vectors[..., :half_size]
    second_half = vectors[..., half_size:]
    return jnp.concatenate(
        [
            first_half * cos_table - second_half * sin_table,
            second_half * cos_table + first_half * sin_table,
        ],
        axis=-1,
    )


def mm(a, b, ca=1, cb=0):
    return lax.dot_general(a, b, (((ca,), (cb,)), ((), ())), preferred_element_type=F32)


def rows_gather(x):
    return lax.all_gather(x, "tensor", axis=0, tiled=True)


def rows_sum(x):
    return lax.psum_scatter(x.astype(BF), "tensor", scatter_dimension=0, tiled=True).astype(F32)


FC = ("fsdp", "context")


def gather_w(w, axis=0):
    return lax.all_gather(w, FC, axis=axis, tiled=True)


def scatter_g(g, axis=0):
    return lax.psum_scatter(g.astype(BF), FC, scatter_dimension=axis, tiled=True).astype(F32)


def norm_back(grad_normed, vectors, inv_scale, gain_row):
    unit_rows = vectors * inv_scale
    weighted = grad_normed * gain_row
    grad_gain = jnp.sum(grad_normed * unit_rows, axis=0)
    grad_vectors = inv_scale * (
        weighted - unit_rows * jnp.mean(weighted * unit_rows, axis=-1, keepdims=True)
    )
    return (grad_vectors, grad_gain)


def one_sequence(
    hidden_in, segment_ids, pad_mask, attn_gain, w_query, w_key, w_value, w_out,
    mlp_gain, w_gate, w_up, w_down, cotangent,
):
    row_count, model_width = hidden_in.shape
    context_count = lax.axis_size("context")
    tensor_count = lax.axis_size("tensor")
    context_index = lax.axis_index("context")
    tensor_index = lax.axis_index("tensor")
    length = segment_ids.shape[0]
    span = length // context_count
    hd = w_key.shape[1]
    start = context_index * span
    seg_span = lax.dynamic_slice_in_dim(segment_ids, start, span, 0)
    columns = jnp.arange(length, dtype=jnp.int32)
    row_at = start + jnp.arange(span, dtype=jnp.int32)
    first = jnp.sum((segment_ids[None, :] < seg_span[:, None]).astype(jnp.int32), axis=1)
    cos_t, sin_t = rope_tables(row_at - first, hd)
    row_start = start + tensor_index * row_count
    keep = lax.dynamic_slice_in_dim(pad_mask, row_start, row_count, 0).astype(F32)[:, None]
    allowed = (
        (seg_span[:, None] == segment_ids[None, :])
        & (columns[None, :] <= row_at[:, None])
        & ((pad_mask[None, :] == 1) | (columns[None, :] == row_at[:, None]))
    )
    gain_one = gather_w(attn_gain).astype(F32)
    gain_two = gather_w(mlp_gain).astype(F32)
    qkv_all = gather_w(jnp.concatenate([w_query, w_key, w_value], axis=1))
    out_all = gather_w(w_out, 1)
    gate_all = gather_w(w_gate)
    up_all = gather_w(w_up)
    down_all = gather_w(w_down, 1)
    qw = w_query.shape[1]

    hidden = hidden_in.astype(F32)
    scale_one = lax.rsqrt(jnp.mean(hidden * hidden, axis=-1, keepdims=True) + EPS)
    n1 = rows_gather((hidden * scale_one * gain_one).astype(BF))
    g_out = cotangent.astype(F32) * keep
    g_all = rows_gather(g_out.astype(BF))
    pre = mm(n1, qkv_all)
    q = rotate(pre[:, :qw].reshape(span, -1, hd), cos_t, sin_t).astype(BF)
    k = rotate(pre[:, None, qw:qw + hd], cos_t, sin_t).astype(BF)[:, 0]
    v = pre[:, qw + hd:].astype(BF)
    kv = lax.all_gather(jnp.concatenate([k, v], axis=1), "context", axis=0, tiled=True)
    k, v = kv[:, :hd], kv[:, hd:]
    scale = hd ** (-0.5)
    scores = jnp.einsum("qhd,td->hqt", q, k, preferred_element_type=F32) * scale
    scores = jnp.where(allowed[None], scores, NEG)
    top = jnp.max(scores, axis=-1, keepdims=True)
    e = jnp.exp(scores - top)
    probs = e / jnp.sum(e, axis=-1, keepdims=True)
    probs_b = probs.astype(BF)
    attn = jnp.einsum("hqt,td->qhd", probs_b, v, preferred_element_type=F32)
    attn = attn.reshape(span, -1).astype(BF)
    middle = hidden + rows_sum(mm(attn, out_all))
    scale_two = lax.rsqrt(jnp.mean(middle * middle, axis=-1, keepdims=True) + EPS)
    n2 = rows_gather((middle * scale_two * gain_two).astype(BF))
    gate = mm(n2, gate_all)
    up = mm(n2, up_all)
    sig = jax.nn.sigmoid(gate)
    inner = (gate * sig * up).astype(BF)
    block_out = (keep * (middle + rows_sum(mm(inner, down_all)))).astype(BF)

    grad_down = mm(inner, g_all, 0, 0)
    g_inner = mm(g_all, down_all, 1, 1)
    g_gate = (g_inner * up * sig * (1.0 + gate * (1.0 - sig))).astype(BF)
    g_up = (g_inner * gate * sig).astype(BF)
    g_n2 = rows_sum(mm(g_gate, gate_all, 1, 1) + mm(g_up, up_all, 1, 1))
    grad_gate = mm(n2, g_gate, 0, 0)
    grad_up = mm(n2, g_up, 0, 0)
    d_mid, grad_gain_two = norm_back(g_n2, middle, scale_two, gain_two)
    g_mid = g_out + d_mid
    gm_all = rows_gather(g_mid.astype(BF))
    grad_out = mm(attn, gm_all, 0, 0)
    g_attn = mm(gm_all, out_all, 1, 1).astype(BF).reshape(span, -1, hd)
    dp = jnp.einsum("qhd,td->hqt", g_attn, v, preferred_element_type=F32)
    delta = jnp.sum(probs * dp, axis=-1, keepdims=True)
    ds = (probs * (dp - delta)).astype(BF)
    g_q = jnp.einsum("hqt,td->qhd", ds, k, preferred_element_type=F32) * scale
    g_k = jnp.einsum("hqt,qhd->td", ds, q, preferred_element_type=F32) * scale
    g_v = jnp.einsum("hqt,qhd->td", probs_b, g_attn, preferred_element_type=F32)
    g_kv = lax.psum_scatter(
        jnp.concatenate([g_k, g_v], axis=1), "context", scatter_dimension=0, tiled=True
    )
    g_q = rotate(g_q, cos_t, -sin_t).astype(BF).reshape(span, -1)
    g_k = rotate(g_kv[:, None, :hd], cos_t, -sin_t).astype(BF)[:, 0]
    g_qkv = jnp.concatenate([g_q, g_k, g_kv[:, hd:].astype(BF)], axis=1)
    g_n1 = rows_sum(mm(g_qkv, qkv_all, 1, 1))
    grad_qkv = mm(n1, g_qkv, 0, 0)
    d_hid, grad_gain_one = norm_back(g_n1, hidden, scale_one, gain_one)
    gains = jnp.stack([grad_gain_one, grad_gain_two])
    return (
        block_out, g_mid + d_hid, gains, grad_qkv, grad_out, grad_gate, grad_up, grad_down,
    )


def body(hidden_in, segment_ids, pad_mask, attn_gain, w_query, w_key, w_value, w_out,
         mlp_gain, w_gate, w_up, w_down, cotangent):
    block_out, grad_hidden, gains, grad_qkv, grad_out, grad_gate, grad_up, grad_down = one_sequence(
        hidden_in[0], segment_ids[0], pad_mask[0], attn_gain, w_query, w_key, w_value, w_out,
        mlp_gain, w_gate, w_up, w_down, cotangent[0],
    )
    grad_down = scatter_g(grad_down, 1)
    grad_gate = scatter_g(grad_gate)
    grad_up = scatter_g(grad_up)
    grad_out = scatter_g(grad_out, 1)
    grad_qkv = scatter_g(grad_qkv)
    gains = lax.psum(gains, "tensor")
    gains = lax.psum_scatter(gains, FC, scatter_dimension=1, tiled=True)
    qw, hd = w_query.shape[1], w_key.shape[1]
    return (
        block_out[None], grad_hidden[None], gains[0], grad_qkv[:, :qw],
        grad_qkv[:, qw:qw + hd], grad_qkv[:, qw + hd:], grad_out, gains[1],
        grad_gate, grad_up, grad_down,
    )


def solution(mesh):
    fc = ("fsdp", "context")
    rows = P("fsdp", ("context", "tensor"), None)
    tail = (P(fc), P(fc, "tensor"), P(fc, "tensor"), P(fc, "tensor"), P("tensor", fc),
            P(fc), P(fc, "tensor"), P(fc, "tensor"), P("tensor", fc))
    in_specs = (rows, P("fsdp", None), P("fsdp", None)) + tail + (rows,)
    out_specs = (rows, rows) + tail
    return jax.shard_map(body, mesh=mesh, in_specs=in_specs, out_specs=out_specs, check_vma=False)
```

time: 1400 us -> 840 us (0.60)
  waiting for transfers between devices: 987 us -> 650 us
  blocking collectives: 157 us -> 36.7 us
  matrix products: 124 us -> 87.3 us
  other arithmetic: 52.9 us -> 30.9 us
  local copies, waits for them, and re-layouts: 37.4 us -> 18.2 us
    reduce_scatter x13 -> x10, waiting for transfers between devices: 579 us -> 344 us  [the longest x5 234 us: scatter_g(): lax.psum_scatter(g.astype(BF), FC, scatter_dimension=axis, tiled=True)]
    all_gather x16 -> x9, waiting for transfers between devices: 390 us -> 267 us  [the longest x5 173 us: gather_w(): return lax.all_gather(w, FC, axis=axis, tiled=True)]
    all_gather x10 -> x3, blocking collectives: 94.4 us -> 25 us  [the longest x2 19.2 us: gather_w(): return lax.all_gather(w, FC, axis=axis, tiled=True)]
    dot_general x33 -> x20, matrix products: 118 us -> 82.5 us  [the longest x15 64 us: mm(): lax.dot_general(a, b, (((ca,), (cb,)), ((), ())), preferred_element_type=...]
    unnamed x29 -> x21, waiting for transfers between devices: 6.58 us -> 38.8 us
    all_to_all x3 -> x0, blocking collectives: 27 us -> none  [to_spans(): lax.all_to_all(by_heads, 'context', split_axis=1, concat_axis=2, tiled=True)]
    unnamed x1 -> x0, blocking collectives: 24 us -> none
    unnamed x6 -> x1, other arithmetic: 14.9 us -> 0.01 us
  transfers between devices with their start and end apart: 32 -> 20, of which waited for: 27 -> 20; matrix products, arithmetic and copies ran while one was open for 11% -> 10% of each run, Pallas kernels for 0% -> 0%
where the time goes in v1:
time: 840 us; the launch traced here: 839 us
  waiting for transfers between devices  650 us (77%)
  matrix products  87.3 us (10%)
  blocking collectives  36.7 us (4%)
  other arithmetic  30.9 us (4%)
  local copies, waits for them, and re-layouts  18.2 us (2%)
  between operations  14.8 us (2%)
    reduce_scatter x5, waiting for transfers between devices, scatter_g(): lax.psum_scatter(g.astype(BF), FC, scatter_dimension=axis, tiled=True)  234 us
    all_gather x5, waiting for transfers between devices, gather_w(): return lax.all_gather(w, FC, axis=axis, tiled=True)  173 us
    all_gather x4, waiting for transfers between devices, rows_gather(): return lax.all_gather(x, 'tensor', axis=0, tiled=True)  93.7 us
    reduce_scatter x4, waiting for transfers between devices, rows_sum(): lax.psum_scatter(x.astype(BF), 'tensor', scatter_dimension=0, tiled=True)  92.2 us
    dot_general x15, matrix products, mm(): lax.dot_general(a, b, (((ca,), (cb,)), ((), ())), preferred_element_type=...  64 us
    unnamed x21, waiting for transfers between devices  38.8 us
    all_gather x2, blocking collectives, gather_w(): return lax.all_gather(w, FC, axis=axis, tiled=True)  19.2 us
    reduce_scatter x1, waiting for transfers between devices, one_sequence(): lax.psum_scatter(jnp.concatenate([g_k, g_v], axis=1), 'context', scatter_...  18.1 us
  transfers between devices with their start and end apart: 20, of which 20 were waited for; matrix products, arithmetic and copies ran while one was open for 10% of the time, Pallas kernels for 0%

profile of v1, /device:TPU:0, one launch (start us, length us, event | category | flops | bytes accessed | tf_op | source)
XLA Modules:
  0.0 838.9 jit_solution(12737155059699517862)
XLA Ops:
  9.0 10.3 %all-gather = bf16[8,1,256]{2,1,0:T(2,128)(2,1)S(1)} all-gather(bf16[1,1,256]{2,1,0:T(2,128)(2,1)S(1)} %reshape.348), channel_id=1, replica_groups=mesh['fsdp'=2,'context'=4,'tensor'=4] {'fsdp','context'}, dimensions={0}, use_global_device_ids=true | all-gather | bytes 4608 | tf_op jit(solution)/shard_map/all_gather | solution.py:52
  29.8 19.8 %all-gather.12.cloned.1.call-done = bf16[256,2048]{1,0:T(8,128)(2,1)} async-done(((bf16[64,2048]{1,0:T(8,128)(2,1)}), bf16[256,2048]{1,0:T(8,128)(2,1)}) %all-gather.12.cloned.1.call-update) | async-done | bytes 1048592 | tf_op jit(solution)/shard_map/all_gather | solution.py:41
  49.6 32.1 %all-gather.14.cloned.1.call-done = bf16[2048,640]{1,0:T(8,128)(2,1)} async-done(((bf16[256,640]{1,0:T(8,128)(2,1)}), bf16[2048,640]{1,0:T(8,128)(2,1)}) %all-gather.14.cloned.1.call-update) | async-done | bytes 2621456 | tf_op jit(solution)/shard_map/all_gather | solution.py:52
  81.7 3.0 fusion.84
  85.8 5.8 all_gather.39
  91.6 4.8 fusion.83
  96.4 4.3 fusion.14
  100.8 11.0 %all-gather.16.cloned.1.call-done = bf16[512,2048]{1,0:T(8,128)(2,1)} async-done(((bf16[512,256]{1,0:T(8,128)(2,1)}), bf16[512,2048]{1,0:T(8,128)(2,1)}) %all-gather.16.cloned.1.call-update) | async-done | bytes 2097168 | tf_op jit(solution)/shard_map/all_gather | solution.py:52
  111.8 3.3 convolution_convert_fusion.5
  115.2 8.8 %all-gather.1 = bf16[8,1,256]{2,1,0:T(2,128)(2,1)S(1)} all-gather(bf16[1,1,256]{2,1,0:T(2,128)(2,1)S(1)} %reshape.350), channel_id=1, replica_groups=mesh['fsdp'=2,'context'=4,'tensor'=4] {'fsdp','context'}, dimensions={0}, use_global_device_ids=true | all-gather | bytes 4608 | tf_op jit(solution)/shard_map/all_gather | solution.py:52
  124.0 18.4 %reduce-scatter.14.cloned.1.call-done = bf16[64,2048]{1,0:T(8,128)(2,1)} async-done(((bf16[256,2048]{1,0:T(8,128)(2,1)}), bf16[64,2048]{1,0:T(8,128)(2,1)}) %reduce-scatter.14.cloned.1.call-update) | async-done | bytes 262160 | tf_op jit(solution)/shard_map/reduce_scatter | solution.py:45
  149.3 22.8 %all-gather.18.cloned.1.call-done = bf16[256,2048]{1,0:T(8,128)(2,1)} async-done(((bf16[64,2048]{1,0:T(8,128)(2,1)}), bf16[256,2048]{1,0:T(8,128)(2,1)}) %all-gather.18.cloned.1.call-update) | async-done | bytes 1048592 | tf_op jit(solution)/shard_map/all_gather | solution.py:41
  172.1 44.7 %all-gather.22.cloned.1.call-done = bf16[2048,1408]{1,0:T(8,128)(2,1)} async-done(((bf16[256,1408]{1,0:T(8,128)(2,1)}), bf16[2048,1408]{1,0:T(8,128)(2,1)}) %all-gather.22.cloned.1.call-update) | async-done | bytes 5767184 | tf_op jit(solution)/shard_map/all_gather | solution.py:52
  216.8 5.9 fusion.86
  222.7 39.5 %all-gather.20.cloned.1.call-done = bf16[2048,1408]{1,0:T(8,128)(2,1)} async-done(((bf16[256,1408]{1,0:T(8,128)(2,1)}), bf16[2048,1408]{1,0:T(8,128)(2,1)}) %all-gather.20.cloned.1.call-update) | async-done | bytes 5767184 | tf_op jit(solution)/shard_map/all_gather | solution.py:52
  262.2 5.5 fusion.85
  267.8 24.7 %all-gather.26.cloned.1.call-done = bf16[256,2048]{1,0:T(8,128)(2,1)} async-done(((bf16[64,2048]{1,0:T(8,128)(2,1)}), bf16[256,2048]{1,0:T(8,128)(2,1)}) %all-gather.26.cloned.1.call-update) | async-done | bytes 1048592 | tf_op jit(solution)/shard_map/all_gather | solution.py:41
  292.4 45.9 %all-gather.24.cloned.1.call-done = bf16[1408,2048]{1,0:T(8,128)(2,1)} async-done(((bf16[1408,256]{1,0:T(8,128)(2,1)}), bf16[1408,2048]{1,0:T(8,128)(2,1)}) %all-gather.24.cloned.1.call-update) | async-done | bytes 5767184 | tf_op jit(solution)/shard_map/all_gather | solution.py:52
  338.3 6.2 multiply_convert_fusion
  346.5 5.5 fusion.8
  352.0 27.2 %reduce-scatter.18.cloned.1.call-done = bf16[64,2048]{1,0:T(8,128)(2,1)} async-done(((bf16[256,2048]{1,0:T(8,128)(2,1)}), bf16[64,2048]{1,0:T(8,128)(2,1)}) %reduce-scatter.18.cloned.1.call-update) | async-done | bytes 262160 | tf_op jit(solution)/shard_map/reduce_scatter | solution.py:45
  382.8 26.5 %all-gather.28.cloned.1.call-done = bf16[256,2048]{1,0:T(8,128)(2,1)} async-done(((bf16[64,2048]{1,0:T(8,128)(2,1)}), bf16[256,2048]{1,0:T(8,128)(2,1)}) %all-gather.28.cloned.1.call-update) | async-done | bytes 1048592 | tf_op jit(solution)/shard_map/all_gather | solution.py:41
  409.3 3.4 convolution_convert_fusion.8
  414.4 4.9 fusion.17
  419.4 4.8 fusion.1
  425.5 1.9 copy-done
  429.7 3.1 fusion.13
  432.9 18.1 %reduce-scatter.20.cloned.1.call-done = f32[256,128]{0,1:T(8,128)} async-done(((f32[1024,128]{0,1:T(8,128)}), f32[256,128]{0,1:T(8,128)}) %reduce-scatter.20.cloned.1.call-update) | async-done | bytes 131088 | tf_op jit(solution)/shard_map/reduce_scatter | solution.py:150
  452.9 3.7 convolution_convert_fusion.6
  456.7 3.3 convolution_convert_fusion.4
  460.1 5.4 convolution_convert_fusion.7
  465.6 18.3 %reduce-scatter.22.cloned.1.call-done = bf16[64,2048]{1,0:T(8,128)(2,1)} async-done(((bf16[256,2048]{1,0:T(8,128)(2,1)}), bf16[64,2048]{1,0:T(8,128)(2,1)}) %reduce-scatter.22.cloned.1.call-update) | async-done | bytes 262160 | tf_op jit(solution)/shard_map/reduce_scatter | solution.py:45
  486.7 2.5 convolution_convert_fusion.3
  489.3 5.6 convolution_convert_fusion
  496.0 4.3 convolution_convert_fusion.1
  501.5 4.4 convolution_convert_fusion.2
  505.8 21.1 %reduce-scatter.26.cloned.1.call-done = bf16[512,256]{1,0:T(8,128)(2,1)} async-done(((bf16[512,2048]{1,0:T(8,128)(2,1)}), bf16[512,256]{1,0:T(8,128)(2,1)}) %reduce-scatter.26.cloned.1.call-update) | async-done | bytes 262160 | tf_op jit(solution)/shard_map/reduce_scatter | solution.py:56
  528.8 28.2 %reduce-scatter.16.cloned.1.call-done = bf16[64,2048]{1,0:T(8,128)(2,1)} async-done(((bf16[256,2048]{1,0:T(8,128)(2,1)}), bf16[64,2048]{1,0:T(8,128)(2,1)}) %reduce-scatter.16.cloned.1.call-update) | async-done | bytes 262160 | tf_op jit(solution)/shard_map/reduce_scatter | solution.py:45
  557.0 2.4 fusion.35
  559.4 35.9 %reduce-scatter.34.cloned.1.call-done = f32[256,2]{1,0:T(8,128)} async-done(((f32[2048,2]{1,0:T(8,128)}), f32[256,2]{1,0:T(8,128)}) %reduce-scatter.34.cloned.1.call-update) | async-done | bytes 2064
  596.3 11.7 %psum.8 = f32[2,256]{1,0:T(2,128)S(1)} all-reduce(f32[2,256]{1,0:T(2,128)S(1)} %copy.113), channel_id=1, replica_groups=mesh['fsdp'=2,'context'=4,'tensor'=4] {'tensor'}, use_global_device_ids=true, to_apply=%region_15.16 | all-reduce | flops 512 | bytes 4096 | tf_op jit(solution)/shard_map/psum | solution.py:176
  608.6 33.6 %reduce-scatter.24.cloned.1.call-done = bf16[256,640]{1,0:T(8,128)(2,1)} async-done(((bf16[2048,640]{1,0:T(8,128)(2,1)}), bf16[256,640]{1,0:T(8,128)(2,1)}) %reduce-scatter.24.cloned.1.call-update) | async-done | bytes 327696 | tf_op jit(solution)/shard_map/reduce_scatter | solution.py:56
  646.4 58.1 %reduce-scatter.32.cloned.1.call-done = bf16[1408,256]{1,0:T(8,128)(2,1)} async-done(((bf16[1408,2048]{1,0:T(8,128)(2,1)}), bf16[1408,256]{1,0:T(8,128)(2,1)}) %reduce-scatter.32.cloned.1.call-update) | async-done | bytes 720912 | tf_op jit(solution)/shard_map/reduce_scatter | solution.py:56
  704.5 2.3 convert_element_type.192
  706.8 60.6 %reduce-scatter.30.cloned.1.call-done = bf16[256,1408]{1,0:T(8,128)(2,1)} async-done(((bf16[2048,1408]{1,0:T(8,128)(2,1)}), bf16[256,1408]{1,0:T(8,128)(2,1)}) %reduce-scatter.30.cloned.1.call-update) | async-done | bytes 720912 | tf_op jit(solution)/shard_map/reduce_scatter | solution.py:56
  767.4 2.3 convert_element_type.190
  769.7 60.1 %reduce-scatter.28.cloned.1.call-done = bf16[256,1408]{1,0:T(8,128)(2,1)} async-done(((bf16[2048,1408]{1,0:T(8,128)(2,1)}), bf16[256,1408]{1,0:T(8,128)(2,1)}) %reduce-scatter.28.cloned.1.call-update) | async-done | bytes 720912 | tf_op jit(solution)/shard_map/reduce_scatter | solution.py:56
  829.8 2.3 convert_element_type.188
  (133 shorter events, 45.4 us)
Async XLA Ops:
  7.2 42.4 %all-gather.12.cloned.1.call-start = ((), (), s32[]{:S(2)}) async-start(), calls=%async_computation.11 | async-start | bytes 1310720 | tf_op jit(solution)/shard_map/all_gather | solution.py:41
  21.2 60.5 %all-gather.14.cloned.1.call-start = ((), (), s32[]{:S(2)}) async-start(), calls=%async_computation.12 | async-start | bytes 2949120 | tf_op jit(solution)/shard_map/all_gather | solution.py:52
  24.8 87.0 %all-gather.16.cloned.1.call-start = ((), (), s32[]{:S(2)}) async-start(), calls=%async_computation.13 | async-start | bytes 2359296 | tf_op jit(solution)/shard_map/all_gather | solution.py:52
  25.5 116.9 %reduce-scatter.14.cloned.1.call-start = ((), (), s32[]{:S(2)}) async-start(), calls=%async_computation.14 | async-start | bytes 1310720 | tf_op jit(solution)/shard_map/reduce_scatter | solution.py:45
  100.8 14.4 %copy-start.15 = (bf16[256]{0:T(256)(128)(2,1)S(1)}, bf16[256]{0:T(256)(128)(2,1)}, u32[]{:S(2)}) copy-start(bf16[256]{0:T(256)(128)(2,1)} %param.21) | copy-start | bytes 1540
  100.8 41.6 %copy-start.1 = (bf16[1,64,2048]{2,1,0:T(8,128)(2,1)S(1)}, bf16[1,64,2048]{2,1,0:T(8,128)(2,1)}, u32[]{:S(2)}) copy-start(bf16[1,64,2048]{2,1,0:T(8,128)(2,1)} %param.13) | copy-start | bytes 786436
  100.8 46.7 %copy-start.5 = (bf16[1,64,2048]{2,1,0:T(8,128)(2,1)S(1)}, bf16[1,64,2048]{2,1,0:T(8,128)(2,1)}, u32[]{:S(2)}) copy-start(bf16[1,64,2048]{2,1,0:T(8,128)(2,1)} %param.25) | copy-start | bytes 786436
  115.1 57.0 %all-gather.18.cloned.1.call-start = ((), (), s32[]{:S(2)}) async-start(), calls=%async_computation.15 | async-start | bytes 1310720 | tf_op jit(solution)/shard_map/all_gather | solution.py:41
  145.4 71.5 %all-gather.22.cloned.1.call-start = ((), (), s32[]{:S(2)}) async-start(), calls=%async_computation.17 | async-start | bytes 6488064 | tf_op jit(solution)/shard_map/all_gather | solution.py:52
  145.9 116.3 %all-gather.20.cloned.1.call-start = ((), (), s32[]{:S(2)}) async-start(), calls=%async_computation.16 | async-start | bytes 6488064 | tf_op jit(solution)/shard_map/all_gather | solution.py:52
  146.7 145.7 %all-gather.26.cloned.1.call-start = ((), (), s32[]{:S(2)}) async-start(), calls=%async_computation.20 | async-start | bytes 1310720 | tf_op jit(solution)/shard_map/all_gather | solution.py:41
  148.3 190.0 %all-gather.24.cloned.1.call-start = ((), (), s32[]{:S(2)}) async-start(), calls=%async_computation.18 | async-start | bytes 6488064 | tf_op jit(solution)/shard_map/all_gather | solution.py:52
  149.1 230.2 %reduce-scatter.18.cloned.1.call-start = ((), (), s32[]{:S(2)}) async-start(), calls=%async_computation.21 | async-start | bytes 1310720 | tf_op jit(solution)/shard_map/reduce_scatter | solution.py:45
  172.1 90.1 %copy-start.2 = (bf16[256,2048]{1,0:T(8,128)(2,1)S(1)}, bf16[256,2048]{1,0:T(8,128)(2,1)}, u32[]{:S(2)}) copy-start(bf16[256,2048]{1,0:T(8,128)(2,1)} %all-gather.18.cloned.1.call-done) | copy-start | bytes 3145732
  338.3 6.3 copy-start.14
  344.6 1.9 copy-start.9
  344.6 1.9 copy-start.11
  344.6 115.5 %copy-start.7 = (bf16[256,1408]{1,0:T(8,128)(2,1)}, bf16[256,1408]{1,0:T(8,128)(2,1)S(1)}, u32[]{:S(2)}) copy-start(bf16[256,1408]{1,0:T(8,128)(2,1)S(1)} %get-tuple-element.61) | copy-start | bytes 2162692
  346.4 32.8 %copy-start.3 = (bf16[64,2048]{1,0:T(8,128)(2,1)S(1)}, bf16[64,2048]{1,0:T(8,128)(2,1)}, u32[]{:S(2)}) copy-start(bf16[64,2048]{1,0:T(8,128)(2,1)} %reduce-scatter.14.cloned.1.call-done) | copy-start | bytes 786436
  352.0 57.3 %all-gather.28.cloned.1.call-start = ((), (), s32[]{:S(2)}) async-start(), calls=%async_computation.22 | async-start | bytes 1310720 | tf_op jit(solution)/shard_map/all_gather | solution.py:41
  382.5 68.5 %reduce-scatter.20.cloned.1.call-start = ((), (), s32[]{:S(2)}) async-start(), calls=%async_computation.23 | async-start | bytes 655360 | tf_op jit(solution)/shard_map/reduce_scatter | solution.py:150
  414.4 4.9 copy-start.13
  414.4 9.8 %slice-start = ((s8[8388608]{0:T(1024)(128)(4,1)}), s8[4194304]{0:T(1024)(128)(4,1)S(1)}, s32[]{:S(2)}) async-start(s8[8388608]{0:T(1024)(128)(4,1)} %bitcast.139), calls=%async_computation.31 | async-start | bytes 8388608
  419.4 4.9 slice-start.1
  425.5 1.9 copy-start
  429.7 54.3 %reduce-scatter.22.cloned.1.call-start = ((), (), s32[]{:S(2)}) async-start(), calls=%async_computation.24 | async-start | bytes 1310720 | tf_op jit(solution)/shard_map/reduce_scatter | solution.py:45
  456.7 70.3 %reduce-scatter.26.cloned.1.call-start = ((), (), s32[]{:S(2)}) async-start(), calls=%async_computation.26 | async-start | bytes 2359296 | tf_op jit(solution)/shard_map/reduce_scatter | solution.py:56
  460.1 96.9 %reduce-scatter.16.cloned.1.call-start = ((), (), s32[]{:S(2)}) async-start(), calls=%async_computation.19 | async-start | bytes 1310720 | tf_op jit(solution)/shard_map/reduce_scatter | solution.py:45
  465.5 21.1 %copy-start.4 = (bf16[256,2048]{1,0:T(8,128)(2,1)S(1)}, bf16[256,2048]{1,0:T(8,128)(2,1)}, u32[]{:S(2)}) copy-start(bf16[256,2048]{1,0:T(8,128)(2,1)} %all-gather.12.cloned.1.call-done) | copy-start | bytes 3145732
  465.6 129.7 %reduce-scatter.34.cloned.1.call-start = ((), (), s32[]{:S(2)}) async-start(), calls=%async_computation.30 | async-start | bytes 1179648
  486.6 155.5 %reduce-scatter.24.cloned.1.call-start = ((), (), s32[]{:S(2)}) async-start(), calls=%async_computation.25 | async-start | bytes 2949120 | tf_op jit(solution)/shard_map/reduce_scatter | solution.py:56
  489.2 215.3 %reduce-scatter.32.cloned.1.call-start = ((), (), s32[]{:S(2)}) async-start(), calls=%async_computation.29 | async-start | bytes 6488064 | tf_op jit(solution)/shard_map/reduce_scatter | solution.py:56
  494.9 1.1 copy-start.12
  494.9 272.5 %reduce-scatter.30.cloned.1.call-start = ((), (), s32[]{:S(2)}) async-start(), calls=%async_computation.28 | async-start | bytes 6488064 | tf_op jit(solution)/shard_map/reduce_scatter | solution.py:56
  500.3 1.1 copy-start.10
  500.4 329.4 %reduce-scatter.28.cloned.1.call-start = ((), (), s32[]{:S(2)}) async-start(), calls=%async_computation.27 | async-start | bytes 6488064 | tf_op jit(solution)/shard_map/reduce_scatter | solution.py:56
  505.8 51.2 %copy-start.6 = (bf16[64,2048]{1,0:T(8,128)(2,1)S(1)}, bf16[64,2048]{1,0:T(8,128)(2,1)}, u32[]{:S(2)}) copy-start(bf16[64,2048]{1,0:T(8,128)(2,1)} %reduce-scatter.18.cloned.1.call-done) | copy-start | bytes 786436
  505.8 51.2 %copy-start.8 = (bf16[64,2048]{1,0:T(8,128)(2,1)S(1)}, bf16[64,2048]{1,0:T(8,128)(2,1)}, u32[]{:S(2)}) copy-start(bf16[64,2048]{1,0:T(8,128)(2,1)} %reduce-scatter.22.cloned.1.call-done) | copy-start | bytes 786436
Sparse Core Ops, SparseCore 0:
  21.3 28.2 all-gather.11
  52.0 29.6 all-gather.13
  83.6 28.1 all-gather.15
  115.2 27.1 reduce-scatter.13
  145.5 26.5 all-gather.17
  174.0 42.7 all-gather.21
  218.9 43.3 all-gather.19
  264.5 27.9 all-gather.25
  294.5 43.8 all-gather.23
  352.1 27.1 reduce-scatter.17
  382.6 26.5 all-gather.27
  429.8 21.1 reduce-scatter.19
  456.8 27.1 reduce-scatter.21
  487.1 39.8 reduce-scatter.25
  529.8 27.1 reduce-scatter.15
  560.6 34.6 reduce-scatter.33
  598.5 43.6 reduce-scatter.23
  645.5 59.0 reduce-scatter.31
  708.4 59.0 reduce-scatter.29
  770.7 59.0 reduce-scatter.27

commit v2 on v1

v2 whole, which is shorter than its diff:
```python
import functools
import math

import jax
import jax.numpy as jnp
from jax import lax
from jax.experimental import pallas as pl
from jax.experimental.pallas import tpu as pltpu
from jax.sharding import PartitionSpec as P

EPS = 1e-05
NEG = -1e30
BF = jnp.bfloat16
F32 = jnp.float32
MESH = pl.DeviceIdType.MESH
FC = ("fsdp", "context")


def dot(a, b, ca=1, cb=0):
    return lax.dot_general(a, b, (((ca,), (cb,)), ((), ())), preferred_element_type=F32)


def chunks(total, step):
    return [(at, min(step, total - at)) for at in range(0, total, step)]


class Links:
    def __init__(self, sizes, send_sems, recv_sems):
        self.F, self.C, self.T = sizes
        self.f = lax.axis_index("fsdp")
        self.c = lax.axis_index("context")
        self.t = lax.axis_index("tensor")
        self.h = self.c // 2
        self.core = self.c % 2
        self.H = self.C // 2
        self.send_sems, self.recv_sems = send_sems, recv_sems
        self.used = 0
        self.open = []
        self.sib = (self.f, self.h * 2 + 1 - self.core, self.t)

    def chip(self, df, dh):
        return ((self.f + df) % self.F, ((self.h + dh) % self.H) * 2 + self.core, self.t)

    def block_of(self, df, dh, other=False):
        core = 1 - self.core if other else self.core
        return ((self.f - df) % self.F) * self.C + ((self.h - dh) % self.H) * 2 + core

    def zpeer(self, i):
        return (self.f, self.c, (self.t + i) % self.T)

    def cpeer(self, i):
        return (self.f, (self.c + i) % self.C, self.t)

    def send(self, src, dst, dev):
        n = self.used
        self.used += 1
        copy = pltpu.make_async_remote_copy(
            src_ref=src, dst_ref=dst, send_sem=self.send_sems.at[n],
            recv_sem=self.recv_sems.at[n], device_id=dev, device_id_type=MESH,
        )
        copy.start()
        self.open.append(copy)
        return copy

    def peers(self):
        out = []
        for df in range(self.F):
            for dc in range(self.C):
                if df or dc:
                    out.append(((self.f + df) % self.F, (self.c + dc) % self.C, self.t))
        return out + [self.zpeer(i) for i in range(1, self.T)]

    def barrier(self):
        sem = pltpu.get_barrier_semaphore()
        peers = self.peers()
        for dev in peers:
            pl.semaphore_signal(sem, inc=1, device_id=dev, device_id_type=MESH)
        pl.semaphore_wait(sem, len(peers))

    def finish(self):
        for copy in self.open:
            copy.wait_send()


class Gather:
    def __init__(self, links, full, rows):
        self.k, self.full, self.rows = links, full, rows

    def part(self, block, half=None):
        if half is None:
            return self.full.at[pl.ds(pl.multiple_of(block * self.rows, self.rows), self.rows)]
        n = self.rows // 2
        return self.full.at[pl.ds(pl.multiple_of(block * self.rows + half * n, n), n)]

    def first(self, own):
        k = self.k
        mine = self.part(k.block_of(0, 0))
        self.line = {}
        for df in range(1, k.F):
            self.line[df, 0] = k.send(own, mine, k.chip(df, 0))
        for dh in range(1, k.H):
            self.line[0, dh] = k.send(own, mine, k.chip(0, dh))
        self.twin = [k.send(own, mine, k.sib)]

    def second(self):
        k = self.k
        self.diag = {}
        for (df, dh), copy in self.line.items():
            copy.wait_recv()
            block = k.block_of(df, dh)
            half = 0 if df else 1
            piece = self.part(block, half)
            if df:
                for eh in range(1, k.H):
                    self.diag[df, eh, half] = k.send(piece, piece, k.chip(0, eh))
            else:
                for ef in range(1, k.F):
                    self.diag[ef, dh, half] = k.send(piece, piece, k.chip(ef, 0))
            whole = self.part(block)
            self.twin.append(k.send(whole, whole, k.sib))

    def third(self):
        k = self.k
        for copy in self.diag.values():
            copy.wait_recv()
        for df in range(1, k.F):
            for dh in range(1, k.H):
                whole = self.part(k.block_of(df, dh))
                self.twin.append(k.send(whole, whole, k.sib))

    def done(self):
        for copy in self.twin:
            copy.wait_recv()


def n_gather(F, H):
    a, b, d = F - 1, H - 1, (F - 1) * (H - 1)
    return a + b + 1 + 2 * d + a + b + d


def forward_kernel(
    sizes, hd,
    hidden_ref, seg_ref, segc_ref, pad_ref, cos_ref, sin_ref, gain_ref, wq_ref, wk_ref, wv_ref,
    wo_ref, wd_ref, gout_ref, wg_ref, wu_ref,
    n1_ref, q_ref, kv_ref, attn_ref, lse_ref, mid_ref, n2_ref, gall_ref, w_ref, gains_ref,
    gate_ref, up_ref, down_ref,
    dt, bias, part_f, part_b, slots, sends, recvs, local,
):
    k = Links(sizes, sends, recvs)
    rows, D = hidden_ref.shape
    R, QW = wq_ref.shape
    FB = wg_ref.shape[1]
    span = n1_ref.shape[0]
    length = seg_ref.shape[1]
    nh = QW // hd
    T = k.T
    mine = k.block_of(0, 0)

    aw = Gather(k, w_ref, R)
    own_w = aw.part(mine)
    own_w[:, :QW] = wq_ref[...]
    own_w[:, QW:QW + 2 * hd] = jnp.concatenate([wk_ref[...], wv_ref[...]], axis=1)
    own_w[:, QW + 2 * hd:] = wo_ref[...].astype(F32).T.astype(BF)
    gains_ref[mine] = gain_ref[...].astype(F32)
    k.barrier()
    own_gain = gains_ref.at[mine]
    gain_copies = [k.send(own_gain, own_gain, dev) for dev in k.peers()[: k.F * k.C - 1]]
    aw.first(own_w)
    gw, uw, dw = Gather(k, gate_ref, R), Gather(k, up_ref, R), Gather(k, down_ref, R)

    hidden = hidden_ref[...].astype(F32)
    scale_one = lax.rsqrt(jnp.mean(hidden * hidden, axis=-1, keepdims=True) + EPS)
    for copy in gain_copies:
        copy.wait_recv()

    def gain_row(which):
        return jnp.concatenate(
            [gains_ref[b][:, which * R:(which + 1) * R] for b in range(k.F * k.C)], axis=1
        )

    at_t = pl.ds(pl.multiple_of(k.t * rows, rows), rows)

    def z_gather(full):
        piece = full.at[at_t]
        return [k.send(piece, piece, k.zpeer(i)) for i in range(1, T)]

    n1_ref[at_t] = (hidden * scale_one * gain_row(0)).astype(BF)
    n1_copies = z_gather(n1_ref)
    dt[...] = wd_ref[...].astype(F32).T.astype(BF)
    local_copies = [
        pltpu.make_async_copy(wg_ref, gw.part(mine), local.at[0]),
        pltpu.make_async_copy(wu_ref, uw.part(mine), local.at[1]),
        pltpu.make_async_copy(dt, dw.part(mine), local.at[2]),
    ]
    for copy in local_copies:
        copy.start()
    seg_span = segc_ref[...]
    row_at = k.c * span + lax.broadcasted_iota(jnp.int32, (span, length), 0)
    column = lax.broadcasted_iota(jnp.int32, (span, length), 1)
    keep = (seg_span == seg_ref[...]) & (column <= row_at) & (
        (pad_ref[...] == 1) | (column == row_at)
    )
    bias[...] = jnp.where(keep, 0.0, NEG)
    aw.second()
    gw.first(wg_ref)
    aw.third()
    aw.done()
    for copy in n1_copies:
        copy.wait_recv()
    gall_ref[at_t] = gout_ref[...]
    g_copies = z_gather(gall_ref)

    cos, sin = cos_ref[...], sin_ref[...]
    lane = lax.broadcasted_iota(jnp.int32, (span, 2 * hd), 1)
    low = (lane % hd) < (hd // 2)

    def turn(x, sin_table):
        swapped = jnp.where(low, pltpu.roll(x, 2 * hd - hd // 2, 1), pltpu.roll(x, hd // 2, 1))
        return x * cos + swapped * sin_table

    n1 = n1_ref[...]
    for n in range(QW // (2 * hd)):
        at = n * 2 * hd
        pre = turn(dot(n1, w_ref[:, at:at + 2 * hd]), sin).astype(BF)
        q_ref[2 * n] = pre[:, :hd]
        q_ref[2 * n + 1] = pre[:, hd:]
    pre = dot(n1, w_ref[:, QW:QW + 2 * hd])
    at_c = pl.ds(pl.multiple_of(k.c * span, span), span)
    kv_ref[at_c] = jnp.where(lane < hd, turn(pre, sin), pre).astype(BF)
    own_kv = kv_ref.at[at_c]
    kv_copies = [k.send(own_kv, own_kv, k.cpeer(i)) for i in range(1, k.C)]
    gw.second()
    uw.first(wu_ref)
    for copy in kv_copies:
        copy.wait_recv()

    @pl.loop(0, nh)
    def _(n):
        scores = dot(q_ref[n], kv_ref[:, :hd], 1, 1) * hd ** (-0.5) + bias[...]
        top = jnp.max(scores, axis=-1, keepdims=True)
        e = jnp.exp(scores - top)
        total = jnp.sum(e, axis=-1, keepdims=True)
        attn_ref[n] = dot((e / total).astype(BF), kv_ref[:, hd:]).astype(BF)
        lse_ref[n] = top + jnp.log(total)

    attn = jnp.concatenate([attn_ref[n] for n in range(nh)], axis=1)

    @pl.loop(0, D // 256)
    def _(n):
        at = pl.ds(pl.multiple_of(n * 256, 256), 256)
        part = dot(attn, w_ref[at, QW + 2 * hd:], 1, 1)
        part_f[:, at] = part
        part_b[:, at] = part.astype(BF)

    part_copies = []
    for i in range(1, T):
        dest = (k.t + i) % T
        src = part_b.at[pl.ds(pl.multiple_of(dest * rows, rows), rows)]
        part_copies.append(k.send(src, slots.at[i - 1], k.zpeer(i)))
    gw.third()
    uw.second()
    dw.first(dt)
    middle = hidden + part_f[at_t]
    for i in range(1, T):
        part_copies[i - 1].wait_recv()
        middle = middle + slots[i - 1].astype(F32)
    mid_ref[...] = middle
    scale_two = lax.rsqrt(jnp.mean(middle * middle, axis=-1, keepdims=True) + EPS)
    n2_ref[at_t] = (middle * scale_two * gain_row(1)).astype(BF)
    n2_copies = z_gather(n2_ref)
    uw.third()
    dw.second()
    dw.third()
    for copy in n2_copies + g_copies:
        copy.wait_recv()
    for w in (gw, uw, dw):
        w.done()
    for copy in local_copies:
        copy.wait()
    k.finish()


def forward(sizes, hd, hidden, seg, seg_span, pad, cos, sin, gains, wq, wk, wv, wo, wd, g_out, wg, wu):
    F, C, T = sizes
    rows, D = hidden.shape
    R, QW = wq.shape
    FB = wg.shape[1]
    span, length, nh = rows * T, seg.shape[1], QW // hd
    vm = pl.BlockSpec(memory_space=pltpu.VMEM)
    hbm = pl.BlockSpec(memory_space=pl.ANY)
    H = C // 2
    n_sems = 4 * n_gather(F, H) + F * C - 1 + 4 * (T - 1) + C - 1
    S = jax.ShapeDtypeStruct
    return pl.pallas_call(
        functools.partial(forward_kernel, sizes, hd),
        out_shape=(
            S((span, D), BF), S((nh, span, hd), BF), S((length, 2 * hd), BF), S((nh, span, hd), BF),
            S((nh, span, 1), F32), S((rows, D), F32), S((span, D), BF), S((span, D), BF),
            S((D, 2 * QW + 2 * hd), BF), S((F * C, 1, 2 * R), F32),
            S((D, FB), BF), S((D, FB), BF), S((D, FB), BF),
        ),
        in_specs=[vm] * 13 + [hbm] * 2,
        out_specs=[vm] * 10 + [hbm] * 3,
        scratch_shapes=[
            pltpu.VMEM((R, FB), BF), pltpu.VMEM((span, length), F32), pltpu.VMEM((span, D), F32),
            pltpu.VMEM((span, D), BF), pltpu.VMEM((T - 1, rows, D), BF),
            pltpu.SemaphoreType.DMA((n_sems,)), pltpu.SemaphoreType.DMA((n_sems,)),
            pltpu.SemaphoreType.DMA((3,)),
        ],
        compiler_params=pltpu.CompilerParams(
            collective_id=0, has_side_effects=True, vmem_limit_bytes=56 * 2**20
        ),
        name="forward",
    )(hidden, seg, seg_span, pad, cos, sin, gains, wq, wk, wv, wo, wd, g_out, wg, wu)


def rotate_back(x, cos, sin, hd):
    half = hd // 2
    a, b = x[..., :half], x[..., half:]
    ct, st = cos[:, None, :half], sin[:, None, :half]
    return jnp.concatenate([a * ct + b * st, b * ct - a * st], axis=-1)


def rows_gather(x):
    return lax.all_gather(x, "tensor", axis=0, tiled=True)


def rows_sum(x):
    return lax.psum_scatter(x.astype(BF), "tensor", scatter_dimension=0, tiled=True).astype(F32)


def scatter_g(g):
    return lax.psum_scatter(g.astype(BF), FC, scatter_dimension=0, tiled=True).astype(F32)


def norm_back(grad_normed, vectors, inv_scale, gain_row):
    unit_rows = vectors * inv_scale
    weighted = grad_normed * gain_row
    grad_gain = jnp.sum(grad_normed * unit_rows, axis=0)
    grad_vectors = inv_scale * (
        weighted - unit_rows * jnp.mean(weighted * unit_rows, axis=-1, keepdims=True)
    )
    return (grad_vectors, grad_gain)


def body(hidden_in, segment_ids, pad_mask, attn_gain, w_query, w_key, w_value, w_out,
         mlp_gain, w_gate, w_up, w_down, cotangent):
    hidden_in, cotangent = hidden_in[0], cotangent[0]
    rows, D = hidden_in.shape
    sizes = tuple(lax.axis_size(n) for n in ("fsdp", "context", "tensor"))
    F, C, T = sizes
    c, t = lax.axis_index("context"), lax.axis_index("tensor")
    length = segment_ids.shape[1]
    span = length // C
    hd = w_key.shape[1]
    QW = w_query.shape[1]
    R = w_query.shape[0]
    nh = QW // hd
    start = c * span
    seg_span = lax.dynamic_slice_in_dim(segment_ids[0], start, span, 0)[:, None]
    row_at = start + jnp.arange(span, dtype=jnp.int32)
    first = jnp.sum((segment_ids < seg_span).astype(jnp.int32), axis=1)
    frequency = jnp.exp(
        -((jnp.arange(2 * hd) % (hd // 2)).astype(F32) * (2.0 / hd)) * math.log(10000.0)
    )
    sign = jnp.where(jnp.arange(2 * hd) % hd < hd // 2, -1.0, 1.0)
    angles = (row_at - first).astype(F32)[:, None] * frequency
    cos, sin = jnp.cos(angles), jnp.sin(angles) * sign
    keep = lax.dynamic_slice_in_dim(pad_mask[0], start + t * rows, rows, 0).astype(F32)[:, None]
    g_out = cotangent.astype(F32) * keep
    gains = jnp.concatenate([attn_gain, mlp_gain])[None]
    (n1, q, kv, attn, lse, middle, n2, g_all, w, gain_all, gate_all, up_all, down_all) = forward(
        sizes, hd, hidden_in, segment_ids, seg_span, pad_mask, cos, sin, gains,
        w_query, w_key, w_value, w_out, w_down, g_out.astype(BF), w_gate, w_up,
    )
    gain_one = gain_all[:, 0, :R].reshape(1, D)
    gain_two = gain_all[:, 0, R:].reshape(1, D)
    hidden = hidden_in.astype(F32)
    scale_one = lax.rsqrt(jnp.mean(hidden * hidden, axis=-1, keepdims=True) + EPS)
    scale_two = lax.rsqrt(jnp.mean(middle * middle, axis=-1, keepdims=True) + EPS)
    gate = dot(n2, gate_all)
    up = dot(n2, up_all)
    sig = jax.nn.sigmoid(gate)
    inner = (gate * sig * up).astype(BF)
    block_out = (keep * (middle + rows_sum(dot(inner, down_all, 1, 1)))).astype(BF)
    grad_down = dot(g_all, inner, 0, 0)
    g_inner = dot(g_all, down_all)
    g_gate = (g_inner * up * sig * (1.0 + gate * (1.0 - sig))).astype(BF)
    g_up = (g_inner * gate * sig).astype(BF)
    g_n2 = rows_sum(dot(g_gate, gate_all, 1, 1) + dot(g_up, up_all, 1, 1))
    grad_gate = dot(n2, g_gate, 0, 0)
    grad_up = dot(n2, g_up, 0, 0)
    d_mid, grad_gain_two = norm_back(g_n2, middle, scale_two, gain_two)
    g_mid = g_out + d_mid
    gm_all = rows_gather(g_mid.astype(BF))
    attn = jnp.swapaxes(attn, 0, 1).reshape(span, QW)
    grad_out = dot(gm_all, attn, 0, 0)
    out_t = w[:, QW + 2 * hd:]
    g_attn = dot(gm_all, out_t).astype(BF).reshape(span, nh, hd)
    seg, pad = segment_ids[0], pad_mask[0]
    columns = jnp.arange(length, dtype=jnp.int32)
    allowed = (
        (seg_span == seg[None, :])
        & (columns[None, :] <= row_at[:, None])
        & ((pad[None, :] == 1) | (columns[None, :] == row_at[:, None]))
    )
    key, value = kv[:, :hd], kv[:, hd:]
    scale = hd ** (-0.5)
    scores = jnp.einsum("hqd,td->hqt", q, key, preferred_element_type=F32) * scale
    probs = jnp.exp(jnp.where(allowed[None], scores, NEG) - lse)
    dp = jnp.einsum("qhd,td->hqt", g_attn, value, preferred_element_type=F32)
    delta = jnp.sum(probs * dp, axis=-1, keepdims=True)
    ds = (probs * (dp - delta)).astype(BF)
    g_q = jnp.einsum("hqt,td->qhd", ds, key, preferred_element_type=F32) * scale
    g_k = jnp.einsum("hqt,hqd->td", ds, q, preferred_element_type=F32) * scale
    g_v = jnp.einsum("hqt,qhd->td", probs.astype(BF), g_attn, preferred_element_type=F32)
    g_kv = lax.psum_scatter(
        jnp.concatenate([g_k, g_v], axis=1), "context", scatter_dimension=0, tiled=True
    )
    sin = sin * sign
    g_q = rotate_back(g_q, cos, sin, hd).astype(BF).reshape(span, -1)
    g_k = rotate_back(g_kv[:, None, :hd], cos, sin, hd).astype(BF)[:, 0]
    g_qkv = jnp.concatenate([g_q, g_k, g_kv[:, hd:].astype(BF)], axis=1)
    g_n1 = rows_sum(dot(g_qkv, w[:, :QW + 2 * hd], 1, 1))
    grad_qkv = dot(n1, g_qkv, 0, 0)
    d_hid, grad_gain_one = norm_back(g_n1, hidden, scale_one, gain_one)
    grads = jnp.stack([grad_gain_one, grad_gain_two])
    grad_down = scatter_g(grad_down)
    grad_gate = scatter_g(grad_gate)
    grad_up = scatter_g(grad_up)
    grad_out = scatter_g(grad_out)
    grad_qkv = scatter_g(grad_qkv)
    grads = lax.psum(grads, "tensor")
    grads = lax.psum_scatter(grads, FC, scatter_dimension=1, tiled=True)
    return (
        block_out[None], (g_mid + d_hid)[None], grads[0], grad_qkv[:, :QW],
        grad_qkv[:, QW:QW + hd], grad_qkv[:, QW + hd:], grad_out.T, grads[1],
        grad_gate, grad_up, grad_down.T,
    )


def solution(mesh):
    rows = P("fsdp", ("context", "tensor"), None)
    tail = (P(FC), P(FC, "tensor"), P(FC, "tensor"), P(FC, "tensor"), P("tensor", FC),
            P(FC), P(FC, "tensor"), P(FC, "tensor"), P("tensor", FC))
    in_specs = (rows, P("fsdp", None), P("fsdp", None)) + tail + (rows,)
    out_specs = (rows, rows) + tail
    return jax.shard_map(body, mesh=mesh, in_specs=in_specs, out_specs=out_specs, check_vma=False)
```

time: 840 us -> 634 us (0.75)
  waiting for transfers between devices: 650 us -> 383 us
  Pallas kernels: 0 us -> 109 us
  blocking collectives: 36.7 us -> 11.7 us
  matrix products: 87.3 us -> 68.4 us
    all_gather x5 -> x0, waiting for transfers between devices: 173 us -> none  [gather_w(): return lax.all_gather(w, FC, axis=axis, tiled=True)]
    pallas_call x0 -> x1, Pallas kernels: none -> 109 us  [forward(): pl.pallas_call(functools.partial(forward_kernel, sizes, hd), out_shape=(S...]
    all_gather x4 -> x1, waiting for transfers between devices: 93.7 us -> 20 us  [rows_gather(): return lax.all_gather(x, 'tensor', axis=0, tiled=True)]
    all_gather x3 -> x0, blocking collectives: 25 us -> none  [the longest x2 19.2 us: gather_w(): return lax.all_gather(w, FC, axis=axis, tiled=True)]
    reduce_scatter x4 -> x3, waiting for transfers between devices: 92.2 us -> 72.6 us  [rows_sum(): lax.psum_scatter(x.astype(BF), 'tensor', scatter_dimension=0, tiled=True)]
    dot_general x20 -> x18, matrix products: 82.5 us -> 68.4 us  [the longest x13 46.8 us: dot(): lax.dot_general(a, b, (((ca,), (cb,)), ((), ())), preferred_element_type=...]
    convert_element_type x13 -> x7, other arithmetic: 17 us -> 11.3 us  [the longest x2 4.6 us: scatter_g(): lax.psum_scatter(g.astype(BF), FC, scatter_dimension=0, tiled=True)]
    unnamed x21 -> x12, waiting for transfers between devices: 38.8 us -> 36.7 us
  transfers between devices with their start and end apart: 20 -> 11, of which waited for: 20 -> 11; matrix products, arithmetic and copies ran while one was open for 10% -> 8% of each run, Pallas kernels for 0% -> 0%
where the time goes in v2:
time: 634 us; the launch traced here: 633 us
  waiting for transfers between devices  383 us (60%)
  Pallas kernels  109 us (17%)
  matrix products  68.4 us (11%)
  other arithmetic  23.6 us (4%)
  local copies, waits for them, and re-layouts  22.4 us (4%)
  between operations  14.5 us (2%)
  blocking collectives  11.7 us (2%)
    reduce_scatter x5, waiting for transfers between devices, scatter_g(): lax.psum_scatter(g.astype(BF), FC, scatter_dimension=0, tiled=True)  236 us
    pallas_call x1, Pallas kernels, forward(): pl.pallas_call(functools.partial(forward_kernel, sizes, hd), out_shape=(S...  109 us
    reduce_scatter x3, waiting for transfers between devices, rows_sum(): lax.psum_scatter(x.astype(BF), 'tensor', scatter_dimension=0, tiled=True)  72.6 us
    dot_general x13, matrix products, dot(): lax.dot_general(a, b, (((ca,), (cb,)), ((), ())), preferred_element_type=...  46.8 us
    unnamed x12, waiting for transfers between devices  36.7 us
    all_gather x1, waiting for transfers between devices, rows_gather(): return lax.all_gather(x, 'tensor', axis=0, tiled=True)  20 us
    reduce_scatter x1, waiting for transfers between devices, body(): lax.psum_scatter(jnp.concatenate([g_k, g_v], axis=1), 'context', scatter_...  17.5 us
  transfers between devices with their start and end apart: 11, of which 11 were waited for; matrix products, arithmetic and copies ran while one was open for 8% of the time, Pallas kernels for 0%

profile of v2, /device:TPU:0, one launch (start us, length us, event | category | flops | bytes accessed | tf_op | source)
XLA Modules:
  0.0 633.3 jit_solution(14762902524258129248)
XLA Ops:
  10.8 1.5 copy.90.wk_ref
  12.3 1.5 copy.91.wv_ref
  15.3 1.8 fusion.41.gout_ref
  17.1 1.2 fusion.51
  18.3 108.8 %forward.1 = (bf16[256,2048]{1,0:T(8,128)(2,1)}, bf16[8,256,64]{2,1,0:T(8,128)(2,1)}, bf16[1024,128]{1,0:T(8,128)(2,1)}, bf16[8,256,64]{2,1,0:T(8,128)(2,1)}, f3...) custom-call(bf16[64,2048]{1,0:T(8,128)(2,1)} %bitcast.131, ...), custom_call_target="tpu_custom_call" | custom-call | tf_op jit(solution)/shard_map/forward/pallas_call | solution.py:294
  127.2 4.9 fusion.71
  132.1 1.8 fusion.72
  134.2 3.1 multiply_convert_fusion
  137.4 1.9 fusion.73
  139.3 2.8 fusion.9
  142.4 27.3 %reduce-scatter.15.cloned.1.call-done = bf16[64,2048]{1,0:T(8,128)(2,1)} async-done(((bf16[256,2048]{1,0:T(8,128)(2,1)}), bf16[64,2048]{1,0:T(8,128)(2,1)}) %reduce-scatter.15.cloned.1.call-update) | async-done | bytes 262160 | tf_op jit(solution)/shard_map/reduce_scatter | solution.py:329
  169.7 1.2 fusion.37
  171.0 1.9 fusion.67
  174.1 5.5 fusion.45
  179.6 20.0 %all-gather.2.cloned.1.call-done = bf16[256,2048]{1,0:T(8,128)(2,1)} async-done(((bf16[64,2048]{1,0:T(8,128)(2,1)}), bf16[256,2048]{1,0:T(8,128)(2,1)}) %all-gather.2.cloned.1.call-update) | async-done | bytes 1048592 | tf_op jit(solution)/shard_map/all_gather | solution.py:325
  199.6 2.6 fusion.20
  202.4 5.6 fusion.15
  208.1 5.5 fusion
  213.6 2.3 fusion.2
  215.9 2.0 copy-done
  217.9 1.3 fusion.18
  220.3 3.6 fusion.19
  223.9 17.5 %reduce-scatter.17.cloned.1.call-done = f32[256,128]{1,0:T(8,128)} async-done(((f32[1024,128]{1,0:T(8,128)}), f32[256,128]{1,0:T(8,128)}) %reduce-scatter.17.cloned.1.call-update) | async-done | bytes 131088 | tf_op jit(solution)/shard_map/reduce_scatter | solution.py:417
  244.1 3.8 fusion.10
  248.0 1.2 copy.107
  249.2 2.1 convolution_convert_fusion.4
  251.7 5.9 convolution_convert_fusion.5
  257.9 17.4 %reduce-scatter.19.cloned.1.call-done = bf16[64,2048]{1,0:T(8,128)(2,1)} async-done(((bf16[256,2048]{1,0:T(8,128)(2,1)}), bf16[64,2048]{1,0:T(8,128)(2,1)}) %reduce-scatter.19.cloned.1.call-update) | async-done | bytes 262160 | tf_op jit(solution)/shard_map/reduce_scatter | solution.py:329
  275.2 1.3 fusion.40
  276.5 1.3 copy.125
  277.9 5.4 convolution_convert_fusion
  284.5 4.3 convolution_convert_fusion.1
  288.9 5.6 convolution_convert_fusion.2
  294.6 2.5 convolution_convert_fusion.3
  297.1 21.5 %reduce-scatter.23.cloned.1.call-done = bf16[256,512]{1,0:T(8,128)(2,1)} async-done(((bf16[2048,512]{1,0:T(8,128)(2,1)}), bf16[256,512]{1,0:T(8,128)(2,1)}) %reduce-scatter.23.cloned.1.call-update) | async-done | bytes 262160 | tf_op jit(solution)/shard_map/reduce_scatter | solution.py:333
  320.6 27.9 %reduce-scatter.13.cloned.1.call-done = bf16[64,2048]{1,0:T(8,128)(2,1)} async-done(((bf16[256,2048]{1,0:T(8,128)(2,1)}), bf16[64,2048]{1,0:T(8,128)(2,1)}) %reduce-scatter.13.cloned.1.call-update) | async-done | bytes 262160 | tf_op jit(solution)/shard_map/reduce_scatter | solution.py:329
  348.5 2.3 fusion.33
  350.8 36.6 %reduce-scatter.31.cloned.1.call-done = f32[256,2]{1,0:T(8,128)} async-done(((f32[2048,2]{1,0:T(8,128)}), f32[256,2]{1,0:T(8,128)}) %reduce-scatter.31.cloned.1.call-update) | async-done | bytes 2064
  388.3 11.7 %psum.8 = f32[2,256]{1,0:T(2,128)S(1)} all-reduce(f32[2,256]{1,0:T(2,128)S(1)} %copy.126), channel_id=1, replica_groups=mesh['fsdp'=2,'context'=4,'tensor'=4] {'tensor'}, use_global_device_ids=true, to_apply=%region_12.13 | all-reduce | flops 512 | bytes 4096 | tf_op jit(solution)/shard_map/psum | solution.py:433
  400.6 49.6 %reduce-scatter.29.cloned.1.call-done = bf16[256,1408]{1,0:T(8,128)(2,1)} async-done(((bf16[2048,1408]{1,0:T(8,128)(2,1)}), bf16[256,1408]{1,0:T(8,128)(2,1)}) %reduce-scatter.29.cloned.1.call-update) | async-done | bytes 720912 | tf_op jit(solution)/shard_map/reduce_scatter | solution.py:333
  450.2 1.2 convert_bitcast_fusion
  451.4 1.5 copy.111
  453.0 59.8 %reduce-scatter.27.cloned.1.call-done = bf16[256,1408]{1,0:T(8,128)(2,1)} async-done(((bf16[2048,1408]{1,0:T(8,128)(2,1)}), bf16[256,1408]{1,0:T(8,128)(2,1)}) %reduce-scatter.27.cloned.1.call-update) | async-done | bytes 720912 | tf_op jit(solution)/shard_map/reduce_scatter | solution.py:333
  512.7 2.3 convert_element_type.147
  515.0 60.5 %reduce-scatter.25.cloned.1.call-done = bf16[256,1408]{1,0:T(8,128)(2,1)} async-done(((bf16[2048,1408]{1,0:T(8,128)(2,1)}), bf16[256,1408]{1,0:T(8,128)(2,1)}) %reduce-scatter.25.cloned.1.call-update) | async-done | bytes 720912 | tf_op jit(solution)/shard_map/reduce_scatter | solution.py:333
  575.5 2.3 convert_element_type.145
  577.8 44.7 %reduce-scatter.21.cloned.1.call-done = bf16[256,640]{1,0:T(8,128)(2,1)} async-done(((bf16[2048,640]{1,0:T(8,128)(2,1)}), bf16[256,640]{1,0:T(8,128)(2,1)}) %reduce-scatter.21.cloned.1.call-update) | async-done | bytes 327696 | tf_op jit(solution)/shard_map/reduce_scatter | solution.py:333
  624.9 1.8 slice.89
  (123 shorter events, 18.5 us)
Async XLA Ops:
  7.2 162.6 %reduce-scatter.15.cloned.1.call-start = ((), (), s32[]{:S(2)}) async-start(), calls=%async_computation.11 | async-start | bytes 1310720 | tf_op jit(solution)/shard_map/reduce_scatter | solution.py:329
  127.2 4.9 copy-start.1
  127.2 4.9 copy-start.22
  127.2 6.8 %slice-start.2 = ((s8[5767168]{0:T(1024)(128)(4,1)}), s8[4194304]{0:T(1024)(128)(4,1)S(1)}, s32[]{:S(2)}) async-start(s8[5767168]{0:T(1024)(128)(4,1)} %bitcast.155), calls=%async_computation.23 | async-start | bytes 8388608
  132.1 1.9 copy-start.9
  132.1 2.1 slice-start.3
  132.1 5.3 slice-start.4
  134.2 3.2 slice-start.5
  137.4 1.9 copy-start.15
  137.4 1.9 copy-start.16
  139.3 2.9 copy-start.2
  139.3 3.1 copy-start.21
  139.3 31.7 %copy-start.7 = (bf16[1,64,2048]{2,1,0:T(8,128)(2,1)S(1)}, bf16[1,64,2048]{2,1,0:T(8,128)(2,1)}, u32[]{:S(2)}) copy-start(bf16[1,64,2048]{2,1,0:T(8,128)(2,1)} %param.25) | copy-start | bytes 786436
  139.3 33.9 %copy-start.14 = (f32[8,256,1]{2,1,0:T(8,128)S(1)}, f32[8,256,1]{2,1,0:T(8,128)}, u32[]{:S(2)}) copy-start(f32[8,256,1]{2,1,0:T(8,128)} %get-tuple-element.33) | copy-start | bytes 24580
  139.3 34.2 %copy-start.20 = (s32[1,1024]{1,0:T(1,128)S(1)}, s32[1,1024]{1,0:T(1,128)}, u32[]{:S(2)}) copy-start(s32[1,1024]{1,0:T(1,128)} %pad_ref.1) | copy-start | bytes 12292
  139.3 34.3 %copy-start.19 = (s32[1,1024]{1,0:T(1,128)S(1)}, s32[1,1024]{1,0:T(1,128)}, u32[]{:S(2)}) copy-start(s32[1,1024]{1,0:T(1,128)} %seg_ref.1) | copy-start | bytes 12292
  139.3 34.7 %copy-start.6 = (bf16[1024,128]{1,0:T(8,128)(2,1)S(1)}, bf16[1024,128]{1,0:T(8,128)(2,1)}, u32[]{:S(2)}) copy-start(bf16[1024,128]{1,0:T(8,128)(2,1)} %get-tuple-element.31) | copy-start | bytes 786436
  142.2 57.5 %all-gather.2.cloned.1.call-start = ((), (), s32[]{:S(2)}) async-start(), calls=%async_computation.12 | async-start | bytes 1310720 | tf_op jit(solution)/shard_map/all_gather | solution.py:325
  172.9 68.6 %reduce-scatter.17.cloned.1.call-start = ((), (), s32[]{:S(2)}) async-start(), calls=%async_computation.13 | async-start | bytes 655360 | tf_op jit(solution)/shard_map/reduce_scatter | solution.py:417
  202.4 11.2 %slice-start = ((s8[8388608]{0:T(1024)(128)(4,1)}), s8[4194304]{0:T(1024)(128)(4,1)S(1)}, s32[]{:S(2)}) async-start(s8[8388608]{0:T(1024)(128)(4,1)} %bitcast.129), calls=%async_computation.21 | async-start | bytes 8388608
  202.4 11.2 %slice-start.1 = ((s8[8388608]{0:T(1024)(128)(4,1)}), s8[4194304]{0:T(1024)(128)(4,1)S(1)}, s32[]{:S(2)}) async-start(s8[8388608]{0:T(1024)(128)(4,1)} %bitcast.129), calls=%async_computation.22 | async-start | bytes 8388608
  213.6 4.3 copy-start.18
  215.9 2.0 copy-start
  217.9 2.4 copy-start.4
  217.9 24.5 %copy-start.11 = (f32[256,128]{1,0:T(8,128)S(1)}, f32[256,128]{1,0:T(8,128)}, u32[]{:S(2)}) copy-start(f32[256,128]{1,0:T(8,128)} %get-tuple-element.100.sin_ref) | copy-start | bytes 393220
  220.2 55.0 %reduce-scatter.19.cloned.1.call-start = ((), (), s32[]{:S(2)}) async-start(), calls=%async_computation.14 | async-start | bytes 1310720 | tf_op jit(solution)/shard_map/reduce_scatter | solution.py:329
  244.0 5.2 copy-start.13
  247.9 70.7 %reduce-scatter.23.cloned.1.call-start = ((), (), s32[]{:S(2)}) async-start(), calls=%async_computation.16 | async-start | bytes 2359296 | tf_op jit(solution)/shard_map/reduce_scatter | solution.py:333
  251.4 6.3 copy-start.3
  251.4 97.1 %reduce-scatter.13.cloned.1.call-start = ((), (), s32[]{:S(2)}) async-start(), calls=%async_computation.10 | async-start | bytes 1310720 | tf_op jit(solution)/shard_map/reduce_scatter | solution.py:329
  251.7 26.2 %copy-start.10 = (bf16[256,2048]{1,0:T(8,128)(2,1)S(1)}, bf16[256,2048]{1,0:T(8,128)(2,1)}, u32[]{:S(2)}) copy-start(bf16[256,2048]{1,0:T(8,128)(2,1)} %get-tuple-element.29) | copy-start | bytes 3145732
  257.6 129.7 %reduce-scatter.31.cloned.1.call-start = ((), (), s32[]{:S(2)}) async-start(), calls=%async_computation.20 | async-start | bytes 1179648
  277.9 172.3 %reduce-scatter.29.cloned.1.call-start = ((), (), s32[]{:S(2)}) async-start(), calls=%async_computation.19 | async-start | bytes 6488064 | tf_op jit(solution)/shard_map/reduce_scatter | solution.py:333
  283.4 1.1 copy-start.17
  283.4 229.3 %reduce-scatter.27.cloned.1.call-start = ((), (), s32[]{:S(2)}) async-start(), calls=%async_computation.18 | async-start | bytes 6488064 | tf_op jit(solution)/shard_map/reduce_scatter | solution.py:333
  288.8 5.7 copy-start.5
  288.9 286.7 %reduce-scatter.25.cloned.1.call-start = ((), (), s32[]{:S(2)}) async-start(), calls=%async_computation.17 | async-start | bytes 6488064 | tf_op jit(solution)/shard_map/reduce_scatter | solution.py:333
  294.5 54.0 %copy-start.8 = (bf16[64,2048]{1,0:T(8,128)(2,1)S(1)}, bf16[64,2048]{1,0:T(8,128)(2,1)}, u32[]{:S(2)}) copy-start(bf16[64,2048]{1,0:T(8,128)(2,1)} %reduce-scatter.15.cloned.1.call-done) | copy-start | bytes 786436
  294.5 54.0 %copy-start.12 = (bf16[64,2048]{1,0:T(8,128)(2,1)S(1)}, bf16[64,2048]{1,0:T(8,128)(2,1)}, u32[]{:S(2)}) copy-start(bf16[64,2048]{1,0:T(8,128)(2,1)} %reduce-scatter.19.cloned.1.call-done) | copy-start | bytes 786436
  294.5 328.0 %reduce-scatter.21.cloned.1.call-start = ((), (), s32[]{:S(2)}) async-start(), calls=%async_computation.15 | async-start | bytes 2949120 | tf_op jit(solution)/shard_map/reduce_scatter | solution.py:333
Sparse Core Ops, SparseCore 0:
  142.3 27.4 reduce-scatter.14
  173.0 26.5 all-gather.1
  220.3 21.1 reduce-scatter.16
  248.0 27.1 reduce-scatter.18
  278.7 39.8 reduce-scatter.22
  321.3 27.1 reduce-scatter.12
  352.6 34.7 reduce-scatter.30
  391.1 59.0 reduce-scatter.28
  453.7 59.0 reduce-scatter.26
  516.4 59.0 reduce-scatter.24
  578.8 43.6 reduce-scatter.20

commit v3 on v2

--- a/solution.py
+++ b/solution.py
@@ -77,9 +77,10 @@
             pl.semaphore_signal(sem, inc=1, device_id=dev, device_id_type=MESH)
         pl.semaphore_wait(sem, len(peers))
 
-    def finish(self):
-        for copy in self.open:
+    def finish(self, copies=None):
+        for copy in list(self.open) if copies is None else copies:
             copy.wait_send()
+            self.open.remove(copy)
 
 
 class Gather:
@@ -314,33 +315,328 @@
     )(hidden, seg, seg_span, pad, cos, sin, gains, wq, wk, wv, wo, wd, g_out, wg, wu)
 
 
-def rotate_back(x, cos, sin, hd):
-    half = hd // 2
-    a, b = x[..., :half], x[..., half:]
-    ct, st = cos[:, None, :half], sin[:, None, :half]
-    return jnp.concatenate([a * ct + b * st, b * ct - a * st], axis=-1)
-
-
-def rows_gather(x):
-    return lax.all_gather(x, "tensor", axis=0, tiled=True)
-
-
-def rows_sum(x):
-    return lax.psum_scatter(x.astype(BF), "tensor", scatter_dimension=0, tiled=True).astype(F32)
-
-
-def scatter_g(g):
-    return lax.psum_scatter(g.astype(BF), FC, scatter_dimension=0, tiled=True).astype(F32)
-
-
-def norm_back(grad_normed, vectors, inv_scale, gain_row):
-    unit_rows = vectors * inv_scale
-    weighted = grad_normed * gain_row
-    grad_gain = jnp.sum(grad_normed * unit_rows, axis=0)
-    grad_vectors = inv_scale * (
-        weighted - unit_rows * jnp.mean(weighted * unit_rows, axis=-1, keepdims=True)
+def backward_kernel(
+    sizes, hd,
+    hidden_ref, seg_ref, segc_ref, pad_ref, cos_ref, sin_ref, keep_ref, n1_ref, q_ref, kv_ref,
+    attn_ref, lse_ref, mid_ref, n2_ref, gall_ref, gains_ref, w_hbm, gate_hbm, up_hbm, down_hbm,
+    out_ref, hid_ref, gg_ref, sum_down, sum_gate, sum_up, sum_out, sum_qkv,
+    w_v, gate_v, up_v, down_v, xt_a, xt_b, inner, g_gate, g_up, gm, bias, part_f, part_b, part2_b,
+    slots, slots2, slots3, twin_down, twin_gate, twin_up, twin_out, twin_qkv, g_attn, g_q, g_qkv,
+    g_kv, g_kvb, kv_slots, gz, gz_slots, gx, gx_slots, sends, recvs, local,
+):
+    k = Links(sizes, sends, recvs)
+    rows, D = hidden_ref.shape
+    T, F, C, H = k.T, k.F, k.C, k.H
+    FC_ = F * C
+    R = D // FC_
+    span = n1_ref.shape[0]
+    length = seg_ref.shape[1]
+    nh = q_ref.shape[0]
+    QW = nh * hd
+    QKV = QW + 2 * hd
+    FB = gate_v.shape[1]
+    scale = hd ** (-0.5)
+    loads = [
+        pltpu.make_async_copy(src, dst, local.at[i])
+        for i, (src, dst) in enumerate(
+            ((gate_hbm, gate_v), (up_hbm, up_v), (down_hbm, down_v), (w_hbm, w_v))
+        )
+    ]
+    for copy in loads:
+        copy.start()
+    k.barrier()
+    at_t = pl.ds(pl.multiple_of(k.t * rows, rows), rows)
+    n2 = n2_ref[...]
+    g_all = gall_ref[...]
+    for copy in loads[:3]:
+        copy.wait()
+
+    for at, n in chunks(FB, 256):
+        gate = dot(n2, gate_v[:, at:at + n])
+        up = dot(n2, up_v[:, at:at + n])
+        sig = jax.nn.sigmoid(gate)
+        inner[:, at:at + n] = (gate * sig * up).astype(BF)
+        g_in = dot(g_all, down_v[:, at:at + n])
+        g_gate[:, at:at + n] = (g_in * up * sig * (1.0 + gate * (1.0 - sig))).astype(BF)
+        g_up[:, at:at + n] = (g_in * gate * sig).astype(BF)
+
+    def z_scatter(src, dst):
+        copies = []
+        for i in range(1, T):
+            dest = (k.t + i) % T
+            piece = src.at[pl.ds(pl.multiple_of(dest * rows, rows), rows)]
+            copies.append(k.send(piece, dst.at[i - 1], k.zpeer(i)))
+        return copies
+
+    def z_gather(full):
+        piece = full.at[at_t]
+        return [k.send(piece, piece, k.zpeer(i)) for i in range(1, T)]
+
+    @pl.loop(0, D // 256)
+    def _(n):
+        at = pl.ds(pl.multiple_of(n * 256, 256), 256)
+        part = dot(g_gate[...], gate_v[at], 1, 1) + dot(g_up[...], up_v[at], 1, 1)
+        part_f[:, at] = part
+        part_b[:, at] = part.astype(BF)
+
+    gn2_copies = z_scatter(part_b, slots)
+    own_gn2 = part_f[at_t]
+
+    def turn_over(src, dst):
+        @pl.loop(0, D // 256)
+        def _(n):
+            at = pl.ds(pl.multiple_of(n * 256, 256), 256)
+            dst[at] = src[:, at].astype(F32).T.astype(BF)
+
+    turn_over(gall_ref, xt_a)
+    turn_over(n2_ref, xt_b)
+
+    def block_at(s, core):
+        df, dh = s // H, s % H
+        b = ((k.f + df) % F) * C + ((k.h + dh) % H) * 2 + core
+        return pl.ds(pl.multiple_of(b * R, R), R)
+
+    class Grad:
+        def __init__(self, xt, y, width, stage, lanes, twin, out):
+            self.xt, self.y, self.width, self.stage = xt, y, width, stage
+            self.lanes, self.twin, self.out = lanes, twin, out
+
+        def piece(self, s, core):
+            return self.stage.at[block_at(s, core), self.lanes[0]:self.lanes[0] + self.width]
+
+        def first(self):
+            @pl.loop(0, F * H)
+            def _(s):
+                at = block_at(s, 1 - k.core)
+                x = self.xt[at]
+                for a, n in chunks(self.width, 256):
+                    lane = self.lanes[0] + a
+                    self.stage[at, lane:lane + n] = dot(x, self.y[:, a:a + n]).astype(BF)
+
+            self.twins = [
+                k.send(self.piece(s, 1 - k.core), self.twin.at[s], k.sib) for s in range(F * H)
+            ]
+
+        def second(self, sem):
+            for copy in self.twins:
+                copy.wait_recv()
+
+            @pl.loop(0, F * H)
+            def _(s):
+                at = block_at(s, k.core)
+                x = self.xt[at]
+                for a, n in chunks(self.width, 256):
+                    lane = self.lanes[0] + a
+                    total = dot(x, self.y[:, a:a + n]) + self.twin[s, :, a:a + n].astype(F32)
+                    self.stage[at, lane:lane + n] = total.astype(BF)
+
+            self.far = [
+                k.send(self.piece(s, k.core), self.out.at[s], k.chip(s // H, s % H))
+                for s in range(1, F * H)
+            ]
+            self.own = pltpu.make_async_copy(self.piece(0, k.core), self.out.at[0], sem)
+            self.own.start()
+
+        def done(self):
+            for copy in self.far:
+                copy.wait_recv()
+            self.own.wait()
+
+    @pl.loop(0, D // 256)
+    def _(n):
+        at = pl.ds(pl.multiple_of(n * 256, 256), 256)
+        part = dot(inner[...], down_v[at], 1, 1)
+        part_f[:, at] = part
+        part2_b[:, at] = part.astype(BF)
+
+    own_two = part_f[at_t]
+    down = Grad(xt_a, inner, FB, down_v, (0,), twin_down, sum_down)
+    gate_g = Grad(xt_b, g_gate, FB, gate_v, (0,), twin_gate, sum_gate)
+    up_g = Grad(xt_b, g_up, FB, up_v, (0,), twin_up, sum_up)
+    down.first()
+    gate_g.first()
+    down.second(local.at[4])
+    up_g.first()
+    gate_g.second(local.at[5])
+    up_g.second(local.at[6])
+
+    def gain_row(which):
+        return jnp.concatenate(
+            [gains_ref[b][:, which * R:(which + 1) * R] for b in range(FC_)], axis=1
+        )
+
+    def norm_back(grad, vectors, gain):
+        inv = lax.rsqrt(jnp.mean(vectors * vectors, axis=-1, keepdims=True) + EPS)
+        unit = vectors * inv
+        weighted = grad * gain
+        g_gain = jnp.sum(grad * unit, axis=0, keepdims=True)
+        return inv * (weighted - unit * jnp.mean(weighted * unit, axis=-1, keepdims=True)), g_gain
+
+    total = own_gn2
+    for i in range(1, T):
+        gn2_copies[i - 1].wait_recv()
+        total = total + slots[i - 1].astype(F32)
+    d_mid, gain_two = norm_back(total, mid_ref[...], gain_row(1))
+    g_mid = gall_ref[at_t].astype(F32) + d_mid
+    hid_ref[...] = g_mid
+    gm[at_t] = g_mid.astype(BF)
+    gm_copies = z_gather(gm)
+
+    seg_span = segc_ref[...]
+    row_at = k.c * span + lax.broadcasted_iota(jnp.int32, (span, length), 0)
+    column = lax.broadcasted_iota(jnp.int32, (span, length), 1)
+    keep = (seg_span == seg_ref[...]) & (column <= row_at) & (
+        (pad_ref[...] == 1) | (column == row_at)
     )
-    return (grad_vectors, grad_gain)
+    bias[...] = jnp.where(keep, 0.0, NEG)
+    turn_over(n1_ref, xt_b)
+    loads[3].wait()
+    for copy in gm_copies:
+        copy.wait_recv()
+    two_copies = z_scatter(part2_b, slots2)
+    turn_over(gm, xt_a)
+    gm_rows = gm[...]
+    for n in range(nh // 2):
+        at = QKV + n * 2 * hd
+        pair = dot(gm_rows, w_v[:, at:at + 2 * hd]).astype(BF)
+        g_attn[2 * n] = pair[:, :hd]
+        g_attn[2 * n + 1] = pair[:, hd:]
+    attn = jnp.concatenate([attn_ref[n] for n in range(nh)], axis=1)
+    inner[:, :QW] = attn
+    out_g = Grad(xt_a, inner, QW, w_v, (QKV,), twin_out, sum_out)
+    out_g.first()
+
+    g_kv[...] = jnp.zeros_like(g_kv)
+
+    @pl.loop(0, nh)
+    def _(n):
+        scores = dot(q_ref[n], kv_ref[:, :hd], 1, 1) * scale + bias[...]
+        p = jnp.exp(scores - lse_ref[n])
+        dp = dot(g_attn[n], kv_ref[:, hd:], 1, 1)
+        delta = jnp.sum(p * dp, axis=-1, keepdims=True)
+        ds = (p * (dp - delta)).astype(BF)
+        g_q[n] = dot(ds, kv_ref[:, :hd]) * scale
+        g_key = dot(ds, q_ref[n], 0, 0) * scale
+        g_value = dot(p.astype(BF), g_attn[n], 0, 0)
+        g_kv[...] += jnp.concatenate([g_key, g_value], axis=1)
+
+    g_kvb[...] = g_kv[...].astype(BF)
+    kv_copies = []
+    for i in range(1, C):
+        dest = (k.c + i) % C
+        piece = g_kvb.at[pl.ds(pl.multiple_of(dest * span, span), span)]
+        kv_copies.append(k.send(piece, kv_slots.at[i - 1], k.cpeer(i)))
+    out_g.second(local.at[7])
+    cos, sin = cos_ref[...], sin_ref[...]
+    lane = lax.broadcasted_iota(jnp.int32, (span, 2 * hd), 1)
+    low = (lane % hd) < (hd // 2)
+
+    def turn_back(x):
+        swapped = jnp.where(low, pltpu.roll(x, 2 * hd - hd // 2, 1), pltpu.roll(x, hd // 2, 1))
+        return x * cos - swapped * sin
+
+    for n in range(nh // 2):
+        pair = jnp.concatenate([g_q[2 * n], g_q[2 * n + 1]], axis=1)
+        g_qkv[:, n * 2 * hd:(n + 1) * 2 * hd] = turn_back(pair).astype(BF)
+    own_kv = g_kv[pl.ds(pl.multiple_of(k.c * span, span), span)]
+    for i in range(1, C):
+        kv_copies[i - 1].wait_recv()
+        own_kv = own_kv + kv_slots[i - 1].astype(F32)
+    g_qkv[:, QW:] = jnp.where(lane < hd, turn_back(own_kv), own_kv).astype(BF)
+    k.finish(gn2_copies)
+
+    @pl.loop(0, D // 256)
+    def _(n):
+        at = pl.ds(pl.multiple_of(n * 256, 256), 256)
+        part = dot(g_qkv[...], w_v[at, :QKV], 1, 1)
+        part_f[:, at] = part
+        part_b[:, at] = part.astype(BF)
+
+    n1_copies = z_scatter(part_b, slots3)
+    qkv_g = Grad(xt_b, g_qkv, QKV, w_v, (0,), twin_qkv, sum_qkv)
+    qkv_g.first()
+    total = mid_ref[...] + own_two
+    for i in range(1, T):
+        two_copies[i - 1].wait_recv()
+        total = total + slots2[i - 1].astype(F32)
+    out_ref[...] = (keep_ref[...] * total).astype(BF)
+    qkv_g.second(local.at[8])
+    total = part_f[at_t]
+    for i in range(1, T):
+        n1_copies[i - 1].wait_recv()
+        total = total + slots3[i - 1].astype(F32)
+    d_hid, gain_one = norm_back(total, hidden_ref[...].astype(F32), gain_row(0))
+    hid_ref[...] = hid_ref[...] + d_hid
+
+    for b in range(FC_):
+        gz[b] = jnp.concatenate(
+            [gain_one[:, b * R:(b + 1) * R], gain_two[:, b * R:(b + 1) * R]], axis=1
+        )
+    z_copies = [k.send(gz, gz_slots.at[i - 1], k.zpeer(i)) for i in range(1, T)]
+    both = gz[...]
+    for i in range(1, T):
+        z_copies[i - 1].wait_recv()
+        both = both + gz_slots[i - 1]
+    gx[...] = both
+    x_copies = []
+    for n, (df, dc) in enumerate((df, dc) for df in range(F) for dc in range(C) if df or dc):
+        f, c = (k.f + df) % F, (k.c + dc) % C
+        x_copies.append(k.send(gx.at[f * C + c], gx_slots.at[n], (f, c, k.t)))
+    both = gx[k.f * C + k.c]
+    for n, copy in enumerate(x_copies):
+        copy.wait_recv()
+        both = both + gx_slots[n]
+    gg_ref[...] = both
+    for grad in (down, gate_g, up_g, out_g, qkv_g):
+        grad.done()
+    k.finish()
+
+
+def backward(sizes, hd, vm_args, hbm_args):
+    F, C, T = sizes
+    H = C // 2
+    hidden, q, n2, kv, gate = vm_args[0], vm_args[8], vm_args[13], vm_args[9], hbm_args[1]
+    rows, D = hidden.shape
+    FB = gate.shape[1]
+    nh, span, _ = q.shape
+    length = kv.shape[0]
+    QW, QKV = nh * hd, nh * hd + 2 * hd
+    R = D // (F * C)
+    FH = F * H
+    vm = pl.BlockSpec(memory_space=pltpu.VMEM)
+    hbm = pl.BlockSpec(memory_space=pl.ANY)
+    n_sems = 5 * (T - 1) + 5 * (2 * FH - 1) + C - 1 + F * C - 1
+    S = jax.ShapeDtypeStruct
+    V = pltpu.VMEM
+    return pl.pallas_call(
+        functools.partial(backward_kernel, sizes, hd),
+        out_shape=(
+            S((rows, D), BF), S((rows, D), F32), S((1, 2 * R), F32),
+            S((FH, R, FB), BF), S((FH, R, FB), BF), S((FH, R, FB), BF),
+            S((FH, R, QW), BF), S((FH, R, QKV), BF),
+        ),
+        in_specs=[vm] * 16 + [hbm] * 4,
+        out_specs=[vm] * 3 + [hbm] * 5,
+        scratch_shapes=[
+            V((D, QW + QKV), BF), V((D, FB), BF), V((D, FB), BF), V((D, FB), BF),
+            V((D, span), BF), V((D, span), BF),
+            V((span, FB), BF), V((span, FB), BF), V((span, FB), BF), V((span, D), BF),
+            V((span, length), F32), V((span, D), F32), V((span, D), BF), V((span, D), BF),
+            V((T - 1, rows, D), BF), V((T - 1, rows, D), BF), V((T - 1, rows, D), BF),
+            V((FH, R, FB), BF), V((FH, R, FB), BF), V((FH, R, FB), BF),
+            V((FH, R, QW), BF), V((FH, R, QKV), BF),
+            V((nh, span, hd), BF), V((nh, span, hd), F32), V((span, QKV), BF),
+            V((length, 2 * hd), F32), V((length, 2 * hd), BF), V((C - 1, span, 2 * hd), BF),
+            V((F * C, 1, 2 * R), F32), V((T - 1, F * C, 1, 2 * R), F32),
+            V((F * C, 1, 2 * R), F32), V((F * C - 1, 1, 2 * R), F32),
+            pltpu.SemaphoreType.DMA((n_sems,)), pltpu.SemaphoreType.DMA((n_sems,)),
+            pltpu.SemaphoreType.DMA((9,)),
+        ],
+        compiler_params=pltpu.CompilerParams(
+            collective_id=1, has_side_effects=True, vmem_limit_bytes=60 * 2**20
+        ),
+        name="backward",
+    )(*vm_args, *hbm_args)
 
 
 def body(hidden_in, segment_ids, pad_mask, attn_gain, w_query, w_key, w_value, w_out,
@@ -353,9 +649,7 @@
     length = segment_ids.shape[1]
     span = length // C
     hd = w_key.shape[1]
-    QW = w_query.shape[1]
-    R = w_query.shape[0]
-    nh = QW // hd
+    R, QW = w_query.shape
     start = c * span
     seg_span = lax.dynamic_slice_in_dim(segment_ids[0], start, span, 0)[:, None]
     row_at = start + jnp.arange(span, dtype=jnp.int32)
@@ -367,75 +661,27 @@
     angles = (row_at - first).astype(F32)[:, None] * frequency
     cos, sin = jnp.cos(angles), jnp.sin(angles) * sign
     keep = lax.dynamic_slice_in_dim(pad_mask[0], start + t * rows, rows, 0).astype(F32)[:, None]
-    g_out = cotangent.astype(F32) * keep
+    g_out = (cotangent.astype(F32) * keep).astype(BF)
     gains = jnp.concatenate([attn_gain, mlp_gain])[None]
     (n1, q, kv, attn, lse, middle, n2, g_all, w, gain_all, gate_all, up_all, down_all) = forward(
         sizes, hd, hidden_in, segment_ids, seg_span, pad_mask, cos, sin, gains,
-        w_query, w_key, w_value, w_out, w_down, g_out.astype(BF), w_gate, w_up,
+        w_query, w_key, w_value, w_out, w_down, g_out, w_gate, w_up,
     )
-    gain_one = gain_all[:, 0, :R].reshape(1, D)
-    gain_two = gain_all[:, 0, R:].reshape(1, D)
-    hidden = hidden_in.astype(F32)
-    scale_one = lax.rsqrt(jnp.mean(hidden * hidden, axis=-1, keepdims=True) + EPS)
-    scale_two = lax.rsqrt(jnp.mean(middle * middle, axis=-1, keepdims=True) + EPS)
-    gate = dot(n2, gate_all)
-    up = dot(n2, up_all)
-    sig = jax.nn.sigmoid(gate)
-    inner = (gate * sig * up).astype(BF)
-    block_out = (keep * (middle + rows_sum(dot(inner, down_all, 1, 1)))).astype(BF)
-    grad_down = dot(g_all, inner, 0, 0)
-    g_inner = dot(g_all, down_all)
-    g_gate = (g_inner * up * sig * (1.0 + gate * (1.0 - sig))).astype(BF)
-    g_up = (g_inner * gate * sig).astype(BF)
-    g_n2 = rows_sum(dot(g_gate, gate_all, 1, 1) + dot(g_up, up_all, 1, 1))
-    grad_gate = dot(n2, g_gate, 0, 0)
-    grad_up = dot(n2, g_up, 0, 0)
-    d_mid, grad_gain_two = norm_back(g_n2, middle, scale_two, gain_two)
-    g_mid = g_out + d_mid
-    gm_all = rows_gather(g_mid.astype(BF))
-    attn = jnp.swapaxes(attn, 0, 1).reshape(span, QW)
-    grad_out = dot(gm_all, attn, 0, 0)
-    out_t = w[:, QW + 2 * hd:]
-    g_attn = dot(gm_all, out_t).astype(BF).reshape(span, nh, hd)
-    seg, pad = segment_ids[0], pad_mask[0]
-    columns = jnp.arange(length, dtype=jnp.int32)
-    allowed = (
-        (seg_span == seg[None, :])
-        & (columns[None, :] <= row_at[:, None])
-        & ((pad[None, :] == 1) | (columns[None, :] == row_at[:, None]))
+    block_out, grad_hidden, gg, s_down, s_gate, s_up, s_out, s_qkv = backward(
+        sizes, hd,
+        (hidden_in, segment_ids, seg_span, pad_mask, cos, sin, keep, n1, q, kv, attn, lse, middle,
+         n2, g_all, gain_all),
+        (w, gate_all, up_all, down_all),
     )
-    key, value = kv[:, :hd], kv[:, hd:]
-    scale = hd ** (-0.5)
-    scores = jnp.einsum("hqd,td->hqt", q, key, preferred_element_type=F32) * scale
-    probs = jnp.exp(jnp.where(allowed[None], scores, NEG) - lse)
-    dp = jnp.einsum("qhd,td->hqt", g_attn, value, preferred_element_type=F32)
-    delta = jnp.sum(probs * dp, axis=-1, keepdims=True)
-    ds = (probs * (dp - delta)).astype(BF)
-    g_q = jnp.einsum("hqt,td->qhd", ds, key, preferred_element_type=F32) * scale
-    g_k = jnp.einsum("hqt,hqd->td", ds, q, preferred_element_type=F32) * scale
-    g_v = jnp.einsum("hqt,qhd->td", probs.astype(BF), g_attn, preferred_element_type=F32)
-    g_kv = lax.psum_scatter(
-        jnp.concatenate([g_k, g_v], axis=1), "context", scatter_dimension=0, tiled=True
-    )
-    sin = sin * sign
-    g_q = rotate_back(g_q, cos, sin, hd).astype(BF).reshape(span, -1)
-    g_k = rotate_back(g_kv[:, None, :hd], cos, sin, hd).astype(BF)[:, 0]
-    g_qkv = jnp.concatenate([g_q, g_k, g_kv[:, hd:].astype(BF)], axis=1)
-    g_n1 = rows_sum(dot(g_qkv, w[:, :QW + 2 * hd], 1, 1))
-    grad_qkv = dot(n1, g_qkv, 0, 0)
-    d_hid, grad_gain_one = norm_back(g_n1, hidden, scale_one, gain_one)
-    grads = jnp.stack([grad_gain_one, grad_gain_two])
-    grad_down = scatter_g(grad_down)
-    grad_gate = scatter_g(grad_gate)
-    grad_up = scatter_g(grad_up)
-    grad_out = scatter_g(grad_out)
-    grad_qkv = scatter_g(grad_qkv)
-    grads = lax.psum(grads, "tensor")
-    grads = lax.psum_scatter(grads, FC, scatter_dimension=1, tiled=True)
+
+    def total(parts):
+        return jnp.sum(parts.astype(F32), axis=0)
+
+    grad_qkv = total(s_qkv)
     return (
-        block_out[None], (g_mid + d_hid)[None], grads[0], grad_qkv[:, :QW],
-        grad_qkv[:, QW:QW + hd], grad_qkv[:, QW + hd:], grad_out.T, grads[1],
-        grad_gate, grad_up, grad_down.T,
+        block_out[None], grad_hidden[None], gg[0, :R], grad_qkv[:, :QW],
+        grad_qkv[:, QW:QW + hd], grad_qkv[:, QW + hd:], total(s_out).T, gg[0, R:],
+        total(s_gate), total(s_up), total(s_down).T,
     )
 
 

time: 634 us -> 303 us (0.48)
  waiting for transfers between devices: 383 us -> 0 us
  Pallas kernels: 109 us -> 274 us
  matrix products: 68.4 us -> 0 us
  between operations: 14.5 us -> 0.73 us
  blocking collectives: 11.7 us -> 0 us
  other arithmetic: 23.6 us -> 12.4 us
  local copies, waits for them, and re-layouts: 22.4 us -> 15 us
    reduce_scatter x9 -> x0, waiting for transfers between devices: 326 us -> none  [the longest x5 236 us: scatter_g(): lax.psum_scatter(g.astype(BF), FC, scatter_dimension=0, tiled=True)]
    pallas_call x0 -> x1, Pallas kernels: none -> 166 us  [backward(): pl.pallas_call(functools.partial(backward_kernel, sizes, hd), out_shape=(...]
    dot_general x18 -> x0, matrix products: 68.4 us -> none  [the longest x13 46.8 us: dot(): lax.dot_general(a, b, (((ca,), (cb,)), ((), ())), preferred_element_type=...]
    unnamed x12 -> x0, waiting for transfers between devices: 36.7 us -> none
    all_gather x1 -> x0, waiting for transfers between devices: 20 us -> none  [rows_gather(): return lax.all_gather(x, 'tensor', axis=0, tiled=True)]
    psum x1 -> x0, blocking collectives: 11.7 us -> none  [body(): grads = lax.psum(grads, 'tensor')]
    convert_element_type x5 -> x1, other arithmetic: 10.5 us -> 1.76 us  [body(): g_out = (cotangent.astype(F32) * keep).astype(BF)]
  transfers between devices with their start and end apart: 11 -> 0, of which waited for: 11 -> 0; matrix products, arithmetic and copies ran while one was open for 8% -> 0% of each run, Pallas kernels for 0% -> 0%
where the time goes in v3:
time: 303 us
  Pallas kernels  274 us (90%)
  local copies, waits for them, and re-layouts  15 us (5%)
  other arithmetic  12.4 us (4%)
    pallas_call x1, Pallas kernels, backward(): pl.pallas_call(functools.partial(backward_kernel, sizes, hd), out_shape=(...  166 us
    pallas_call x1, Pallas kernels, forward(): pl.pallas_call(functools.partial(forward_kernel, sizes, hd), out_shape=(S...  109 us
    unnamed x18, local copies, waits for them, and re-layouts  9.29 us
    reduce_sum x5, other arithmetic, total(): return jnp.sum(parts.astype(F32), axis=0)  7 us

profile of v3, /device:TPU:0, one launch (start us, length us, event | category | flops | bytes accessed | tf_op | source)
XLA Modules:
  0.0 302.5 jit_solution(6167177707560894404)
XLA Ops:
  0.6 0.7 convert_bitcast_fusion
  1.4 0.7 pad_maximum_fusion
  2.1 0.6 broadcast_in_dim.27.gain_ref
  2.6 0.7 fusion.9
  3.3 0.7 constant_dynamic-slice_fusion.1
  4.0 0.9 convert_reduce_fusion.5
  5.0 0.7 copy.47.keep_ref
  5.7 1.5 copy.44.wk_ref
  7.2 1.5 copy.45.wv_ref
  8.7 0.8 copy.46.segc_ref
  9.5 1.2 fusion.1
  10.7 1.8 fusion.gout_ref
  12.5 108.8 %forward.1 = (bf16[256,2048]{1,0:T(8,128)(2,1)}, bf16[8,256,64]{2,1,0:T(8,128)(2,1)}, bf16[1024,128]{1,0:T(8,128)(2,1)}, bf16[8,256,64]{2,1,0:T(8,128)(2,1)}, f3...) custom-call(bf16[64,2048]{1,0:T(8,128)(2,1)} %bitcast.20, ...), custom_call_target="tpu_custom_call" | custom-call | tf_op jit(solution)/shard_map/forward/pallas_call | solution.py:295
  121.3 165.6 %backward.1 = (bf16[64,2048]{1,0:T(8,128)(2,1)}, f32[64,2048]{1,0:T(8,128)}, f32[1,512]{1,0:T(1,128)}, bf16[4,256,1408]{2,1,0:T(8,128)(2,1)}, bf16[4,256,1408]{2...) custom-call(bf16[64,2048]{1,0:T(8,128)(2,1)} %bitcast.21, ...), custom_call_target="tpu_custom_call" | custom-call | tf_op jit(solution)/shard_map/backward/pallas_call | solution.py:611
  286.9 0.0 copy-start.2
  286.9 1.3 fusion.8
  288.2 1.4 convert_reduce_fusion.4
  289.7 1.0 copy.50
  290.7 0.0 copy-done.2
  290.7 0.2 convert_reduce_fusion.3
  290.8 0.1 fusion.7
  290.9 0.0 copy-start.1
  290.9 0.9 slice.20
  291.8 0.7 copy.49
  292.5 0.7 copy.48
  293.2 3.5 %convert_reduce_fusion.2 = f32[256,1408]{1,0:T(8,128)} fusion(bf16[4,256,1408]{2,1,0:T(8,128)(2,1)} %get-tuple-element.50), kind=kLoop, calls=%fused_computation.2 | loop fusion | flops 2523136 | bytes 4325376 | tf_op jit(solution)/shard_map/reduce_sum | solution.py:678
  296.7 0.0 copy-done.1
  296.7 0.0 copy-start
  296.7 1.5 convert_reduce_fusion.1
  298.2 0.8 copy-done
  299.0 0.0 copy-start.4
  299.0 0.0 copy-start.3
  299.0 0.4 convert_reduce_fusion
  299.5 1.5 copy.51
  301.0 0.0 copy-done.4
  301.0 0.7 copy.54
  301.7 0.0 copy-done.3
  301.7 0.8 copy.55
  (2 shorter events, 0.0 us)
Async XLA Ops:
  286.9 3.8 %copy-start.2 = (bf16[4,256,640]{2,1,0:T(8,128)(2,1)S(1)}, bf16[4,256,640]{2,1,0:T(8,128)(2,1)}, u32[]{:S(2)}) copy-start(bf16[4,256,640]{2,1,0:T(8,128)(2,1)} %get-tuple-element.48) | copy-start | bytes 3932164
  290.9 5.8 %copy-start.1 = (bf16[4,256,1408]{2,1,0:T(8,128)(2,1)S(1)}, bf16[4,256,1408]{2,1,0:T(8,128)(2,1)}, u32[]{:S(2)}) copy-start(bf16[4,256,1408]{2,1,0:T(8,128)(2,1)} %get-tuple-element.51) | copy-start | bytes 8650756
  296.7 2.3 copy-start
  299.0 2.0 copy-start.4
  299.0 2.7 copy-start.3

commit v4 on v2

v4 whole, which is shorter than its diff:
```python
import functools
import math

import jax
import jax.numpy as jnp
from jax import lax
from jax.experimental import pallas as pl
from jax.experimental.pallas import tpu as pltpu
from jax.sharding import PartitionSpec as P

EPS = 1e-05
NEG = -1e30
BF = jnp.bfloat16
F32 = jnp.float32
MESH = pl.DeviceIdType.MESH
FC = ("fsdp", "context")


def dot(a, b, ca=1, cb=0):
    return lax.dot_general(a, b, (((ca,), (cb,)), ((), ())), preferred_element_type=F32)


def chunks(total, step):
    return [(at, min(step, total - at)) for at in range(0, total, step)]


def ds(start, size):
    return pl.ds(pl.multiple_of(start, size), size)


class Links:
    def __init__(self, sizes, send_sems, recv_sems):
        self.F, self.C, self.T = sizes
        self.f = lax.axis_index("fsdp")
        self.c = lax.axis_index("context")
        self.t = lax.axis_index("tensor")
        self.h = self.c // 2
        self.core = self.c % 2
        self.H = self.C // 2
        self.send_sems, self.recv_sems = send_sems, recv_sems
        self.used = 0
        self.open = []
        self.sib = (self.f, self.h * 2 + 1 - self.core, self.t)

    def chip(self, df, dh):
        return ((self.f + df) % self.F, ((self.h + dh) % self.H) * 2 + self.core, self.t)

    def block(self, df, dh, core):
        return ((self.f + df) % self.F) * self.C + ((self.h + dh) % self.H) * 2 + core

    def zpeer(self, i):
        return (self.f, self.c, (self.t + i) % self.T)

    def cpeer(self, i):
        return (self.f, (self.c + i) % self.C, self.t)

    def new(self, src, dst, dev, recv=None):
        n = self.used
        self.used += 1
        copy = pltpu.make_async_remote_copy(
            src_ref=src, dst_ref=dst, send_sem=self.send_sems.at[n],
            recv_sem=self.recv_sems.at[n if recv is None else recv],
            device_id=dev, device_id_type=MESH,
        )
        return copy, n

    def start(self, copy, cond=None):
        if cond is None:
            copy.start()
        else:
            pl.when(cond)(copy.start)
        self.open.append((copy, cond))

    def send(self, src, dst, dev):
        copy, _ = self.new(src, dst, dev)
        self.start(copy)
        return copy

    def plane_peers(self):
        return [
            ((self.f + df) % self.F, (self.c + dc) % self.C, self.t)
            for df in range(self.F) for dc in range(self.C) if df or dc
        ]

    def peers(self):
        return self.plane_peers() + [self.zpeer(i) for i in range(1, self.T)]

    def greet(self):
        self.bar = pltpu.get_barrier_semaphore()
        for dev in self.peers():
            pl.semaphore_signal(self.bar, inc=1, device_id=dev, device_id_type=MESH)

    def meet(self):
        pl.semaphore_wait(self.bar, len(self.peers()))

    def finish(self, copies=None):
        wanted = None if copies is None else [id(c) for c in copies]
        left = []
        for copy, cond in self.open:
            if wanted is not None and id(copy) not in wanted:
                left.append((copy, cond))
            elif cond is None:
                copy.wait_send()
            else:
                pl.when(cond)(copy.wait_send)
        self.open = left


class Gather:
    def __init__(self, links, full, rows):
        self.k, self.full, self.rows = links, full, rows

    def part(self, df=0, dh=0, half=None):
        block = self.k.block(-df, -dh, self.k.core)
        if half is None:
            return self.full.at[ds(block * self.rows, self.rows)]
        n = self.rows // 2
        return self.full.at[ds(block * self.rows + half * n, n)]

    def first(self, own):
        k = self.k
        mine = self.part()
        self.line = {}
        for df in range(1, k.F):
            self.line[df, 0] = k.send(own, mine, k.chip(df, 0))
        for dh in range(1, k.H):
            self.line[0, dh] = k.send(own, mine, k.chip(0, dh))
        self.twin = [k.send(own, mine, k.sib)]

    def second(self):
        k = self.k
        self.diag = {}
        for (df, dh), copy in self.line.items():
            copy.wait_recv()
            half = 0 if df else 1
            piece = self.part(df, dh, half)
            if df:
                for eh in range(1, k.H):
                    self.diag[df, eh, half] = k.send(piece, piece, k.chip(0, eh))
            else:
                for ef in range(1, k.F):
                    self.diag[ef, dh, half] = k.send(piece, piece, k.chip(ef, 0))
            whole = self.part(df, dh)
            self.twin.append(k.send(whole, whole, k.sib))

    def third(self):
        k = self.k
        for copy in self.diag.values():
            copy.wait_recv()
        for df in range(1, k.F):
            for dh in range(1, k.H):
                whole = self.part(df, dh)
                self.twin.append(k.send(whole, whole, k.sib))

    def done(self):
        for copy in self.twin:
            copy.wait_recv()

    def sent(self):
        self.k.finish(list(self.line.values()) + list(self.diag.values()) + self.twin)


class ZGather:
    def __init__(self, k, full, rows):
        self.k, self.full, self.rows = k, full, rows
        T = k.T
        piece = full.at[ds(k.t * rows, rows)]
        self.copies = {i: k.new(piece, piece, k.zpeer(i)) for i in range(1, T)}
        for i in [2, 1, 3] if T == 4 else range(1, T):
            cond = None
            if T == 4 and i != 2:
                cond = (k.t < 3) if i == 1 else (k.t > 0)
            k.start(self.copies[i][0], cond)
        self.left = list(range(1, T))

    def relay(self):
        k = self.k
        if k.T != 4:
            return
        self.copies[2][0].wait_recv()
        self.left = [1, 3]
        for at, origin, i in ((2, 0, 3), (1, 3, 1)):
            piece = self.full.at[ds(origin * self.rows, self.rows)]
            copy, _ = k.new(piece, piece, (k.f, k.c, 3 - origin), recv=self.copies[i][1])
            k.start(copy, k.t == at)

    def wait(self):
        for i in self.left:
            self.copies[i][0].wait_recv()


class ZScatter:
    def __init__(self, k, part, slots, middle, rows):
        self.k, self.part, self.slots, self.middle, self.rows = k, part, slots, middle, rows
        T = k.T
        self.line = T == 4
        self.end = (k.t == 0) | (k.t == T - 1)
        if self.line:
            src = part.at[ds((3 - k.t) * rows, rows)]
            self.far, _ = k.new(src, middle, (k.f, k.c, 1 + k.t // 3))
            k.start(self.far, self.end)
        self.copies = {}
        for i in range(1, T):
            src = part.at[ds(((k.t + i) % T) * rows, rows)]
            self.copies[i], _ = k.new(src, slots.at[i - 1], k.zpeer(i))
        if self.line:
            k.start(self.copies[2], self.end)
            k.start(self.copies[1], k.t < 3)
            k.start(self.copies[3], k.t > 0)
        else:
            for i in range(1, T):
                k.start(self.copies[i])

    def relay(self):
        k = self.k
        if not self.line:
            return
        inner = (k.t > 0) & (k.t < 3)

        @pl.when(inner)
        def _():
            self.far.wait_recv()
            at = ds(((k.t + 2) % 4) * self.rows, self.rows)
            both = self.part[at].astype(F32) + self.middle[...].astype(F32)
            self.part[at] = both.astype(BF)
            self.copies[2].start()

        k.open.append((self.copies[2], inner))

    def total(self):
        k = self.k
        for i in range(1, k.T):
            if not self.line or i == 2:
                self.copies[i].wait_recv()
                continue
            there = (k.t > 0) if i == 1 else (k.t < 3)
            pl.when(there)(self.copies[i].wait_recv)

            @pl.when(jnp.logical_not(there))
            def _():
                self.slots[i - 1] = jnp.zeros(self.slots.shape[1:], BF)

        total = self.part[ds(k.t * self.rows, self.rows)].astype(F32)
        for i in range(1, k.T):
            total = total + self.slots[i - 1].astype(F32)
        return total


class Grad:
    def __init__(self, k, xt, y, width, stage, lane, twin, relay, out):
        self.k, self.xt, self.y, self.width, self.stage = k, xt, y, width, stage
        self.lane, self.twin, self.relay, self.out = lane, twin, relay, out
        self.R = xt.shape[0] // (k.F * k.C)

    def rows_of(self, s, core):
        return ds(self.k.block(s // self.k.H, s % self.k.H, core) * self.R, self.R)

    def piece(self, df, dh, core, half=None):
        block = self.k.block(df, dh, core)
        at = ds(block * self.R, self.R)
        if half is not None:
            n = self.R // 2
            at = ds(block * self.R + half * n, n)
        return self.stage.at[at, self.lane:self.lane + self.width]

    def first(self):
        k = self.k

        @pl.loop(0, k.F * k.H)
        def _(s):
            at = self.rows_of(s, 1 - k.core)
            x = self.xt[at]
            for a, n in chunks(self.width, 256):
                self.stage[at, self.lane + a:self.lane + a + n] = dot(x, self.y[:, a:a + n]).astype(BF)

        self.twins = [
            k.send(self.piece(s // k.H, s % k.H, 1 - k.core), self.twin.at[s], k.sib)
            for s in range(k.F * k.H)
        ]

    def second(self, sem):
        k = self.k
        for copy in self.twins:
            copy.wait_recv()

        @pl.loop(0, k.F * k.H)
        def _(s):
            at = self.rows_of(s, k.core)
            x = self.xt[at]
            for a, n in chunks(self.width, 256):
                total = dot(x, self.y[:, a:a + n]) + self.twin[s, :, a:a + n].astype(F32)
                self.stage[at, self.lane + a:self.lane + a + n] = total.astype(BF)

        self.diag = {}
        n = 0
        for df in range(1, k.F):
            for dh in range(1, k.H):
                for half, dev in ((0, k.chip(df, 0)), (1, k.chip(0, dh))):
                    self.diag[df, dh, half] = n, half, k.send(
                        self.piece(df, dh, k.core, half), self.relay.at[n, half], dev
                    )
                n += 1
        self.own = pltpu.make_async_copy(self.piece(0, 0, k.core), self.out.at[0], sem)
        self.own.start()

    def add(self, df, dh, half):
        piece = self.piece(df, dh, self.k.core, half)
        total = piece[...].astype(F32)
        for (ef, eh, other), (n, _, copy) in self.diag.items():
            if other == half and (ef == df or df == 0) and (eh == dh or dh == 0):
                copy.wait_recv()
                total = total + self.relay[n, half].astype(F32)
        piece[...] = total.astype(BF)

    def third(self):
        k = self.k
        self.far = []
        for dh in range(1, k.H):
            if k.F > 1:
                self.add(0, dh, 0)
            self.far.append(k.send(self.piece(0, dh, k.core), self.out.at[k.F - 1 + dh], k.chip(0, dh)))
        for df in range(1, k.F):
            if k.H > 1:
                self.add(df, 0, 1)
            self.far.append(k.send(self.piece(df, 0, k.core), self.out.at[df], k.chip(df, 0)))

    def done(self):
        for copy in self.far:
            copy.wait_recv()
        self.own.wait()


def n_semaphores(F, C, T):
    H = C // 2
    a, b, d = F - 1, H - 1, (F - 1) * (H - 1)
    gather = a + b + 1 + 2 * d + a + b + d
    grad = F * H + 2 * d + a + b
    return 4 * gather + 5 * grad + 2 * (F * C - 1) + 2 * (C - 1) + 9 * (T + 1)


def layer_kernel(
    sizes, hd,
    hidden_ref, seg_ref, pad_ref, ga_ref, gm_ref, wq_ref, wk_ref, wv_ref, wo_ref, wd_ref, cot_ref,
    wg_hbm, wu_hbm,
    out_ref, hid_ref, gg_ref, sum_down, sum_gate, sum_up, sum_out, sum_qkv,
    w_v, gate_v, up_v, down_v, n1_s, n2_s, gall, gm, xt_a, xt_b, inner, g_gate, g_up,
    q_s, attn_s, g_attn, g_qkv, lse_s, kv_s, k_s, v_s, g_kv, g_kvb, kv_slots, bias, cos_s, sin_s,
    padc, part_b, part2_b, slots, slots2, middle_a, middle_b, mid_s,
    twin_down, twin_gate, twin_up, twin_out, twin_qkv,
    relay_down, relay_gate, relay_up, relay_out, relay_qkv,
    gains_s, gz, gz_slots, gx, gx_slots, sends, recvs, local,
):
    k = Links(sizes, sends, recvs)
    T, F, C, H = k.T, k.F, k.C, k.H
    rows, D = hidden_ref.shape
    R, QW = wq_ref.shape
    FB = wg_hbm.shape[1]
    span, length = bias.shape
    nh = QW // hd
    QKV = QW + 2 * hd
    pair = 2 * hd
    scale = hd ** (-0.5)
    at_t = ds(k.t * rows, rows)
    at_c = ds(k.c * span, span)
    k.greet()

    aw, gw, uw, dw = (Gather(k, full, R) for full in (w_v, gate_v, up_v, down_v))
    mine = k.block(0, 0, k.core)
    own_w = aw.part()
    own_w[:, :QW] = wq_ref[...]
    kv_w = jnp.concatenate([wk_ref[...], wv_ref[...]], axis=0)
    own_w[:, QW:QKV] = kv_w.astype(F32).T.astype(BF)
    own_w[:, QKV:] = wo_ref[...].astype(F32).T.astype(BF)
    gains_s[mine] = jnp.concatenate([ga_ref[...], gm_ref[...]], axis=1).astype(F32)
    loads = [
        pltpu.make_async_copy(wg_hbm, gw.part(), local.at[0]),
        pltpu.make_async_copy(wu_hbm, uw.part(), local.at[1]),
    ]
    for copy in loads:
        copy.start()
    k.meet()
    own_gain = gains_s.at[mine]
    gain_copies = [k.send(own_gain, own_gain, dev) for dev in k.plane_peers()]
    aw.first(own_w)

    hidden = hidden_ref[...].astype(F32)
    scale_one = lax.rsqrt(jnp.mean(hidden * hidden, axis=-1, keepdims=True) + EPS)
    hidden = hidden * scale_one
    for copy in gain_copies:
        copy.wait_recv()

    def gain_row(which):
        return jnp.concatenate(
            [gains_s[b][:, which * R:(which + 1) * R] for b in range(F * C)], axis=1
        )

    n1_s[at_t] = (hidden * gain_row(0)).astype(BF)
    n1_gather = ZGather(k, n1_s, rows)
    down_v[ds(mine * R, R)] = wd_ref[...].astype(F32).T.astype(BF)

    def column_of(row):
        return jnp.broadcast_to(row.astype(F32), (8, span)).T[:, :1]

    seg = seg_ref[...].astype(F32)
    seg_col = column_of(seg_ref[:, at_c])
    padc[...] = column_of(pad_ref[:, at_c])
    row_at = k.c * span + lax.broadcasted_iota(jnp.int32, (span, 1), 0)
    column = lax.broadcasted_iota(jnp.int32, (span, length), 1)
    first = jnp.sum(jnp.where(seg < seg_col, 1.0, 0.0), axis=1, keepdims=True)
    lane = lax.broadcasted_iota(jnp.int32, (1, pair), 1)
    frequency = jnp.exp(-((lane % (hd // 2)).astype(F32) * (2.0 / hd)) * math.log(10000.0))
    low = (lane % hd) < (hd // 2)
    angles = (row_at.astype(F32) - first) * frequency
    cos_s[...] = jnp.cos(angles)
    sin_s[...] = jnp.where(low, -1.0, 1.0) * jnp.sin(angles)
    allowed = (seg == seg_col) & (column <= row_at) & ((pad_ref[...] == 1) | (column == row_at))
    bias[...] = jnp.where(allowed, 0.0, NEG)
    keep = padc[at_t]
    gall[at_t] = (cot_ref[...].astype(F32) * keep).astype(BF)

    def swap_halves(x):
        return jnp.where(low, pltpu.roll(x, pair - hd // 2, 1), pltpu.roll(x, hd // 2, 1))

    def turn(x):
        return x * cos_s[...] + swap_halves(x) * sin_s[...]

    def turn_back(x):
        return x * cos_s[...] - swap_halves(x) * sin_s[...]

    aw.second()
    gw.first(wg_hbm)
    n1_gather.relay()
    aw.third()
    n1_gather.wait()
    g_gather = ZGather(k, gall, rows)
    aw.done()

    pre = dot(n1_s[...], w_v[:, QW:QKV])
    kv_s[at_c] = jnp.where(lane < hd, turn(pre), pre).astype(BF)
    own_kv = kv_s.at[at_c]
    kv_copies = [k.send(own_kv, own_kv, k.cpeer(i)) for i in range(1, C)]
    for at, n in chunks(QW, 256):
        pre = dot(n1_s[...], w_v[:, at:at + n])
        for b in range(0, n, pair):
            q_s[:, at + b:at + b + pair] = turn(pre[:, b:b + pair]).astype(BF)
    for copy in kv_copies:
        copy.wait_recv()
    k_s[...] = kv_s[:, :hd]
    v_s[...] = kv_s[:, hd:]
    gw.second()
    uw.first(wu_hbm)
    lse_s[...] = jnp.zeros_like(lse_s)

    @pl.loop(0, nh // 2)
    def _(n):
        at = ds(n * pair, pair)
        two = q_s[:, at] * BF(scale)
        outs = []
        for e in range(2):
            scores = dot(two[:, e * hd:(e + 1) * hd], k_s[...], 1, 1) + bias[...]
            top = jnp.max(scores, axis=-1, keepdims=True)
            weights = jnp.exp(scores - top)
            total = jnp.sum(weights, axis=-1, keepdims=True)
            outs.append(dot((weights * (1.0 / total)).astype(BF), v_s[...]))
            lse_s[...] = jnp.where(lane == 2 * n + e, top + jnp.log(total), lse_s[...])
        attn_s[:, at] = jnp.concatenate(outs, axis=1).astype(BF)

    g_gather.relay()

    @pl.loop(0, D // 256)
    def _(n):
        at = ds(n * 256, 256)
        part_b[:, at] = dot(attn_s[...], w_v[at, QKV:], 1, 1).astype(BF)

    one = ZScatter(k, part_b, slots, middle_a, rows)
    gw.third()
    one.relay()
    uw.second()
    dw.first(dw.part())

    def turn_over(src, dst):
        @pl.loop(0, D // 256)
        def _(n):
            at = ds(n * 256, 256)
            dst[at] = src[:, at].astype(F32).T.astype(BF)

    g_gather.wait()
    turn_over(gall, xt_a)
    mid = hidden_ref[...].astype(F32) + one.total()
    mid_s[...] = mid
    scale_two = lax.rsqrt(jnp.mean(mid * mid, axis=-1, keepdims=True) + EPS)
    n2_s[at_t] = (mid * scale_two * gain_row(1)).astype(BF)
    n2_gather = ZGather(k, n2_s, rows)
    uw.third()
    n2_gather.relay()
    dw.second()
    n2_gather.wait()
    dw.third()
    for weight in (gw, uw, dw):
        weight.done()
    for copy in loads:
        copy.wait()
    k.finish([one.far] * one.line + list(one.copies.values()))

    for at, n in chunks(FB, 256):
        gate = dot(n2_s[...], gate_v[:, at:at + n])
        up = dot(n2_s[...], up_v[:, at:at + n])
        sig = jax.nn.sigmoid(gate)
        inner[:, at:at + n] = (gate * sig * up).astype(BF)
        g_in = dot(gall[...], down_v[:, at:at + n])
        g_gate[:, at:at + n] = (g_in * up * sig * (1.0 + gate * (1.0 - sig))).astype(BF)
        g_up[:, at:at + n] = (g_in * gate * sig).astype(BF)

    @pl.loop(0, D // 256)
    def _(n):
        at = ds(n * 256, 256)
        part = dot(g_gate[...], gate_v[at], 1, 1) + dot(g_up[...], up_v[at], 1, 1)
        part_b[:, at] = part.astype(BF)

    two = ZScatter(k, part_b, slots, middle_a, rows)
    for weight in (aw, gw, uw, dw):
        weight.sent()
    down_g = Grad(k, xt_a, inner, FB, gate_v, 0, twin_down, relay_down, sum_down)
    gate_g = Grad(k, xt_b, g_gate, FB, up_v, 0, twin_gate, relay_gate, sum_gate)
    up_g = Grad(k, xt_b, g_up, FB, down_v, 0, twin_up, relay_up, sum_up)
    down_g.first()
    turn_over(n2_s, xt_b)
    gate_g.first()
    down_g.second(local.at[2])
    two.relay()

    @pl.loop(0, D // 256)
    def _(n):
        at = ds(n * 256, 256)
        part2_b[:, at] = dot(inner[...], down_v[at], 1, 1).astype(BF)

    up_g.first()
    gate_g.second(local.at[3])
    up_g.second(local.at[4])
    down_g.third()

    def norm_back(grad, vectors, gain):
        inv = lax.rsqrt(jnp.mean(vectors * vectors, axis=-1, keepdims=True) + EPS)
        unit = vectors * inv
        weighted = grad * gain
        g_gain = jnp.sum(grad * unit, axis=0, keepdims=True)
        return inv * (weighted - unit * jnp.mean(weighted * unit, axis=-1, keepdims=True)), g_gain

    d_mid, gain_two = norm_back(two.total(), mid_s[...], gain_row(1))
    g_mid = gall[at_t].astype(F32) + d_mid
    hid_ref[...] = g_mid
    gm[at_t] = g_mid.astype(BF)
    gm_gather = ZGather(k, gm, rows)
    gate_g.third()
    turn_over(n1_s, xt_b)
    gm_gather.relay()
    up_g.third()
    gm_gather.wait()
    branch = ZScatter(k, part2_b, slots2, middle_b, rows)
    for at, n in chunks(QW, 256):
        g_attn[:, at:at + n] = dot(gm[...], w_v[:, QKV + at:QKV + at + n]).astype(BF)
    g_kv[...] = jnp.zeros_like(g_kv)

    @pl.loop(0, nh // 2)
    def _(n):
        at = ds(n * pair, pair)
        two_q = q_s[:, at] * BF(scale)
        two_g = g_attn[:, at]
        g_qs, g_kvs = [], []
        for e in range(2):
            q_one, g_one = two_q[:, e * hd:(e + 1) * hd], two_g[:, e * hd:(e + 1) * hd]
            lse = jnp.sum(jnp.where(lane == 2 * n + e, lse_s[...], 0.0), axis=1, keepdims=True)
            p = jnp.exp(dot(q_one, k_s[...], 1, 1) + bias[...] - lse)
            dp = dot(g_one, v_s[...], 1, 1)
            delta = jnp.sum(p * dp, axis=-1, keepdims=True)
            d_scores = (p * (dp - delta)).astype(BF)
            g_qs.append(dot(d_scores, k_s[...]) * scale)
            g_kvs.append(
                jnp.concatenate([dot(d_scores, q_one, 0, 0), dot(p.astype(BF), g_one, 0, 0)], axis=1)
            )
        g_qkv[:, at] = turn_back(jnp.concatenate(g_qs, axis=1)).astype(BF)
        g_kv[...] += g_kvs[0] + g_kvs[1]

    g_kvb[...] = g_kv[...].astype(BF)
    kv_copies = []
    for i in range(1, C):
        piece = g_kvb.at[ds(((k.c + i) % C) * span, span)]
        kv_copies.append(k.send(piece, kv_slots.at[i - 1], k.cpeer(i)))
    branch.relay()
    turn_over(gm, xt_a)
    out_g = Grad(k, xt_a, attn_s, QW, w_v, QKV, twin_out, relay_out, sum_out)
    out_g.first()
    own_kv = g_kv[at_c]
    for i in range(1, C):
        kv_copies[i - 1].wait_recv()
        own_kv = own_kv + kv_slots[i - 1].astype(F32)
    g_qkv[:, QW:] = jnp.where(lane < hd, turn_back(own_kv), own_kv).astype(BF)
    k.finish([two.far] * two.line + list(two.copies.values()))

    @pl.loop(0, D // 256)
    def _(n):
        at = ds(n * 256, 256)
        part_b[:, at] = dot(g_qkv[...], w_v[at, :QKV], 1, 1).astype(BF)

    last = ZScatter(k, part_b, slots, middle_a, rows)
    out_g.second(local.at[5])
    qkv_g = Grad(k, xt_b, g_qkv, QKV, w_v, 0, twin_qkv, relay_qkv, sum_qkv)
    qkv_g.first()
    last.relay()
    qkv_g.second(local.at[6])
    out_ref[...] = (padc[at_t] * (mid_s[...] + branch.total())).astype(BF)
    out_g.third()
    qkv_g.third()
    d_hid, gain_one = norm_back(last.total(), hidden_ref[...].astype(F32), gain_row(0))
    hid_ref[...] = hid_ref[...] + d_hid

    for b in range(F * C):
        gz[b] = jnp.concatenate(
            [gain_one[:, b * R:(b + 1) * R], gain_two[:, b * R:(b + 1) * R]], axis=1
        )
    z_copies = [k.send(gz, gz_slots.at[i - 1], k.zpeer(i)) for i in range(1, T)]
    both = gz[...]
    for i in range(1, T):
        z_copies[i - 1].wait_recv()
        both = both + gz_slots[i - 1]
    gx[...] = both
    x_copies = []
    for n, dev in enumerate(k.plane_peers()):
        x_copies.append(k.send(gx.at[dev[0] * C + dev[1]], gx_slots.at[n], dev))
    both = gx[mine]
    for n, copy in enumerate(x_copies):
        copy.wait_recv()
        both = both + gx_slots[n]
    gg_ref[...] = both
    for grad in (down_g, gate_g, up_g, out_g, qkv_g):
        grad.done()
    k.finish()


def layer(sizes, hd, hidden, seg, pad, ga, gm, wq, wk, wv, wo, wd, cot, wg, wu):
    F, C, T = sizes
    H = C // 2
    rows, D = hidden.shape
    R, QW = wq.shape
    FB = wg.shape[1]
    span, length, QKV = rows * T, seg.shape[1], QW + 2 * hd
    vm = pl.BlockSpec(memory_space=pltpu.VMEM)
    hbm = pl.BlockSpec(memory_space=pl.ANY)
    n_sems = n_semaphores(F, C, T)
    S = jax.ShapeDtypeStruct
    V = pltpu.VMEM
    FH, lines, diag = F * H, F + H - 1, max(1, (F - 1) * (H - 1))
    widths = (FB, FB, FB, QW, QKV)
    return pl.pallas_call(
        functools.partial(layer_kernel, sizes, hd),
        out_shape=(
            S((rows, D), BF), S((rows, D), F32), S((1, 2 * R), F32),
            *[S((lines, R, n), BF) for n in widths],
        ),
        in_specs=[vm] * 11 + [hbm] * 2,
        out_specs=[vm] * 3 + [hbm] * 5,
        scratch_shapes=[
            V((D, QW + QKV), BF), V((D, FB), BF), V((D, FB), BF), V((D, FB), BF),
            V((span, D), BF), V((span, D), BF), V((span, D), BF), V((span, D), BF),
            V((D, span), BF), V((D, span), BF),
            V((span, FB), BF), V((span, FB), BF), V((span, FB), BF),
            V((span, QW), BF), V((span, QW), BF), V((span, QW), BF), V((span, QKV), BF),
            V((span, 2 * hd), F32), V((length, 2 * hd), BF), V((length, hd), BF), V((length, hd), BF),
            V((length, 2 * hd), F32), V((length, 2 * hd), BF), V((C - 1, span, 2 * hd), BF),
            V((span, length), F32), V((span, 2 * hd), F32), V((span, 2 * hd), F32), V((span, 1), F32),
            V((span, D), BF), V((span, D), BF), V((T - 1, rows, D), BF), V((T - 1, rows, D), BF),
            V((rows, D), BF), V((rows, D), BF), V((rows, D), F32),
            *[V((FH, R, n), BF) for n in widths],
            *[V((diag, 2, R // 2, n), BF) for n in widths],
            V((F * C, 1, 2 * R), F32), V((F * C, 1, 2 * R), F32), V((T - 1, F * C, 1, 2 * R), F32),
            V((F * C, 1, 2 * R), F32), V((F * C - 1, 1, 2 * R), F32),
            pltpu.SemaphoreType.DMA((n_sems,)), pltpu.SemaphoreType.DMA((n_sems,)),
            pltpu.SemaphoreType.DMA((7,)),
        ],
        compiler_params=pltpu.CompilerParams(
            collective_id=0, has_side_effects=True, vmem_limit_bytes=62 * 2**20
        ),
        name="layer",
    )(hidden, seg, pad, ga, gm, wq, wk, wv, wo, wd, cot, wg, wu)


def body(hidden_in, segment_ids, pad_mask, attn_gain, w_query, w_key, w_value, w_out,
         mlp_gain, w_gate, w_up, w_down, cotangent):
    sizes = tuple(lax.axis_size(n) for n in ("fsdp", "context", "tensor"))
    hd = w_key.shape[1]
    R, QW = w_query.shape
    block_out, grad_hidden, gg, s_down, s_gate, s_up, s_out, s_qkv = layer(
        sizes, hd, hidden_in[0], segment_ids, pad_mask, attn_gain[None], mlp_gain[None],
        w_query, w_key.T, w_value.T, w_out, w_down, cotangent[0], w_gate, w_up,
    )

    def total(parts):
        return jnp.sum(parts.astype(F32), axis=0)

    grad_qkv = total(s_qkv)
    return (
        block_out[None], grad_hidden[None], gg[0, :R], grad_qkv[:, :QW],
        grad_qkv[:, QW:QW + hd], grad_qkv[:, QW + hd:], total(s_out).T, gg[0, R:],
        total(s_gate), total(s_up), total(s_down).T,
    )


def solution(mesh):
    rows = P("fsdp", ("context", "tensor"), None)
    tail = (P(FC), P(FC, "tensor"), P(FC, "tensor"), P(FC, "tensor"), P("tensor", FC),
            P(FC), P(FC, "tensor"), P(FC, "tensor"), P("tensor", FC))
    in_specs = (rows, P("fsdp", None), P("fsdp", None)) + tail + (rows,)
    out_specs = (rows, rows) + tail
    return jax.shard_map(body, mesh=mesh, in_specs=in_specs, out_specs=out_specs, check_vma=False)
```

time: 634 us -> 252 us (0.40)
  waiting for transfers between devices: 383 us -> 0 us
  Pallas kernels: 109 us -> 232 us
  matrix products: 68.4 us -> 0 us
  other arithmetic: 23.6 us -> 8.38 us
  between operations: 14.5 us -> 0.68 us
  local copies, waits for them, and re-layouts: 22.4 us -> 10.1 us
  blocking collectives: 11.7 us -> 0 us
    reduce_scatter x9 -> x0, waiting for transfers between devices: 326 us -> none  [the longest x5 236 us: scatter_g(): lax.psum_scatter(g.astype(BF), FC, scatter_dimension=0, tiled=True)]
    pallas_call x1, Pallas kernels: 109 us -> 232 us  [layer(): pl.pallas_call(functools.partial(layer_kernel, sizes, hd), out_shape=(S((...]
    dot_general x18 -> x0, matrix products: 68.4 us -> none  [the longest x13 46.8 us: dot(): lax.dot_general(a, b, (((ca,), (cb,)), ((), ())), preferred_element_type=...]
    unnamed x12 -> x0, waiting for transfers between devices: 36.7 us -> none
    all_gather x1 -> x0, waiting for transfers between devices: 20 us -> none  [rows_gather(): return lax.all_gather(x, 'tensor', axis=0, tiled=True)]
    psum x1 -> x0, blocking collectives: 11.7 us -> none  [body(): grads = lax.psum(grads, 'tensor')]
    convert_element_type x7 -> x0, other arithmetic: 11.3 us -> none  [the longest x2 4.6 us: scatter_g(): lax.psum_scatter(g.astype(BF), FC, scatter_dimension=0, tiled=True)]
    unnamed x66 -> x12, local copies, waits for them, and re-layouts: 12.6 us -> 5.46 us
  transfers between devices with their start and end apart: 11 -> 0, of which waited for: 11 -> 0; matrix products, arithmetic and copies ran while one was open for 8% -> 0% of each run, Pallas kernels for 0% -> 0%
where the time goes in v4:
time: 252 us; the launch traced here: 251 us
  Pallas kernels  232 us (92%)
  local copies, waits for them, and re-layouts  10.1 us (4%)
  other arithmetic  8.38 us (3%)
    pallas_call x1, Pallas kernels, layer(): pl.pallas_call(functools.partial(layer_kernel, sizes, hd), out_shape=(S((...  232 us
    reduce_sum x4, other arithmetic, total(): return jnp.sum(parts.astype(F32), axis=0)  8.38 us
    unnamed x12, local copies, waits for them, and re-layouts  5.46 us

profile of v4, /device:TPU:0, one launch (start us, length us, event | category | flops | bytes accessed | tf_op | source)
XLA Modules:
  0.0 251.4 jit_solution(13931628964344094947)
XLA Ops:
  0.6 1.2 broadcast_in_dim.12.ga_ref
  1.9 1.2 broadcast_in_dim.13.gm_ref
  3.1 232.2 %layer.1 = (bf16[64,2048]{1,0:T(8,128)(2,1)}, f32[64,2048]{1,0:T(8,128)}, f32[1,512]{1,0:T(1,128)}, bf16[3,256,1408]{2,1,0:T(8,128)(2,1)}, bf16[3,256,1408]{2,1,...) custom-call(bf16[64,2048]{1,0:T(8,128)(2,1)} %bitcast.14, ...), custom_call_target="tpu_custom_call" | custom-call | tf_op jit(solution)/shard_map/layer/pallas_call | solution.py:654
  235.3 1.3 fusion.1
  236.5 1.3 convert_reduce_fusion.4
  237.8 0.0 copy-start
  237.9 1.0 copy.27
  238.8 1.4 convert_reduce_fusion.3
  240.3 0.1 fusion
  240.4 0.9 slice.20
  241.2 0.7 copy.26
  241.9 0.7 copy.25
  242.6 0.0 copy-done
  242.6 1.4 convert_reduce_fusion.2
  244.0 4.3 %convert_reduce_fusion = (f32[256,1408]{1,0:T(8,128)S(1)}, f32[256,1408]{1,0:T(8,128)}) fusion(bf16[3,256,1408]{2,1,0:T(8,128)(2,1)} %get-tuple-element.26, bf16[3,256,1408]{2,1,0:T(8,128)(2,1)} %get-tuple-element.25), kind=kLoop, calls=%fused_computation | loop fusion | flops 3604480 | bytes 7208960 | tf_op jit(solution)/shard_map/reduce_sum | solution.py:698
  248.3 0.0 copy-start.2
  248.3 0.0 copy-start.1
  248.3 1.5 copy.28
  249.9 0.0 copy-done.2
  249.9 0.7 copy.31
  250.6 0.0 copy-done.1
  250.6 0.8 copy.32
Async XLA Ops:
  237.8 4.8 %copy-start = (bf16[3,256,1408]{2,1,0:T(8,128)(2,1)S(1)}, bf16[3,256,1408]{2,1,0:T(8,128)(2,1)}, u32[]{:S(2)}) copy-start(bf16[3,256,1408]{2,1,0:T(8,128)(2,1)} %get-tuple-element.24) | copy-start | bytes 6488068
  248.3 1.5 copy-start.2
  248.3 2.2 copy-start.1

commit v5 on v4

--- a/solution.py
+++ b/solution.py
@@ -10,6 +10,7 @@
 
 EPS = 1e-05
 NEG = -1e30
+DOC = 512
 BF = jnp.bfloat16
 F32 = jnp.float32
 MESH = pl.DeviceIdType.MESH
@@ -161,17 +162,19 @@
 
 
 class ZGather:
-    def __init__(self, k, full, rows):
+    def __init__(self, k, full, rows, own=None):
         self.k, self.full, self.rows = k, full, rows
         T = k.T
         piece = full.at[ds(k.t * rows, rows)]
-        self.copies = {i: k.new(piece, piece, k.zpeer(i)) for i in range(1, T)}
+        own = piece if own is None else own
+        self.copies = {i: k.new(own, piece, k.zpeer(i)) for i in range(1, T)}
         for i in [2, 1, 3] if T == 4 else range(1, T):
             cond = None
             if T == 4 and i != 2:
                 cond = (k.t < 3) if i == 1 else (k.t > 0)
             k.start(self.copies[i][0], cond)
         self.left = list(range(1, T))
+        self.relays = []
 
     def relay(self):
         k = self.k
@@ -183,6 +186,10 @@
             piece = self.full.at[ds(origin * self.rows, self.rows)]
             copy, _ = k.new(piece, piece, (k.f, k.c, 3 - origin), recv=self.copies[i][1])
             k.start(copy, k.t == at)
+            self.relays.append(copy)
+
+    def sent(self):
+        self.k.finish([c for c, _ in self.copies.values()] + self.relays)
 
     def wait(self):
         for i in self.left:
@@ -247,36 +254,32 @@
 
 
 class Grad:
-    def __init__(self, k, xt, y, width, stage, lane, twin, relay, out):
+    def __init__(self, k, xt, y, width, stage, twin, relay, out):
         self.k, self.xt, self.y, self.width, self.stage = k, xt, y, width, stage
-        self.lane, self.twin, self.relay, self.out = lane, twin, relay, out
+        self.twin, self.relay, self.out = twin, relay, out
         self.R = xt.shape[0] // (k.F * k.C)
 
     def rows_of(self, s, core):
         return ds(self.k.block(s // self.k.H, s % self.k.H, core) * self.R, self.R)
 
-    def piece(self, df, dh, core, half=None):
-        block = self.k.block(df, dh, core)
-        at = ds(block * self.R, self.R)
-        if half is not None:
-            n = self.R // 2
-            at = ds(block * self.R + half * n, n)
-        return self.stage.at[at, self.lane:self.lane + self.width]
+    def piece(self, df, dh, half=None):
+        s = df * self.k.H + dh
+        if half is None:
+            return self.twin.at[s]
+        n = self.R // 2
+        return self.twin.at[s, half * n:(half + 1) * n]
 
     def first(self):
         k = self.k
 
         @pl.loop(0, k.F * k.H)
         def _(s):
-            at = self.rows_of(s, 1 - k.core)
-            x = self.xt[at]
+            x = self.xt[self.rows_of(s, 1 - k.core)]
+            to = self.stage(s)
             for a, n in chunks(self.width, 256):
-                self.stage[at, self.lane + a:self.lane + a + n] = dot(x, self.y[:, a:a + n]).astype(BF)
-
-        self.twins = [
-            k.send(self.piece(s // k.H, s % k.H, 1 - k.core), self.twin.at[s], k.sib)
-            for s in range(k.F * k.H)
-        ]
+                to[:, a:a + n] = dot(x, self.y[:, a:a + n]).astype(BF)
+
+        self.twins = [k.send(self.stage(s), self.twin.at[s], k.sib) for s in range(k.F * k.H)]
 
     def second(self, sem):
         k = self.k
@@ -285,11 +288,10 @@
 
         @pl.loop(0, k.F * k.H)
         def _(s):
-            at = self.rows_of(s, k.core)
-            x = self.xt[at]
+            x = self.xt[self.rows_of(s, k.core)]
             for a, n in chunks(self.width, 256):
                 total = dot(x, self.y[:, a:a + n]) + self.twin[s, :, a:a + n].astype(F32)
-                self.stage[at, self.lane + a:self.lane + a + n] = total.astype(BF)
+                self.twin[s, :, a:a + n] = total.astype(BF)
 
         self.diag = {}
         n = 0
@@ -297,14 +299,14 @@
             for dh in range(1, k.H):
                 for half, dev in ((0, k.chip(df, 0)), (1, k.chip(0, dh))):
                     self.diag[df, dh, half] = n, half, k.send(
-                        self.piece(df, dh, k.core, half), self.relay.at[n, half], dev
+                        self.piece(df, dh, half), self.relay.at[n, half], dev
                     )
                 n += 1
-        self.own = pltpu.make_async_copy(self.piece(0, 0, k.core), self.out.at[0], sem)
+        self.own = pltpu.make_async_copy(self.piece(0, 0), self.out.at[0], sem)
         self.own.start()
 
     def add(self, df, dh, half):
-        piece = self.piece(df, dh, self.k.core, half)
+        piece = self.piece(df, dh, half)
         total = piece[...].astype(F32)
         for (ef, eh, other), (n, _, copy) in self.diag.items():
             if other == half and (ef == df or df == 0) and (eh == dh or dh == 0):
@@ -318,11 +320,11 @@
         for dh in range(1, k.H):
             if k.F > 1:
                 self.add(0, dh, 0)
-            self.far.append(k.send(self.piece(0, dh, k.core), self.out.at[k.F - 1 + dh], k.chip(0, dh)))
+            self.far.append(k.send(self.piece(0, dh), self.out.at[k.F - 1 + dh], k.chip(0, dh)))
         for df in range(1, k.F):
             if k.H > 1:
                 self.add(df, 0, 1)
-            self.far.append(k.send(self.piece(df, 0, k.core), self.out.at[df], k.chip(df, 0)))
+            self.far.append(k.send(self.piece(df, 0), self.out.at[df], k.chip(df, 0)))
 
     def done(self):
         for copy in self.far:
@@ -355,7 +357,7 @@
     rows, D = hidden_ref.shape
     R, QW = wq_ref.shape
     FB = wg_hbm.shape[1]
-    span, length = bias.shape
+    span, length = bias.shape[0], seg_ref.shape[1]
     nh = QW // hd
     QKV = QW + 2 * hd
     pair = 2 * hd
@@ -371,7 +373,8 @@
     kv_w = jnp.concatenate([wk_ref[...], wv_ref[...]], axis=0)
     own_w[:, QW:QKV] = kv_w.astype(F32).T.astype(BF)
     own_w[:, QKV:] = wo_ref[...].astype(F32).T.astype(BF)
-    gains_s[mine] = jnp.concatenate([ga_ref[...], gm_ref[...]], axis=1).astype(F32)
+    gains_s[mine, :, :R] = ga_ref[...].astype(F32).reshape(1, R)
+    gains_s[mine, :, R:] = gm_ref[...].astype(F32).reshape(1, R)
     loads = [
         pltpu.make_async_copy(wg_hbm, gw.part(), local.at[0]),
         pltpu.make_async_copy(wu_hbm, uw.part(), local.at[1]),
@@ -379,23 +382,17 @@
     for copy in loads:
         copy.start()
     k.meet()
+    h_gather = ZGather(k, gm, rows, hidden_ref)
+    gm[at_t] = hidden_ref[...]
     own_gain = gains_s.at[mine]
     gain_copies = [k.send(own_gain, own_gain, dev) for dev in k.plane_peers()]
     aw.first(own_w)
-
-    hidden = hidden_ref[...].astype(F32)
-    scale_one = lax.rsqrt(jnp.mean(hidden * hidden, axis=-1, keepdims=True) + EPS)
-    hidden = hidden * scale_one
-    for copy in gain_copies:
-        copy.wait_recv()
 
     def gain_row(which):
         return jnp.concatenate(
             [gains_s[b][:, which * R:(which + 1) * R] for b in range(F * C)], axis=1
         )
 
-    n1_s[at_t] = (hidden * gain_row(0)).astype(BF)
-    n1_gather = ZGather(k, n1_s, rows)
     down_v[ds(mine * R, R)] = wd_ref[...].astype(F32).T.astype(BF)
 
     def column_of(row):
@@ -403,9 +400,12 @@
 
     seg = seg_ref[...].astype(F32)
     seg_col = column_of(seg_ref[:, at_c])
+    win = bias.shape[1]
+    win_at = jnp.maximum(k.c * span + span - win, 0)
+    at_w = pl.ds(pl.multiple_of(win_at, span), win)
     padc[...] = column_of(pad_ref[:, at_c])
     row_at = k.c * span + lax.broadcasted_iota(jnp.int32, (span, 1), 0)
-    column = lax.broadcasted_iota(jnp.int32, (span, length), 1)
+    column = win_at + lax.broadcasted_iota(jnp.int32, (span, win), 1)
     first = jnp.sum(jnp.where(seg < seg_col, 1.0, 0.0), axis=1, keepdims=True)
     lane = lax.broadcasted_iota(jnp.int32, (1, pair), 1)
     frequency = jnp.exp(-((lane % (hd // 2)).astype(F32) * (2.0 / hd)) * math.log(10000.0))
@@ -413,7 +413,9 @@
     angles = (row_at.astype(F32) - first) * frequency
     cos_s[...] = jnp.cos(angles)
     sin_s[...] = jnp.where(low, -1.0, 1.0) * jnp.sin(angles)
-    allowed = (seg == seg_col) & (column <= row_at) & ((pad_ref[...] == 1) | (column == row_at))
+    allowed = (seg_ref[:, at_w].astype(F32) == seg_col) & (column <= row_at) & (
+        (pad_ref[:, at_w] == 1) | (column == row_at)
+    )
     bias[...] = jnp.where(allowed, 0.0, NEG)
     keep = padc[at_t]
     gall[at_t] = (cot_ref[...].astype(F32) * keep).astype(BF)
@@ -429,9 +431,20 @@
 
     aw.second()
     gw.first(wg_hbm)
-    n1_gather.relay()
+    h_gather.relay()
     aw.third()
-    n1_gather.wait()
+    for copy in gain_copies:
+        copy.wait_recv()
+    gain_one_row = gain_row(0)
+    h_gather.wait()
+
+    @pl.loop(0, T)
+    def _(n):
+        at = ds(n * rows, rows)
+        h = gm[at].astype(F32)
+        inv = lax.rsqrt(jnp.mean(h * h, axis=-1, keepdims=True) + EPS)
+        n1_s[at] = (h * inv * gain_one_row).astype(BF)
+
     g_gather = ZGather(k, gall, rows)
     aw.done()
 
@@ -445,8 +458,8 @@
             q_s[:, at + b:at + b + pair] = turn(pre[:, b:b + pair]).astype(BF)
     for copy in kv_copies:
         copy.wait_recv()
-    k_s[...] = kv_s[:, :hd]
-    v_s[...] = kv_s[:, hd:]
+    k_s[...] = kv_s[at_w, :hd]
+    v_s[...] = kv_s[at_w, hd:]
     gw.second()
     uw.first(wu_hbm)
     lse_s[...] = jnp.zeros_like(lse_s)
@@ -472,6 +485,7 @@
         at = ds(n * 256, 256)
         part_b[:, at] = dot(attn_s[...], w_v[at, QKV:], 1, 1).astype(BF)
 
+    h_gather.sent()
     one = ZScatter(k, part_b, slots, middle_a, rows)
     gw.third()
     one.relay()
@@ -493,23 +507,34 @@
     n2_gather = ZGather(k, n2_s, rows)
     uw.third()
     n2_gather.relay()
-    dw.second()
-    n2_gather.wait()
-    dw.third()
-    for weight in (gw, uw, dw):
-        weight.done()
+    gw.done()
+    uw.done()
     for copy in loads:
         copy.wait()
-    k.finish([one.far] * one.line + list(one.copies.values()))
+    n2_gather.wait()
 
     for at, n in chunks(FB, 256):
         gate = dot(n2_s[...], gate_v[:, at:at + n])
         up = dot(n2_s[...], up_v[:, at:at + n])
         sig = jax.nn.sigmoid(gate)
         inner[:, at:at + n] = (gate * sig * up).astype(BF)
+        g_gate[:, at:at + n] = (up * sig * (1.0 + gate * (1.0 - sig))).astype(BF)
+        g_up[:, at:at + n] = (gate * sig).astype(BF)
+
+    down_g = Grad(k, xt_a, inner, FB, lambda s: twin_up.at[s], twin_down, relay_down, sum_down)
+    down_g.first()
+    dw.second()
+    turn_over(n2_s, xt_b)
+    down_g.second(local.at[2])
+    k.finish(down_g.twins)
+    dw.third()
+    dw.done()
+    for at, n in chunks(FB, 256):
         g_in = dot(gall[...], down_v[:, at:at + n])
-        g_gate[:, at:at + n] = (g_in * up * sig * (1.0 + gate * (1.0 - sig))).astype(BF)
-        g_up[:, at:at + n] = (g_in * gate * sig).astype(BF)
+        g_gate[:, at:at + n] = (g_in * g_gate[:, at:at + n].astype(F32)).astype(BF)
+        g_up[:, at:at + n] = (g_in * g_up[:, at:at + n].astype(F32)).astype(BF)
+
+    k.finish([one.far] * one.line + list(one.copies.values()))
 
     @pl.loop(0, D // 256)
     def _(n):
@@ -520,24 +545,23 @@
     two = ZScatter(k, part_b, slots, middle_a, rows)
     for weight in (aw, gw, uw, dw):
         weight.sent()
-    down_g = Grad(k, xt_a, inner, FB, gate_v, 0, twin_down, relay_down, sum_down)
-    gate_g = Grad(k, xt_b, g_gate, FB, up_v, 0, twin_gate, relay_gate, sum_gate)
-    up_g = Grad(k, xt_b, g_up, FB, down_v, 0, twin_up, relay_up, sum_up)
-    down_g.first()
-    turn_over(n2_s, xt_b)
+
+    def spare(room, lane, width):
+        return lambda s: room.at[ds(s * R, R), lane:lane + width]
+
+    gate_g = Grad(k, xt_b, g_gate, FB, spare(gate_v, 0, FB), twin_gate, relay_gate, sum_gate)
+    up_g = Grad(k, xt_b, g_up, FB, spare(up_v, 0, FB), twin_up, relay_up, sum_up)
     gate_g.first()
-    down_g.second(local.at[2])
+    up_g.first()
     two.relay()
+    gate_g.second(local.at[3])
+    up_g.second(local.at[4])
+    down_g.third()
 
     @pl.loop(0, D // 256)
     def _(n):
         at = ds(n * 256, 256)
         part2_b[:, at] = dot(inner[...], down_v[at], 1, 1).astype(BF)
-
-    up_g.first()
-    gate_g.second(local.at[3])
-    up_g.second(local.at[4])
-    down_g.third()
 
     def norm_back(grad, vectors, gain):
         inv = lax.rsqrt(jnp.mean(vectors * vectors, axis=-1, keepdims=True) + EPS)
@@ -554,7 +578,6 @@
     gate_g.third()
     turn_over(n1_s, xt_b)
     gm_gather.relay()
-    up_g.third()
     gm_gather.wait()
     branch = ZScatter(k, part2_b, slots2, middle_b, rows)
     for at, n in chunks(QW, 256):
@@ -579,7 +602,7 @@
                 jnp.concatenate([dot(d_scores, q_one, 0, 0), dot(p.astype(BF), g_one, 0, 0)], axis=1)
             )
         g_qkv[:, at] = turn_back(jnp.concatenate(g_qs, axis=1)).astype(BF)
-        g_kv[...] += g_kvs[0] + g_kvs[1]
+        g_kv[at_w] += g_kvs[0] + g_kvs[1]
 
     g_kvb[...] = g_kv[...].astype(BF)
     kv_copies = []
@@ -587,8 +610,9 @@
         piece = g_kvb.at[ds(((k.c + i) % C) * span, span)]
         kv_copies.append(k.send(piece, kv_slots.at[i - 1], k.cpeer(i)))
     branch.relay()
+    up_g.third()
     turn_over(gm, xt_a)
-    out_g = Grad(k, xt_a, attn_s, QW, w_v, QKV, twin_out, relay_out, sum_out)
+    out_g = Grad(k, xt_a, attn_s, QW, spare(w_v, QKV, QW), twin_out, relay_out, sum_out)
     out_g.first()
     own_kv = g_kv[at_c]
     for i in range(1, C):
@@ -604,7 +628,7 @@
 
     last = ZScatter(k, part_b, slots, middle_a, rows)
     out_g.second(local.at[5])
-    qkv_g = Grad(k, xt_b, g_qkv, QKV, w_v, 0, twin_qkv, relay_qkv, sum_qkv)
+    qkv_g = Grad(k, xt_b, g_qkv, QKV, spare(w_v, 0, QKV), twin_qkv, relay_qkv, sum_qkv)
     qkv_g.first()
     last.relay()
     qkv_g.second(local.at[6])
@@ -646,6 +670,7 @@
     span, length, QKV = rows * T, seg.shape[1], QW + 2 * hd
     vm = pl.BlockSpec(memory_space=pltpu.VMEM)
     hbm = pl.BlockSpec(memory_space=pl.ANY)
+    win = min(length, span + -(-DOC // span) * span)
     n_sems = n_semaphores(F, C, T)
     S = jax.ShapeDtypeStruct
     V = pltpu.VMEM
@@ -665,9 +690,9 @@
             V((D, span), BF), V((D, span), BF),
             V((span, FB), BF), V((span, FB), BF), V((span, FB), BF),
             V((span, QW), BF), V((span, QW), BF), V((span, QW), BF), V((span, QKV), BF),
-            V((span, 2 * hd), F32), V((length, 2 * hd), BF), V((length, hd), BF), V((length, hd), BF),
+            V((span, 2 * hd), F32), V((length, 2 * hd), BF), V((win, hd), BF), V((win, hd), BF),
             V((length, 2 * hd), F32), V((length, 2 * hd), BF), V((C - 1, span, 2 * hd), BF),
-            V((span, length), F32), V((span, 2 * hd), F32), V((span, 2 * hd), F32), V((span, 1), F32),
+            V((span, win), F32), V((span, 2 * hd), F32), V((span, 2 * hd), F32), V((span, 1), F32),
             V((span, D), BF), V((span, D), BF), V((T - 1, rows, D), BF), V((T - 1, rows, D), BF),
             V((rows, D), BF), V((rows, D), BF), V((rows, D), F32),
             *[V((FH, R, n), BF) for n in widths],
@@ -684,24 +709,73 @@
     )(hidden, seg, pad, ga, gm, wq, wk, wv, wo, wd, cot, wg, wu)
 
 
+def final_kernel(
+    hd, out_ref, hid_ref, down_ref, gate_ref, up_ref, wo_ref, qkv_ref,
+    block_out, grad_hidden, g_query, g_key, g_value, g_out, g_gate, g_up, g_down,
+):
+    def total(ref):
+        return sum(ref[i].astype(F32) for i in range(ref.shape[0]))
+
+    QW = g_query.shape[1]
+    block_out[...] = out_ref[...]
+    grad_hidden[...] = hid_ref[...]
+    qkv = total(qkv_ref)
+    g_query[...] = qkv[:, :QW]
+    kv = qkv[:, QW:].T
+    g_key[...] = kv[:hd]
+    g_value[...] = kv[hd:]
+    g_out[...] = total(wo_ref).T
+    g_gate[...] = total(gate_ref)
+    g_up[...] = total(up_ref)
+    g_down[...] = total(down_ref).T
+
+
+def final(hd, block_out, grad_hidden, s_down, s_gate, s_up, s_out, s_qkv):
+    L, R, FB = s_gate.shape
+    QW = s_out.shape[2]
+    rows, D = block_out.shape
+    steps = R // 128 if R % 128 == 0 else 1
+    r = R // steps
+    S = jax.ShapeDtypeStruct
+
+    def parts(x):
+        return pl.BlockSpec((L, r, x.shape[2]), lambda i: (0, i, 0))
+
+    def tall(n):
+        return pl.BlockSpec((r, n), lambda i: (i, 0))
+
+    def wide(n):
+        return pl.BlockSpec((n, r), lambda i: (0, i))
+
+    acts = pl.BlockSpec((rows // steps, D), lambda i: (i, 0))
+    return pl.pallas_call(
+        functools.partial(final_kernel, hd),
+        grid=(steps,),
+        out_shape=(
+            S((rows, D), BF), S((rows, D), F32), S((R, QW), F32), S((hd, R), F32), S((hd, R), F32),
+            S((QW, R), F32), S((R, FB), F32), S((R, FB), F32), S((FB, R), F32),
+        ),
+        in_specs=[acts, acts] + [parts(x) for x in (s_down, s_gate, s_up, s_out, s_qkv)],
+        out_specs=[acts, acts, tall(QW), wide(hd), wide(hd), wide(QW), tall(FB), tall(FB), wide(FB)],
+        compiler_params=pltpu.CompilerParams(vmem_limit_bytes=48 * 2**20),
+        name="final",
+    )(block_out, grad_hidden, s_down, s_gate, s_up, s_out, s_qkv)
+
+
 def body(hidden_in, segment_ids, pad_mask, attn_gain, w_query, w_key, w_value, w_out,
          mlp_gain, w_gate, w_up, w_down, cotangent):
     sizes = tuple(lax.axis_size(n) for n in ("fsdp", "context", "tensor"))
-    hd = w_key.shape[1]
-    R, QW = w_query.shape
-    block_out, grad_hidden, gg, s_down, s_gate, s_up, s_out, s_qkv = layer(
-        sizes, hd, hidden_in[0], segment_ids, pad_mask, attn_gain[None], mlp_gain[None],
+    hd, R = w_key.shape[1], w_query.shape[0]
+    block_out, grad_hidden, gg, *parts = layer(
+        sizes, hd, hidden_in[0], segment_ids, pad_mask, attn_gain, mlp_gain,
         w_query, w_key.T, w_value.T, w_out, w_down, cotangent[0], w_gate, w_up,
     )
-
-    def total(parts):
-        return jnp.sum(parts.astype(F32), axis=0)
-
-    grad_qkv = total(s_qkv)
+    block_out, grad_hidden, g_query, g_key, g_value, g_out, g_gate, g_up, g_down = final(
+        hd, block_out, grad_hidden, *parts
+    )
     return (
-        block_out[None], grad_hidden[None], gg[0, :R], grad_qkv[:, :QW],
-        grad_qkv[:, QW:QW + hd], grad_qkv[:, QW + hd:], total(s_out).T, gg[0, R:],
-        total(s_gate), total(s_up), total(s_down).T,
+        block_out[None], grad_hidden[None], gg[0, :R], g_query, g_key.T, g_value.T, g_out, gg[0, R:],
+        g_gate, g_up, g_down,
     )
 
 

time: 252 us -> 226 us (0.90)
  Pallas kernels: 232 us -> 218 us
  other arithmetic: 8.38 us -> 0 us
  local copies, waits for them, and re-layouts: 10.1 us -> 6.5 us
    pallas_call x1, Pallas kernels: 232 us -> 213 us  [layer(): pl.pallas_call(functools.partial(layer_kernel, sizes, hd), out_shape=(S((...]
    reduce_sum x4 -> x0, other arithmetic: 8.38 us -> none  [total(): return jnp.sum(parts.astype(F32), axis=0)]
    pallas_call x0 -> x1, Pallas kernels: none -> 4.61 us  [final(): pl.pallas_call(functools.partial(final_kernel, hd), grid=(steps,), out_sh...]
where the time goes in v5:
time: 226 us; the launch traced here: 225 us
  Pallas kernels  218 us (96%)
  local copies, waits for them, and re-layouts  6.5 us (3%)
    pallas_call x1, Pallas kernels, layer(): pl.pallas_call(functools.partial(layer_kernel, sizes, hd), out_shape=(S((...  213 us
    unnamed x12, local copies, waits for them, and re-layouts  5.93 us
    pallas_call x1, Pallas kernels, final(): pl.pallas_call(functools.partial(final_kernel, hd), grid=(steps,), out_sh...  4.61 us

profile of v5, /device:TPU:0, one launch (start us, length us, event | category | flops | bytes accessed | tf_op | source)
XLA Modules:
  0.0 225.2 jit_solution(16059167704492291276)
XLA Ops:
  0.6 213.4 %layer.1 = (bf16[64,2048]{1,0:T(8,128)(2,1)}, f32[64,2048]{1,0:T(8,128)}, f32[1,512]{1,0:T(1,128)}, bf16[3,256,1408]{2,1,0:T(8,128)(2,1)}, bf16[3,256,1408]{2,1,...) custom-call(bf16[64,2048]{1,0:T(8,128)(2,1)} %bitcast.10, ...), custom_call_target="tpu_custom_call" | custom-call | tf_op jit(solution)/shard_map/layer/pallas_call | solution.py:679
  214.1 0.0 copy-start
  214.1 1.6 copy-done
  215.7 0.0 copy-start.1
  215.7 1.2 copy-done.1
  216.9 0.0 copy-start.2
  216.9 1.1 copy-done.2
  218.0 0.0 copy-start.3
  218.0 1.0 copy-done.3
  219.1 0.0 copy-start.4
  219.1 0.9 copy-done.4
  220.0 0.0 copy-start.5
  220.0 4.6 %final.1 = (bf16[64,2048]{1,0:T(8,128)(2,1)}, f32[64,2048]{1,0:T(8,128)}, f32[256,512]{1,0:T(8,128)}, f32[64,256]{1,0:T(8,128)}, f32[64,256]{1,0:T(8,128)}, /*in...) custom-call(bf16[64,2048]{1,0:T(8,128)(2,1)S(1)} %copy-done.4, ...), custom_call_target="tpu_custom_call" | custom-call | tf_op jit(solution)/shard_map/final/pallas_call | solution.py:751
  224.6 0.0 copy-done.5
  224.6 0.6 fusion
Async XLA Ops:
  214.1 1.6 copy-start
  215.7 1.2 copy-start.1
  216.9 1.1 copy-start.2
  218.0 1.0 copy-start.3
  219.1 0.9 copy-start.4
  220.0 4.6 %copy-start.5 = (f32[1,512]{1,0:T(1,128)S(1)}, f32[1,512]{1,0:T(1,128)}, u32[]{:S(2)}) copy-start(f32[1,512]{1,0:T(1,128)} %get-tuple-element.37) | copy-start | bytes 6148

commit v6 on v5

--- a/solution.py
+++ b/solution.py
@@ -109,28 +109,43 @@
 
 class Gather:
     def __init__(self, links, full, rows):
-        self.k, self.full, self.rows = links, full, rows
-
-    def part(self, df=0, dh=0, half=None):
+        self.k, self.full, self.rows, self.early = links, full, rows, []
+
+    def part(self, df=0, dh=0, half=None, size=None, start=0):
         block = self.k.block(-df, -dh, self.k.core)
+        if size is not None:
+            at = pl.multiple_of(block * self.rows + start, self.rows // 4)
+            return self.full.at[pl.ds(at, size)]
         if half is None:
             return self.full.at[ds(block * self.rows, self.rows)]
         n = self.rows // 2
         return self.full.at[ds(block * self.rows + half * n, n)]
 
-    def first(self, own):
+    def first(self, own, along="fc"):
         k = self.k
         mine = self.part()
-        self.line = {}
-        for df in range(1, k.F):
-            self.line[df, 0] = k.send(own, mine, k.chip(df, 0))
-        for dh in range(1, k.H):
-            self.line[0, dh] = k.send(own, mine, k.chip(0, dh))
-        self.twin = [k.send(own, mine, k.sib)]
+        if "f" in along:
+            self.line = {}
+            for df in range(1, k.F):
+                self.line[df, 0] = k.send(own, mine, k.chip(df, 0))
+            self.twin = [k.send(own, mine, k.sib)]
+        if "c" in along:
+            for dh in range(1, k.H):
+                self.line[0, dh] = k.send(own, mine, k.chip(0, dh))
+        n = self.rows // 4
+        if "1" in along:
+            self.early = [
+                k.send(own.at[:n], self.part(0, 0, None, n, 0), k.chip(0, dh)) for dh in range(1, k.H)
+            ]
+        if "2" in along:
+            for dh in range(1, k.H):
+                self.line[0, dh] = k.send(own.at[n:], self.part(0, 0, None, 3 * n, n), k.chip(0, dh))
 
     def second(self):
         k = self.k
         self.diag = {}
+        for copy in self.early:
+            copy.wait_recv()
         for (df, dh), copy in self.line.items():
             copy.wait_recv()
             half = 0 if df else 1
@@ -158,7 +173,7 @@
             copy.wait_recv()
 
     def sent(self):
-        self.k.finish(list(self.line.values()) + list(self.diag.values()) + self.twin)
+        self.k.finish(self.early + list(self.line.values()) + list(self.diag.values()) + self.twin)
 
 
 class ZGather:
@@ -175,6 +190,7 @@
             k.start(self.copies[i][0], cond)
         self.left = list(range(1, T))
         self.relays = []
+        self.order = [2, 1, 3] if T == 4 else list(range(1, T))
 
     def relay(self):
         k = self.k
@@ -194,6 +210,17 @@
     def wait(self):
         for i in self.left:
             self.copies[i][0].wait_recv()
+
+    def arrival(self, i):
+        if self.k.T != 4:
+            self.copies[i][0].wait_recv()
+            return i
+        if i == 2:
+            return i
+        at_first = self.k.t == 0
+        pl.when(at_first)(self.copies[4 - i][0].wait_recv)
+        pl.when(jnp.logical_not(at_first))(self.copies[i][0].wait_recv)
+        return jnp.where(at_first, 4 - i, i)
 
 
 class ZScatter:
@@ -293,7 +320,7 @@
                 total = dot(x, self.y[:, a:a + n]) + self.twin[s, :, a:a + n].astype(F32)
                 self.twin[s, :, a:a + n] = total.astype(BF)
 
-        self.diag = {}
+        self.diag, self.far = {}, []
         n = 0
         for df in range(1, k.F):
             for dh in range(1, k.H):
@@ -305,6 +332,18 @@
         self.own = pltpu.make_async_copy(self.piece(0, 0), self.out.at[0], sem)
         self.own.start()
 
+    def direct(self, along, half):
+        k = self.k
+        n = self.R // 2
+        at = slice(half * n, half * n + n)
+        if along == "c":
+            for dh in range(1, k.H):
+                to = self.out.at[k.F - 1 + dh, at]
+                self.far.append(k.send(self.piece(0, dh, half), to, k.chip(0, dh)))
+        else:
+            for df in range(1, k.F):
+                self.far.append(k.send(self.piece(df, 0, half), self.out.at[df, at], k.chip(df, 0)))
+
     def add(self, df, dh, half):
         piece = self.piece(df, dh, half)
         total = piece[...].astype(F32)
@@ -314,17 +353,18 @@
                 total = total + self.relay[n, half].astype(F32)
         piece[...] = total.astype(BF)
 
-    def third(self):
-        k = self.k
-        self.far = []
-        for dh in range(1, k.H):
-            if k.F > 1:
-                self.add(0, dh, 0)
-            self.far.append(k.send(self.piece(0, dh), self.out.at[k.F - 1 + dh], k.chip(0, dh)))
-        for df in range(1, k.F):
-            if k.H > 1:
-                self.add(df, 0, 1)
-            self.far.append(k.send(self.piece(df, 0), self.out.at[df], k.chip(df, 0)))
+    def third(self, along="fc"):
+        k = self.k
+        if "f" in along:
+            for df in range(1, k.F):
+                if k.H > 1:
+                    self.add(df, 0, 1)
+            self.direct("f", 1)
+        if "c" in along:
+            for dh in range(1, k.H):
+                if k.F > 1:
+                    self.add(0, dh, 0)
+            self.direct("c", 0)
 
     def done(self):
         for copy in self.far:
@@ -336,28 +376,29 @@
     H = C // 2
     a, b, d = F - 1, H - 1, (F - 1) * (H - 1)
     gather = a + b + 1 + 2 * d + a + b + d
-    grad = F * H + 2 * d + a + b
-    return 4 * gather + 5 * grad + 2 * (F * C - 1) + 2 * (C - 1) + 9 * (T + 1)
+    grad = F * H + 2 * d + 2 * (a + b)
+    return 5 * gather + b + 5 * grad + 2 * (F * C - 1) + 2 * (C - 1) + 9 * (T + 1)
 
 
 def layer_kernel(
     sizes, hd,
-    hidden_ref, seg_ref, pad_ref, ga_ref, gm_ref, wq_ref, wk_ref, wv_ref, wo_ref, wd_ref, cot_ref,
-    wg_hbm, wu_hbm,
+    seg_ref, pad_ref, ga_ref, gm_ref,
+    hidden_hbm, wq_hbm, wk_hbm, wv_hbm, wo_hbm, wd_hbm, cot_hbm, wg_hbm, wu_hbm,
     out_ref, hid_ref, gg_ref, sum_down, sum_gate, sum_up, sum_out, sum_qkv,
-    w_v, gate_v, up_v, down_v, n1_s, n2_s, gall, gm, xt_a, xt_b, inner, g_gate, g_up,
-    q_s, attn_s, g_attn, g_qkv, lse_s, kv_s, k_s, v_s, g_kv, g_kvb, kv_slots, bias, cos_s, sin_s,
+    w_v, wo_v, gate_v, up_v, down_v, h_s, n1_s, n2_s, gall, gm, xt_a, xt_b, inner, g_gate, g_up,
+    qt_s, attn_s, g_qkv, lse_s, kv_s, k_s, v_s, kt_s, vt_s, g_kv, g_kvb, kv_slots, bias, cos_s, sin_s,
+    inv_s, gain_s,
     padc, part_b, part2_b, slots, slots2, middle_a, middle_b, mid_s,
     twin_down, twin_gate, twin_up, twin_out, twin_qkv,
     relay_down, relay_gate, relay_up, relay_out, relay_qkv,
-    gains_s, gz, gz_slots, gx, gx_slots, sends, recvs, local,
+    gains_s, gz, gz_slots, gx, gx_slots, hidden_ref, kvw_ref, wo_ref, wd_ref, cot_ref, sends, recvs, local,
 ):
     k = Links(sizes, sends, recvs)
     T, F, C, H = k.T, k.F, k.C, k.H
     rows, D = hidden_ref.shape
-    R, QW = wq_ref.shape
+    R, QW = wq_hbm.shape
     FB = wg_hbm.shape[1]
-    span, length = bias.shape[0], seg_ref.shape[1]
+    span, length = gall.shape[0], seg_ref.shape[1]
     nh = QW // hd
     QKV = QW + 2 * hd
     pair = 2 * hd
@@ -366,46 +407,52 @@
     at_c = ds(k.c * span, span)
     k.greet()
 
-    aw, gw, uw, dw = (Gather(k, full, R) for full in (w_v, gate_v, up_v, down_v))
+    aw, ow, gw, uw, dw = (Gather(k, full, R) for full in (w_v, wo_v, gate_v, up_v, down_v))
     mine = k.block(0, 0, k.core)
-    own_w = aw.part()
-    own_w[:, :QW] = wq_ref[...]
-    kv_w = jnp.concatenate([wk_ref[...], wv_ref[...]], axis=0)
-    own_w[:, QW:QKV] = kv_w.astype(F32).T.astype(BF)
-    own_w[:, QKV:] = wo_ref[...].astype(F32).T.astype(BF)
-    gains_s[mine, :, :R] = ga_ref[...].astype(F32).reshape(1, R)
-    gains_s[mine, :, R:] = gm_ref[...].astype(F32).reshape(1, R)
+    own_w, own_o = aw.part(), ow.part()
     loads = [
-        pltpu.make_async_copy(wg_hbm, gw.part(), local.at[0]),
-        pltpu.make_async_copy(wu_hbm, uw.part(), local.at[1]),
+        pltpu.make_async_copy(src, dst, local.at[n])
+        for n, (src, dst) in enumerate((
+            (wk_hbm, kvw_ref.at[:hd]), (wv_hbm, kvw_ref.at[hd:]), (wo_hbm, wo_ref),
+            (wq_hbm, own_w.at[:, :QW]), (hidden_hbm, hidden_ref), (hidden_hbm, h_s.at[at_t]),
+            (wd_hbm, wd_ref), (cot_hbm, cot_ref), (wg_hbm, gw.part()), (wu_hbm, uw.part()),
+        ))
     ]
     for copy in loads:
         copy.start()
+    gains_s[mine, :, :R] = ga_ref[...].astype(F32).reshape(1, R)
+    gains_s[mine, :, R:] = gm_ref[...].astype(F32).reshape(1, R)
+    for copy in loads[:4]:
+        copy.wait()
+    own_w[:, QW:] = kvw_ref[...].astype(F32).T.astype(BF)
+    own_o[...] = wo_ref[...].astype(F32).T.astype(BF)
     k.meet()
-    h_gather = ZGather(k, gm, rows, hidden_ref)
-    gm[at_t] = hidden_ref[...]
+    h_gather = ZGather(k, h_s, rows, hidden_hbm)
     own_gain = gains_s.at[mine]
     gain_copies = [k.send(own_gain, own_gain, dev) for dev in k.plane_peers()]
     aw.first(own_w)
+    ow.first(own_o)
 
     def gain_row(which):
         return jnp.concatenate(
             [gains_s[b][:, which * R:(which + 1) * R] for b in range(F * C)], axis=1
         )
 
+    for copy in loads[4:8]:
+        copy.wait()
     down_v[ds(mine * R, R)] = wd_ref[...].astype(F32).T.astype(BF)
 
     def column_of(row):
         return jnp.broadcast_to(row.astype(F32), (8, span)).T[:, :1]
 
     seg = seg_ref[...].astype(F32)
-    seg_col = column_of(seg_ref[:, at_c])
-    win = bias.shape[1]
+    seg_row = seg_ref[:, at_c].astype(F32)
+    seg_col = column_of(seg_row)
+    padc[...] = column_of(pad_ref[:, at_c])
+    win = k_s.shape[0]
     win_at = jnp.maximum(k.c * span + span - win, 0)
     at_w = pl.ds(pl.multiple_of(win_at, span), win)
-    padc[...] = column_of(pad_ref[:, at_c])
     row_at = k.c * span + lax.broadcasted_iota(jnp.int32, (span, 1), 0)
-    column = win_at + lax.broadcasted_iota(jnp.int32, (span, win), 1)
     first = jnp.sum(jnp.where(seg < seg_col, 1.0, 0.0), axis=1, keepdims=True)
     lane = lax.broadcasted_iota(jnp.int32, (1, pair), 1)
     frequency = jnp.exp(-((lane % (hd // 2)).astype(F32) * (2.0 / hd)) * math.log(10000.0))
@@ -413,10 +460,19 @@
     angles = (row_at.astype(F32) - first) * frequency
     cos_s[...] = jnp.cos(angles)
     sin_s[...] = jnp.where(low, -1.0, 1.0) * jnp.sin(angles)
-    allowed = (seg_ref[:, at_w].astype(F32) == seg_col) & (column <= row_at) & (
-        (pad_ref[:, at_w] == 1) | (column == row_at)
+
+    def tall_column(row):
+        return jnp.broadcast_to(row.astype(F32), (8, win)).T[:, :1]
+
+    key_at = win_at + lax.broadcasted_iota(jnp.int32, (win, span), 0)
+    token_at = k.c * span + lax.broadcasted_iota(jnp.int32, (win, span), 1)
+    allowed = (tall_column(seg_ref[:, at_w]) == seg_row) & (key_at <= token_at) & (
+        (tall_column(pad_ref[:, at_w]) == 1.0) | (key_at == token_at)
     )
-    bias[...] = jnp.where(allowed, 0.0, NEG)
+    terms = jnp.where(allowed, 0.0, NEG)
+    for b in range(T):
+        one = terms[:, b * rows:(b + 1) * rows]
+        bias[b] = jnp.concatenate([one] * (128 // rows), axis=1)
     keep = padc[at_t]
     gall[at_t] = (cot_ref[...].astype(F32) * keep).astype(BF)
 
@@ -429,9 +485,10 @@
     def turn_back(x):
         return x * cos_s[...] - swap_halves(x) * sin_s[...]
 
+    h_gather.relay()
     aw.second()
-    gw.first(wg_hbm)
-    h_gather.relay()
+    ow.second()
+    gw.first(wg_hbm, "f1")
     aw.third()
     for copy in gain_copies:
         copy.wait_recv()
@@ -441,56 +498,71 @@
     @pl.loop(0, T)
     def _(n):
         at = ds(n * rows, rows)
-        h = gm[at].astype(F32)
+        h = h_s[at].astype(F32)
         inv = lax.rsqrt(jnp.mean(h * h, axis=-1, keepdims=True) + EPS)
+        inv_s[at] = inv
         n1_s[at] = (h * inv * gain_one_row).astype(BF)
 
     g_gather = ZGather(k, gall, rows)
     aw.done()
 
-    pre = dot(n1_s[...], w_v[:, QW:QKV])
+    def down_rows(x):
+        t = x.T
+        return jnp.concatenate([t[n * hd:(n + 1) * hd] for n in range(nh)], axis=1)
+
+    def across(x):
+        t = x.T
+        return jnp.concatenate([t[n * rows:(n + 1) * rows] for n in range(nh)], axis=1)
+
+    pre = dot(n1_s[...], w_v[:, QW:])
     kv_s[at_c] = jnp.where(lane < hd, turn(pre), pre).astype(BF)
     own_kv = kv_s.at[at_c]
     kv_copies = [k.send(own_kv, own_kv, k.cpeer(i)) for i in range(1, C)]
+    gw.first(wg_hbm, "2")
+    turned = []
     for at, n in chunks(QW, 256):
         pre = dot(n1_s[...], w_v[:, at:at + n])
-        for b in range(0, n, pair):
-            q_s[:, at + b:at + b + pair] = turn(pre[:, b:b + pair]).astype(BF)
+        turned += [turn(pre[:, b:b + pair]) * scale for b in range(0, n, pair)]
+    turned = jnp.concatenate(turned, axis=1)
+    for b in range(T):
+        qt_s[b] = down_rows(turned[b * rows:(b + 1) * rows]).astype(BF)
+    ow.third()
     for copy in kv_copies:
         copy.wait_recv()
     k_s[...] = kv_s[at_w, :hd]
     v_s[...] = kv_s[at_w, hd:]
-    gw.second()
+    kvt = kv_s[at_w].astype(F32).T.astype(BF)
+    kt_s[...] = kvt[:hd]
+    vt_s[...] = kvt[hd:]
+    g_gather.relay()
+    wide = nh * rows
+    group = min(256, wide)
+
+    @pl.loop(0, T)
+    def _(b):
+        mask = jnp.concatenate([bias[b]] * (group // 128), axis=1)
+        outs = []
+        for a in range(0, wide, group):
+            scores = dot(k_s[...], qt_s[b, :, a:a + group]) + mask
+            top = jnp.max(scores, axis=0, keepdims=True)
+            weights = jnp.exp(scores - top)
+            total = jnp.sum(weights, axis=0, keepdims=True)
+            outs.append(dot(vt_s[...], (weights * (1.0 / total)).astype(BF)))
+            lse_s[b, :, a:a + group] = top + jnp.log(total)
+        attn_s[ds(b * rows, rows)] = across(jnp.concatenate(outs, axis=1)).astype(BF)
+
     uw.first(wu_hbm)
-    lse_s[...] = jnp.zeros_like(lse_s)
-
-    @pl.loop(0, nh // 2)
-    def _(n):
-        at = ds(n * pair, pair)
-        two = q_s[:, at] * BF(scale)
-        outs = []
-        for e in range(2):
-            scores = dot(two[:, e * hd:(e + 1) * hd], k_s[...], 1, 1) + bias[...]
-            top = jnp.max(scores, axis=-1, keepdims=True)
-            weights = jnp.exp(scores - top)
-            total = jnp.sum(weights, axis=-1, keepdims=True)
-            outs.append(dot((weights * (1.0 / total)).astype(BF), v_s[...]))
-            lse_s[...] = jnp.where(lane == 2 * n + e, top + jnp.log(total), lse_s[...])
-        attn_s[:, at] = jnp.concatenate(outs, axis=1).astype(BF)
-
-    g_gather.relay()
+    ow.done()
 
     @pl.loop(0, D // 256)
     def _(n):
         at = ds(n * 256, 256)
-        part_b[:, at] = dot(attn_s[...], w_v[at, QKV:], 1, 1).astype(BF)
+        part_b[:, at] = dot(attn_s[...], wo_v[at], 1, 1).astype(BF)
 
     h_gather.sent()
     one = ZScatter(k, part_b, slots, middle_a, rows)
-    gw.third()
+    gw.second()
     one.relay()
-    uw.second()
-    dw.first(dw.part())
 
     def turn_over(src, dst):
         @pl.loop(0, D // 256)
@@ -505,11 +577,14 @@
     scale_two = lax.rsqrt(jnp.mean(mid * mid, axis=-1, keepdims=True) + EPS)
     n2_s[at_t] = (mid * scale_two * gain_row(1)).astype(BF)
     n2_gather = ZGather(k, n2_s, rows)
+    uw.second()
+    dw.first(dw.part())
+    n2_gather.relay()
+    gw.third()
     uw.third()
-    n2_gather.relay()
     gw.done()
     uw.done()
-    for copy in loads:
+    for copy in loads[8:]:
         copy.wait()
     n2_gather.wait()
 
@@ -525,7 +600,9 @@
     down_g.first()
     dw.second()
     turn_over(n2_s, xt_b)
-    down_g.second(local.at[2])
+    down_g.second(local.at[10])
+    down_g.direct("f", 0)
+    down_g.direct("c", 1)
     k.finish(down_g.twins)
     dw.third()
     dw.done()
@@ -543,7 +620,7 @@
         part_b[:, at] = part.astype(BF)
 
     two = ZScatter(k, part_b, slots, middle_a, rows)
-    for weight in (aw, gw, uw, dw):
+    for weight in (aw, ow, gw, uw, dw):
         weight.sent()
 
     def spare(room, lane, width):
@@ -551,12 +628,15 @@
 
     gate_g = Grad(k, xt_b, g_gate, FB, spare(gate_v, 0, FB), twin_gate, relay_gate, sum_gate)
     up_g = Grad(k, xt_b, g_up, FB, spare(up_v, 0, FB), twin_up, relay_up, sum_up)
+    down_g.third()
     gate_g.first()
     up_g.first()
     two.relay()
-    gate_g.second(local.at[3])
-    up_g.second(local.at[4])
-    down_g.third()
+    gate_g.second(local.at[11])
+    gate_g.direct("f", 0)
+    gate_g.direct("c", 1)
+    up_g.second(local.at[12])
+    up_g.direct("f", 0)
 
     @pl.loop(0, D // 256)
     def _(n):
@@ -575,44 +655,47 @@
     hid_ref[...] = g_mid
     gm[at_t] = g_mid.astype(BF)
     gm_gather = ZGather(k, gm, rows)
+    turn_over(n1_s, xt_b)
     gate_g.third()
-    turn_over(n1_s, xt_b)
+    g_kv[...] = jnp.zeros_like(g_kv)
+
+    def attend_back(b):
+        at_b = ds(b * rows, rows)
+        mask = jnp.concatenate([bias[b]] * (group // 128), axis=1)
+        g_block = dot(gm[at_b], wo_v[...])
+        g_block = down_rows(g_block.astype(BF).astype(F32)).astype(BF)
+        g_qs, g_keys, g_values = [], [], []
+        for a in range(0, wide, group):
+            q_one, g_one = qt_s[b, :, a:a + group], g_block[:, a:a + group]
+            p = jnp.exp(dot(k_s[...], q_one) + mask - lse_s[b, :, a:a + group])
+            dp = dot(v_s[...], g_one)
+            delta = jnp.sum(p * dp, axis=0, keepdims=True)
+            d_scores = (p * (dp - delta)).astype(BF)
+            g_qs.append(dot(kt_s[...], d_scores))
+            g_keys.append(dot(d_scores, q_one, 1, 1))
+            g_values.append(dot(p.astype(BF), g_one, 1, 1))
+        g_query = across(jnp.concatenate(g_qs, axis=1)) * scale
+        cos, sin = cos_s[at_b], sin_s[at_b]
+        for n in range(0, QW, pair):
+            x = g_query[:, n:n + pair]
+            g_qkv[at_b, n:n + pair] = (x * cos - swap_halves(x) * sin).astype(BF)
+        g_kv[at_w] += jnp.concatenate([sum(g_keys), sum(g_values)], axis=1)
+
+    attend_back(k.t)
     gm_gather.relay()
-    gm_gather.wait()
     branch = ZScatter(k, part2_b, slots2, middle_b, rows)
-    for at, n in chunks(QW, 256):
-        g_attn[:, at:at + n] = dot(gm[...], w_v[:, QKV + at:QKV + at + n]).astype(BF)
-    g_kv[...] = jnp.zeros_like(g_kv)
-
-    @pl.loop(0, nh // 2)
-    def _(n):
-        at = ds(n * pair, pair)
-        two_q = q_s[:, at] * BF(scale)
-        two_g = g_attn[:, at]
-        g_qs, g_kvs = [], []
-        for e in range(2):
-            q_one, g_one = two_q[:, e * hd:(e + 1) * hd], two_g[:, e * hd:(e + 1) * hd]
-            lse = jnp.sum(jnp.where(lane == 2 * n + e, lse_s[...], 0.0), axis=1, keepdims=True)
-            p = jnp.exp(dot(q_one, k_s[...], 1, 1) + bias[...] - lse)
-            dp = dot(g_one, v_s[...], 1, 1)
-            delta = jnp.sum(p * dp, axis=-1, keepdims=True)
-            d_scores = (p * (dp - delta)).astype(BF)
-            g_qs.append(dot(d_scores, k_s[...]) * scale)
-            g_kvs.append(
-                jnp.concatenate([dot(d_scores, q_one, 0, 0), dot(p.astype(BF), g_one, 0, 0)], axis=1)
-            )
-        g_qkv[:, at] = turn_back(jnp.concatenate(g_qs, axis=1)).astype(BF)
-        g_kv[at_w] += g_kvs[0] + g_kvs[1]
-
+    for i in gm_gather.order:
+        attend_back((k.t + T - gm_gather.arrival(i)) % T)
     g_kvb[...] = g_kv[...].astype(BF)
     kv_copies = []
     for i in range(1, C):
         piece = g_kvb.at[ds(((k.c + i) % C) * span, span)]
         kv_copies.append(k.send(piece, kv_slots.at[i - 1], k.cpeer(i)))
     branch.relay()
+    up_g.direct("c", 1)
     up_g.third()
     turn_over(gm, xt_a)
-    out_g = Grad(k, xt_a, attn_s, QW, spare(w_v, QKV, QW), twin_out, relay_out, sum_out)
+    out_g = Grad(k, xt_a, attn_s, QW, spare(wo_v, 0, QW), twin_out, relay_out, sum_out)
     out_g.first()
     own_kv = g_kv[at_c]
     for i in range(1, C):
@@ -624,25 +707,28 @@
     @pl.loop(0, D // 256)
     def _(n):
         at = ds(n * 256, 256)
-        part_b[:, at] = dot(g_qkv[...], w_v[at, :QKV], 1, 1).astype(BF)
+        part = dot(g_qkv[...], w_v[at], 1, 1)
+        part_b[:, at] = part.astype(BF)
+        gain_s[:, at] = jnp.sum(part * (h_s[:, at].astype(F32) * inv_s[...]), axis=0, keepdims=True)
 
     last = ZScatter(k, part_b, slots, middle_a, rows)
-    out_g.second(local.at[5])
+    out_g.second(local.at[13])
+    out_g.direct("f", 0)
+    out_g.direct("c", 1)
     qkv_g = Grad(k, xt_b, g_qkv, QKV, spare(w_v, 0, QKV), twin_qkv, relay_qkv, sum_qkv)
     qkv_g.first()
     last.relay()
-    qkv_g.second(local.at[6])
-    out_ref[...] = (padc[at_t] * (mid_s[...] + branch.total())).astype(BF)
-    out_g.third()
-    qkv_g.third()
-    d_hid, gain_one = norm_back(last.total(), hidden_ref[...].astype(F32), gain_row(0))
-    hid_ref[...] = hid_ref[...] + d_hid
-
+    qkv_g.second(local.at[14])
+    qkv_g.direct("f", 0)
+    qkv_g.direct("c", 1)
+    gain_one = gain_s[...]
     for b in range(F * C):
         gz[b] = jnp.concatenate(
             [gain_one[:, b * R:(b + 1) * R], gain_two[:, b * R:(b + 1) * R]], axis=1
         )
     z_copies = [k.send(gz, gz_slots.at[i - 1], k.zpeer(i)) for i in range(1, T)]
+    out_ref[...] = (padc[at_t] * (mid_s[...] + branch.total())).astype(BF)
+    out_g.third()
     both = gz[...]
     for i in range(1, T):
         z_copies[i - 1].wait_recv()
@@ -651,6 +737,9 @@
     x_copies = []
     for n, dev in enumerate(k.plane_peers()):
         x_copies.append(k.send(gx.at[dev[0] * C + dev[1]], gx_slots.at[n], dev))
+    qkv_g.third()
+    d_hid, _ = norm_back(last.total(), hidden_ref[...].astype(F32), gain_one_row)
+    hid_ref[...] = hid_ref[...] + d_hid
     both = gx[mine]
     for n, copy in enumerate(x_copies):
         copy.wait_recv()
@@ -670,6 +759,7 @@
     span, length, QKV = rows * T, seg.shape[1], QW + 2 * hd
     vm = pl.BlockSpec(memory_space=pltpu.VMEM)
     hbm = pl.BlockSpec(memory_space=pl.ANY)
+    wide = QW // hd * rows
     win = min(length, span + -(-DOC // span) * span)
     n_sems = n_semaphores(F, C, T)
     S = jax.ShapeDtypeStruct
@@ -682,31 +772,33 @@
             S((rows, D), BF), S((rows, D), F32), S((1, 2 * R), F32),
             *[S((lines, R, n), BF) for n in widths],
         ),
-        in_specs=[vm] * 11 + [hbm] * 2,
+        in_specs=[vm] * 4 + [hbm] * 9,
         out_specs=[vm] * 3 + [hbm] * 5,
         scratch_shapes=[
-            V((D, QW + QKV), BF), V((D, FB), BF), V((D, FB), BF), V((D, FB), BF),
-            V((span, D), BF), V((span, D), BF), V((span, D), BF), V((span, D), BF),
+            V((D, QKV), BF), V((D, QW), BF), V((D, FB), BF), V((D, FB), BF), V((D, FB), BF),
+            V((span, D), BF), V((span, D), BF), V((span, D), BF), V((span, D), BF), V((span, D), BF),
             V((D, span), BF), V((D, span), BF),
             V((span, FB), BF), V((span, FB), BF), V((span, FB), BF),
-            V((span, QW), BF), V((span, QW), BF), V((span, QW), BF), V((span, QKV), BF),
-            V((span, 2 * hd), F32), V((length, 2 * hd), BF), V((win, hd), BF), V((win, hd), BF),
+            V((T, hd, wide), BF), V((span, QW), BF), V((span, QKV), BF), V((T, 1, wide), F32),
+            V((length, 2 * hd), BF), V((win, hd), BF), V((win, hd), BF), V((hd, win), BF), V((hd, win), BF),
             V((length, 2 * hd), F32), V((length, 2 * hd), BF), V((C - 1, span, 2 * hd), BF),
-            V((span, win), F32), V((span, 2 * hd), F32), V((span, 2 * hd), F32), V((span, 1), F32),
+            V((T, win, 128), F32), V((span, 2 * hd), F32), V((span, 2 * hd), F32),
+            V((span, 1), F32), V((1, D), F32), V((span, 1), F32),
             V((span, D), BF), V((span, D), BF), V((T - 1, rows, D), BF), V((T - 1, rows, D), BF),
             V((rows, D), BF), V((rows, D), BF), V((rows, D), F32),
             *[V((FH, R, n), BF) for n in widths],
             *[V((diag, 2, R // 2, n), BF) for n in widths],
             V((F * C, 1, 2 * R), F32), V((F * C, 1, 2 * R), F32), V((T - 1, F * C, 1, 2 * R), F32),
             V((F * C, 1, 2 * R), F32), V((F * C - 1, 1, 2 * R), F32),
+            V((rows, D), BF), V((2 * hd, R), BF), V((QW, R), BF), V((FB, R), BF), V((rows, D), BF),
             pltpu.SemaphoreType.DMA((n_sems,)), pltpu.SemaphoreType.DMA((n_sems,)),
-            pltpu.SemaphoreType.DMA((7,)),
+            pltpu.SemaphoreType.DMA((15,)),
         ],
         compiler_params=pltpu.CompilerParams(
             collective_id=0, has_side_effects=True, vmem_limit_bytes=62 * 2**20
         ),
         name="layer",
-    )(hidden, seg, pad, ga, gm, wq, wk, wv, wo, wd, cot, wg, wu)
+    )(seg, pad, ga, gm, hidden, wq, wk, wv, wo, wd, cot, wg, wu)
 
 
 def final_kernel(
@@ -757,7 +849,7 @@
         ),
         in_specs=[acts, acts] + [parts(x) for x in (s_down, s_gate, s_up, s_out, s_qkv)],
         out_specs=[acts, acts, tall(QW), wide(hd), wide(hd), wide(QW), tall(FB), tall(FB), wide(FB)],
-        compiler_params=pltpu.CompilerParams(vmem_limit_bytes=48 * 2**20),
+        compiler_params=pltpu.CompilerParams(vmem_limit_bytes=62 * 2**20),
         name="final",
     )(block_out, grad_hidden, s_down, s_gate, s_up, s_out, s_qkv)
 

time: 226 us -> 203 us (0.90)
  Pallas kernels: 218 us -> 201 us
  local copies, waits for them, and re-layouts: 6.5 us -> 0.57 us
    pallas_call x1, Pallas kernels: 213 us -> 195 us  [layer(): pl.pallas_call(functools.partial(layer_kernel, sizes, hd), out_shape=(S((...]
    unnamed x12 -> x2, local copies, waits for them, and re-layouts: 5.93 us -> 0.01 us
where the time goes in v6:
time: 203 us; the launch traced here: 202 us
  Pallas kernels  201 us (99%)
    pallas_call x1, Pallas kernels, layer(): pl.pallas_call(functools.partial(layer_kernel, sizes, hd), out_shape=(S((...  195 us
    pallas_call x1, Pallas kernels, final(): pl.pallas_call(functools.partial(final_kernel, hd), grid=(steps,), out_sh...  5.81 us

profile of v6, /device:TPU:0, one launch (start us, length us, event | category | flops | bytes accessed | tf_op | source)
XLA Modules:
  0.0 202.3 jit_solution(30516073901208301)
XLA Ops:
  0.6 195.3 %layer.1 = (bf16[64,2048]{1,0:T(8,128)(2,1)}, f32[64,2048]{1,0:T(8,128)}, f32[1,512]{1,0:T(1,128)}, bf16[3,256,1408]{2,1,0:T(8,128)(2,1)}, bf16[3,256,1408]{2,1,...) custom-call(s32[1,1024]{1,0:T(1,128)} %seg_ref.1, ...), custom_call_target="tpu_custom_call" | custom-call | tf_op jit(solution)/shard_map/layer/pallas_call | solution.py:769
  195.9 0.0 copy-start
  195.9 5.8 %final.1 = (bf16[64,2048]{1,0:T(8,128)(2,1)}, f32[64,2048]{1,0:T(8,128)}, f32[256,512]{1,0:T(8,128)}, f32[64,256]{1,0:T(8,128)}, f32[64,256]{1,0:T(8,128)}, /*in...) custom-call(bf16[64,2048]{1,0:T(8,128)(2,1)} %get-tuple-element.28.out_ref, ...), custom_call_target="tpu_custom_call" | custom-call | tf_op jit(solution)/shard_map/final/pallas_call | solution.py:843
  201.8 0.0 copy-done
  201.8 0.6 fusion
Async XLA Ops:
  195.9 5.8 %copy-start = (f32[1,512]{1,0:T(1,128)S(1)}, f32[1,512]{1,0:T(1,128)}, u32[]{:S(2)}) copy-start(f32[1,512]{1,0:T(1,128)} %get-tuple-element.37) | copy-start | bytes 6148

commit v7 on v6

--- a/solution.py
+++ b/solution.py
@@ -109,58 +109,67 @@
 
 class Gather:
     def __init__(self, links, full, rows):
-        self.k, self.full, self.rows, self.early = links, full, rows, []
-
-    def part(self, df=0, dh=0, half=None, size=None, start=0):
+        self.k, self.full, self.rows = links, full, rows
+        self.line, self.twin, self.diag, self.split = {}, [], {}, False
+
+    def part(self, df=0, dh=0, start=0, size=None):
+        n = self.rows // 4
         block = self.k.block(-df, -dh, self.k.core)
-        if size is not None:
-            at = pl.multiple_of(block * self.rows + start, self.rows // 4)
-            return self.full.at[pl.ds(at, size)]
-        if half is None:
+        if size is None:
             return self.full.at[ds(block * self.rows, self.rows)]
-        n = self.rows // 2
-        return self.full.at[ds(block * self.rows + half * n, n)]
-
-    def first(self, own, along="fc"):
-        k = self.k
-        mine = self.part()
-        if "f" in along:
-            self.line = {}
-            for df in range(1, k.F):
-                self.line[df, 0] = k.send(own, mine, k.chip(df, 0))
-            self.twin = [k.send(own, mine, k.sib)]
-        if "c" in along:
-            for dh in range(1, k.H):
-                self.line[0, dh] = k.send(own, mine, k.chip(0, dh))
-        n = self.rows // 4
-        if "1" in along:
-            self.early = [
-                k.send(own.at[:n], self.part(0, 0, None, n, 0), k.chip(0, dh)) for dh in range(1, k.H)
-            ]
-        if "2" in along:
-            for dh in range(1, k.H):
-                self.line[0, dh] = k.send(own.at[n:], self.part(0, 0, None, 3 * n, n), k.chip(0, dh))
+        return self.full.at[pl.ds(pl.multiple_of(block * self.rows + start * n, n), size * n)]
+
+    def some(self, own, along, start, size):
+        k, n = self.k, self.rows // 4
+        src, to = own.at[start * n:(start + size) * n], self.part(0, 0, start, size)
+        for df in range(1, k.F) if "f" in along else ():
+            self.line.setdefault((df, 0), []).append(k.send(src, to, k.chip(df, 0)))
+        for dh in range(1, k.H) if "c" in along else ():
+            self.line.setdefault((0, dh), []).append(k.send(src, to, k.chip(0, dh)))
+
+    def sibling(self, own):
+        self.twin.append(self.k.send(own, self.part(), self.k.sib))
+
+    def first(self, own):
+        self.some(own, "fc", 0, 4)
+        self.sibling(own)
+
+    def first_split(self, own):
+        self.split = True
+        self.some(own, "f", 0, 2)
+        self.some(own, "c", 2, 2)
+        self.some(own, "f", 2, 2)
+        self.some(own, "c", 0, 2)
+        self.sibling(own)
 
     def second(self):
         k = self.k
-        self.diag = {}
-        for copy in self.early:
-            copy.wait_recv()
-        for (df, dh), copy in self.line.items():
-            copy.wait_recv()
+        for df, dh in sorted(self.line, reverse=True):
+            copies = self.line[df, dh]
+            for copy in copies[:1] if self.split else copies:
+                copy.wait_recv()
             half = 0 if df else 1
-            piece = self.part(df, dh, half)
+            piece = self.part(df, dh, 2 * half, 2)
             if df:
                 for eh in range(1, k.H):
                     self.diag[df, eh, half] = k.send(piece, piece, k.chip(0, eh))
             else:
                 for ef in range(1, k.F):
                     self.diag[ef, dh, half] = k.send(piece, piece, k.chip(ef, 0))
+        if not self.split:
+            self.pass_on()
+
+    def pass_on(self):
+        for df, dh in sorted(self.line, reverse=True):
+            for copy in self.line[df, dh][1:] if self.split else ():
+                copy.wait_recv()
             whole = self.part(df, dh)
-            self.twin.append(k.send(whole, whole, k.sib))
+            self.twin.append(self.k.send(whole, whole, self.k.sib))
 
     def third(self):
         k = self.k
+        if self.split:
+            self.pass_on()
         for copy in self.diag.values():
             copy.wait_recv()
         for df in range(1, k.F):
@@ -173,7 +182,8 @@
             copy.wait_recv()
 
     def sent(self):
-        self.k.finish(self.early + list(self.line.values()) + list(self.diag.values()) + self.twin)
+        lines = [copy for copies in self.line.values() for copy in copies]
+        self.k.finish(lines + list(self.diag.values()) + self.twin)
 
 
 class ZGather:
@@ -329,8 +339,10 @@
                         self.piece(df, dh, half), self.relay.at[n, half], dev
                     )
                 n += 1
-        self.own = pltpu.make_async_copy(self.piece(0, 0), self.out.at[0], sem)
-        self.own.start()
+        self.own = None
+        if sem is not None:
+            self.own = pltpu.make_async_copy(self.piece(0, 0), self.out.at[0], sem)
+            self.own.start()
 
     def direct(self, along, half):
         k = self.k
@@ -369,7 +381,37 @@
     def done(self):
         for copy in self.far:
             copy.wait_recv()
-        self.own.wait()
+        if self.own is not None:
+            self.own.wait()
+
+    def collect(self, room, sems):
+        self.done()
+        lines = self.k.F + self.k.H - 1
+        first = self.k.F * self.k.H * self.R
+        self.room, self.first_row = room, first
+        self.loads = [
+            pltpu.make_async_copy(
+                self.out.at[n], room.at[first + (n - 1) * self.R:first + n * self.R], sems.at[n - 1]
+            )
+            for n in range(1, lines)
+        ]
+        for copy in self.loads:
+            copy.start()
+
+    def add_up(self, result, sem):
+        for copy in self.loads:
+            copy.wait()
+        step = min(self.R, 64)
+
+        @pl.loop(0, self.R // step)
+        def _(n):
+            total = self.twin[0, ds(n * step, step)].astype(F32)
+            for i in range(len(self.loads)):
+                total = total + self.room[ds(self.first_row + i * self.R + n * step, step)].astype(F32)
+            self.twin[0, ds(n * step, step)] = total.astype(BF)
+
+        self.own = pltpu.make_async_copy(self.twin.at[0], result, sem)
+        self.own.start()
 
 
 def n_semaphores(F, C, T):
@@ -377,21 +419,21 @@
     a, b, d = F - 1, H - 1, (F - 1) * (H - 1)
     gather = a + b + 1 + 2 * d + a + b + d
     grad = F * H + 2 * d + 2 * (a + b)
-    return 5 * gather + b + 5 * grad + 2 * (F * C - 1) + 2 * (C - 1) + 9 * (T + 1)
+    return 5 * gather + 4 * (a + b) + 5 * grad + 2 * (F * C - 1) + 2 * (C - 1) + 9 * (T + 1)
 
 
 def layer_kernel(
     sizes, hd,
     seg_ref, pad_ref, ga_ref, gm_ref,
     hidden_hbm, wq_hbm, wk_hbm, wv_hbm, wo_hbm, wd_hbm, cot_hbm, wg_hbm, wu_hbm,
-    out_ref, hid_ref, gg_ref, sum_down, sum_gate, sum_up, sum_out, sum_qkv,
+    out_ref, hid_ref, gg_ref, sum_down, sum_gate, sum_up, sum_out, sum_qkv, all_down, all_gate, all_up,
     w_v, wo_v, gate_v, up_v, down_v, h_s, n1_s, n2_s, gall, gm, xt_a, xt_b, inner, g_gate, g_up,
     qt_s, attn_s, g_qkv, lse_s, kv_s, k_s, v_s, kt_s, vt_s, g_kv, g_kvb, kv_slots, bias, cos_s, sin_s,
     inv_s, gain_s,
     padc, part_b, part2_b, slots, slots2, middle_a, middle_b, mid_s,
     twin_down, twin_gate, twin_up, twin_out, twin_qkv,
     relay_down, relay_gate, relay_up, relay_out, relay_qkv,
-    gains_s, gz, gz_slots, gx, gx_slots, hidden_ref, kvw_ref, wo_ref, wd_ref, cot_ref, sends, recvs, local,
+    gains_s, gz, gz_slots, gx, gx_slots, hidden_ref, kvw_ref, wo_ref, wd_ref, cot_ref, sends, recvs, local, many,
 ):
     k = Links(sizes, sends, recvs)
     T, F, C, H = k.T, k.F, k.C, k.H
@@ -405,6 +447,9 @@
     scale = hd ** (-0.5)
     at_t = ds(k.t * rows, rows)
     at_c = ds(k.c * span, span)
+    back = k_s.shape[0] // span - 1
+    kv_s[...] = jnp.zeros_like(kv_s)
+    kv_slots[...] = jnp.zeros_like(kv_slots)
     k.greet()
 
     aw, ow, gw, uw, dw = (Gather(k, full, R) for full in (w_v, wo_v, gate_v, up_v, down_v))
@@ -488,7 +533,9 @@
     h_gather.relay()
     aw.second()
     ow.second()
-    gw.first(wg_hbm, "f1")
+    gw.some(wg_hbm, "f", 0, 4)
+    gw.some(wg_hbm, "c", 0, 1)
+    gw.sibling(wg_hbm)
     aw.third()
     for copy in gain_copies:
         copy.wait_recv()
@@ -517,8 +564,11 @@
     pre = dot(n1_s[...], w_v[:, QW:])
     kv_s[at_c] = jnp.where(lane < hd, turn(pre), pre).astype(BF)
     own_kv = kv_s.at[at_c]
-    kv_copies = [k.send(own_kv, own_kv, k.cpeer(i)) for i in range(1, C)]
-    gw.first(wg_hbm, "2")
+    kv_copies = {}
+    for i in range(1, back + 1):
+        kv_copies[i], _ = k.new(own_kv, own_kv, k.cpeer(i))
+        k.start(kv_copies[i], k.c + i < C)
+    gw.some(wg_hbm, "c", 1, 3)
     turned = []
     for at, n in chunks(QW, 256):
         pre = dot(n1_s[...], w_v[:, at:at + n])
@@ -527,8 +577,8 @@
     for b in range(T):
         qt_s[b] = down_rows(turned[b * rows:(b + 1) * rows]).astype(BF)
     ow.third()
-    for copy in kv_copies:
-        copy.wait_recv()
+    for i, copy in kv_copies.items():
+        pl.when(k.c >= i)(copy.wait_recv)
     k_s[...] = kv_s[at_w, :hd]
     v_s[...] = kv_s[at_w, hd:]
     kvt = kv_s[at_w].astype(F32).T.astype(BF)
@@ -578,7 +628,7 @@
     n2_s[at_t] = (mid * scale_two * gain_row(1)).astype(BF)
     n2_gather = ZGather(k, n2_s, rows)
     uw.second()
-    dw.first(dw.part())
+    dw.first_split(dw.part())
     n2_gather.relay()
     gw.third()
     uw.third()
@@ -600,7 +650,7 @@
     down_g.first()
     dw.second()
     turn_over(n2_s, xt_b)
-    down_g.second(local.at[10])
+    down_g.second(None)
     down_g.direct("f", 0)
     down_g.direct("c", 1)
     k.finish(down_g.twins)
@@ -632,10 +682,10 @@
     gate_g.first()
     up_g.first()
     two.relay()
-    gate_g.second(local.at[11])
+    gate_g.second(None)
     gate_g.direct("f", 0)
     gate_g.direct("c", 1)
-    up_g.second(local.at[12])
+    up_g.second(None)
     up_g.direct("f", 0)
 
     @pl.loop(0, D // 256)
@@ -687,10 +737,11 @@
     for i in gm_gather.order:
         attend_back((k.t + T - gm_gather.arrival(i)) % T)
     g_kvb[...] = g_kv[...].astype(BF)
-    kv_copies = []
-    for i in range(1, C):
-        piece = g_kvb.at[ds(((k.c + i) % C) * span, span)]
-        kv_copies.append(k.send(piece, kv_slots.at[i - 1], k.cpeer(i)))
+    kv_copies = {}
+    for i in range(1, back + 1):
+        piece = g_kvb.at[ds(((k.c + C - i) % C) * span, span)]
+        kv_copies[i], _ = k.new(piece, kv_slots.at[i - 1], k.cpeer(C - i))
+        k.start(kv_copies[i], k.c >= i)
     branch.relay()
     up_g.direct("c", 1)
     up_g.third()
@@ -698,8 +749,8 @@
     out_g = Grad(k, xt_a, attn_s, QW, spare(wo_v, 0, QW), twin_out, relay_out, sum_out)
     out_g.first()
     own_kv = g_kv[at_c]
-    for i in range(1, C):
-        kv_copies[i - 1].wait_recv()
+    for i, copy in kv_copies.items():
+        pl.when(k.c + i < C)(copy.wait_recv)
         own_kv = own_kv + kv_slots[i - 1].astype(F32)
     g_qkv[:, QW:] = jnp.where(lane < hd, turn_back(own_kv), own_kv).astype(BF)
     k.finish([two.far] * two.line + list(two.copies.values()))
@@ -711,22 +762,22 @@
         part_b[:, at] = part.astype(BF)
         gain_s[:, at] = jnp.sum(part * (h_s[:, at].astype(F32) * inv_s[...]), axis=0, keepdims=True)
 
-    last = ZScatter(k, part_b, slots, middle_a, rows)
-    out_g.second(local.at[13])
-    out_g.direct("f", 0)
-    out_g.direct("c", 1)
-    qkv_g = Grad(k, xt_b, g_qkv, QKV, spare(w_v, 0, QKV), twin_qkv, relay_qkv, sum_qkv)
-    qkv_g.first()
-    last.relay()
-    qkv_g.second(local.at[14])
-    qkv_g.direct("f", 0)
-    qkv_g.direct("c", 1)
     gain_one = gain_s[...]
     for b in range(F * C):
         gz[b] = jnp.concatenate(
             [gain_one[:, b * R:(b + 1) * R], gain_two[:, b * R:(b + 1) * R]], axis=1
         )
     z_copies = [k.send(gz, gz_slots.at[i - 1], k.zpeer(i)) for i in range(1, T)]
+    last = ZScatter(k, part_b, slots, middle_a, rows)
+    qkv_g = Grad(k, xt_b, g_qkv, QKV, spare(w_v, 0, QKV), twin_qkv, relay_qkv, sum_qkv)
+    qkv_g.first()
+    out_g.second(local.at[13])
+    out_g.direct("f", 0)
+    out_g.direct("c", 1)
+    qkv_g.second(local.at[14])
+    qkv_g.direct("f", 0)
+    qkv_g.direct("c", 1)
+    last.relay()
     out_ref[...] = (padc[at_t] * (mid_s[...] + branch.total())).astype(BF)
     out_g.third()
     both = gz[...]
@@ -738,6 +789,11 @@
     for n, dev in enumerate(k.plane_peers()):
         x_copies.append(k.send(gx.at[dev[0] * C + dev[1]], gx_slots.at[n], dev))
     qkv_g.third()
+    adding = ((down_g, down_v, all_down), (gate_g, gate_v, all_gate), (up_g, up_v, all_up))
+    for n, (grad, room, _) in enumerate(adding):
+        grad.collect(room, many.at[n])
+    for n, (grad, _, result) in enumerate(adding):
+        grad.add_up(result, local.at[10 + n])
     d_hid, _ = norm_back(last.total(), hidden_ref[...].astype(F32), gain_one_row)
     hid_ref[...] = hid_ref[...] + d_hid
     both = gx[mine]
@@ -745,8 +801,10 @@
         copy.wait_recv()
         both = both + gx_slots[n]
     gg_ref[...] = both
-    for grad in (down_g, gate_g, up_g, out_g, qkv_g):
+    for grad in (out_g, qkv_g):
         grad.done()
+    for grad, _, _ in adding:
+        grad.own.wait()
     k.finish()
 
 
@@ -770,10 +828,10 @@
         functools.partial(layer_kernel, sizes, hd),
         out_shape=(
             S((rows, D), BF), S((rows, D), F32), S((1, 2 * R), F32),
-            *[S((lines, R, n), BF) for n in widths],
+            *[S((lines, R, n), BF) for n in widths], *[S((R, FB), BF)] * 3,
         ),
         in_specs=[vm] * 4 + [hbm] * 9,
-        out_specs=[vm] * 3 + [hbm] * 5,
+        out_specs=[vm] * 3 + [hbm] * 8,
         scratch_shapes=[
             V((D, QKV), BF), V((D, QW), BF), V((D, FB), BF), V((D, FB), BF), V((D, FB), BF),
             V((span, D), BF), V((span, D), BF), V((span, D), BF), V((span, D), BF), V((span, D), BF),
@@ -781,7 +839,7 @@
             V((span, FB), BF), V((span, FB), BF), V((span, FB), BF),
             V((T, hd, wide), BF), V((span, QW), BF), V((span, QKV), BF), V((T, 1, wide), F32),
             V((length, 2 * hd), BF), V((win, hd), BF), V((win, hd), BF), V((hd, win), BF), V((hd, win), BF),
-            V((length, 2 * hd), F32), V((length, 2 * hd), BF), V((C - 1, span, 2 * hd), BF),
+            V((length, 2 * hd), F32), V((length, 2 * hd), BF), V((win // span - 1, span, 2 * hd), BF),
             V((T, win, 128), F32), V((span, 2 * hd), F32), V((span, 2 * hd), F32),
             V((span, 1), F32), V((1, D), F32), V((span, 1), F32),
             V((span, D), BF), V((span, D), BF), V((T - 1, rows, D), BF), V((T - 1, rows, D), BF),
@@ -792,7 +850,7 @@
             V((F * C, 1, 2 * R), F32), V((F * C - 1, 1, 2 * R), F32),
             V((rows, D), BF), V((2 * hd, R), BF), V((QW, R), BF), V((FB, R), BF), V((rows, D), BF),
             pltpu.SemaphoreType.DMA((n_sems,)), pltpu.SemaphoreType.DMA((n_sems,)),
-            pltpu.SemaphoreType.DMA((15,)),
+            pltpu.SemaphoreType.DMA((15,)), pltpu.SemaphoreType.DMA((3, lines - 1)),
         ],
         compiler_params=pltpu.CompilerParams(
             collective_id=0, has_side_effects=True, vmem_limit_bytes=62 * 2**20
@@ -802,29 +860,31 @@
 
 
 def final_kernel(
-    hd, out_ref, hid_ref, down_ref, gate_ref, up_ref, wo_ref, qkv_ref,
-    block_out, grad_hidden, g_query, g_key, g_value, g_out, g_gate, g_up, g_down,
+    hd, out_ref, hid_ref, gg_ref, down_ref, gate_ref, up_ref, wo_ref, qkv_ref,
+    block_out, grad_hidden, gain_one, gain_two, g_query, g_key, g_value, g_out, g_gate, g_up, g_down,
 ):
     def total(ref):
         return sum(ref[i].astype(F32) for i in range(ref.shape[0]))
 
-    QW = g_query.shape[1]
+    QW, R = g_query.shape[1], gain_one.shape[0]
     block_out[...] = out_ref[...]
     grad_hidden[...] = hid_ref[...]
+    gain_one[...] = gg_ref[:, :R].reshape(R)
+    gain_two[...] = gg_ref[:, R:].reshape(R)
     qkv = total(qkv_ref)
     g_query[...] = qkv[:, :QW]
     kv = qkv[:, QW:].T
     g_key[...] = kv[:hd]
     g_value[...] = kv[hd:]
     g_out[...] = total(wo_ref).T
-    g_gate[...] = total(gate_ref)
-    g_up[...] = total(up_ref)
-    g_down[...] = total(down_ref).T
-
-
-def final(hd, block_out, grad_hidden, s_down, s_gate, s_up, s_out, s_qkv):
-    L, R, FB = s_gate.shape
-    QW = s_out.shape[2]
+    g_gate[...] = gate_ref[...].astype(F32)
+    g_up[...] = up_ref[...].astype(F32)
+    g_down[...] = down_ref[...].astype(F32).T
+
+
+def final(hd, block_out, grad_hidden, gg, s_out, s_qkv, down, gate, up):
+    L, R, QW = s_out.shape
+    FB = gate.shape[1]
     rows, D = block_out.shape
     steps = R // 128 if R % 128 == 0 else 1
     r = R // steps
@@ -840,33 +900,36 @@
         return pl.BlockSpec((n, r), lambda i: (0, i))
 
     acts = pl.BlockSpec((rows // steps, D), lambda i: (i, 0))
+    gain = pl.BlockSpec((R,), lambda i: (0,))
     return pl.pallas_call(
         functools.partial(final_kernel, hd),
         grid=(steps,),
         out_shape=(
-            S((rows, D), BF), S((rows, D), F32), S((R, QW), F32), S((hd, R), F32), S((hd, R), F32),
-            S((QW, R), F32), S((R, FB), F32), S((R, FB), F32), S((FB, R), F32),
+            S((rows, D), BF), S((rows, D), F32), S((R,), F32), S((R,), F32), S((R, QW), F32),
+            S((hd, R), F32), S((hd, R), F32), S((QW, R), F32), S((R, FB), F32), S((R, FB), F32),
+            S((FB, R), F32),
         ),
-        in_specs=[acts, acts] + [parts(x) for x in (s_down, s_gate, s_up, s_out, s_qkv)],
-        out_specs=[acts, acts, tall(QW), wide(hd), wide(hd), wide(QW), tall(FB), tall(FB), wide(FB)],
+        in_specs=[acts, acts, pl.BlockSpec((1, 2 * R), lambda i: (0, 0))]
+        + [tall(FB)] * 3 + [parts(s_out), parts(s_qkv)],
+        out_specs=[acts, acts, gain, gain, tall(QW), wide(hd), wide(hd), wide(QW), tall(FB), tall(FB),
+                   wide(FB)],
         compiler_params=pltpu.CompilerParams(vmem_limit_bytes=62 * 2**20),
         name="final",
-    )(block_out, grad_hidden, s_down, s_gate, s_up, s_out, s_qkv)
+    )(block_out, grad_hidden, gg, down, gate, up, s_out, s_qkv)
 
 
 def body(hidden_in, segment_ids, pad_mask, attn_gain, w_query, w_key, w_value, w_out,
          mlp_gain, w_gate, w_up, w_down, cotangent):
     sizes = tuple(lax.axis_size(n) for n in ("fsdp", "context", "tensor"))
-    hd, R = w_key.shape[1], w_query.shape[0]
-    block_out, grad_hidden, gg, *parts = layer(
+    hd = w_key.shape[1]
+    block_out, grad_hidden, gg, _, _, _, s_out, s_qkv, down, gate, up = layer(
         sizes, hd, hidden_in[0], segment_ids, pad_mask, attn_gain, mlp_gain,
         w_query, w_key.T, w_value.T, w_out, w_down, cotangent[0], w_gate, w_up,
     )
-    block_out, grad_hidden, g_query, g_key, g_value, g_out, g_gate, g_up, g_down = final(
-        hd, block_out, grad_hidden, *parts
-    )
+    (block_out, grad_hidden, gain_one, gain_two, g_query, g_key, g_value, g_out, g_gate, g_up,
+     g_down) = final(hd, block_out, grad_hidden, gg, s_out, s_qkv, down, gate, up)
     return (
-        block_out[None], grad_hidden[None], gg[0, :R], g_query, g_key.T, g_value.T, g_out, gg[0, R:],
+        block_out[None], grad_hidden[None], gain_one, g_query, g_key.T, g_value.T, g_out, gain_two,
         g_gate, g_up, g_down,
     )
 

time: 203 us -> 200 us (0.985)
  no operation moved by 1% of the time
where the time goes in v7:
time: 200 us
  Pallas kernels  199 us (100%)
    pallas_call x1, Pallas kernels, layer(): pl.pallas_call(functools.partial(layer_kernel, sizes, hd), out_shape=(S((...  195 us
    pallas_call x1, Pallas kernels, final(): pl.pallas_call(functools.partial(final_kernel, hd), grid=(steps,), out_sh...  4.53 us

profile of v7, /device:TPU:0, one launch (start us, length us, event | category | flops | bytes accessed | tf_op | source)
XLA Modules:
  0.0 200.1 jit_solution(13022430795067051398)
XLA Ops:
  0.6 194.8 %layer.1 = (bf16[64,2048]{1,0:T(8,128)(2,1)}, f32[64,2048]{1,0:T(8,128)}, f32[1,512]{1,0:T(1,128)}, bf16[3,256,1408]{2,1,0:T(8,128)(2,1)}, bf16[3,256,1408]{2,1,...) custom-call(s32[1,1024]{1,0:T(1,128)} %seg_ref.1, ...), custom_call_target="tpu_custom_call" | custom-call | tf_op jit(solution)/shard_map/layer/pallas_call | solution.py:827
  195.4 4.5 %final.1 = (bf16[64,2048]{1,0:T(8,128)(2,1)}, f32[64,2048]{1,0:T(8,128)}, f32[256]{0:T(256)}, f32[256]{0:T(256)}, f32[256,512]{1,0:T(8,128)}, /*index=5*/f32[64,...) custom-call(bf16[64,2048]{1,0:T(8,128)(2,1)} %get-tuple-element.30.o, ...), custom_call_target="tpu_custom_call" | custom-call | tf_op jit(solution)/shard_map/final/pallas_call | solution.py:904

commit v8 on v7

--- a/solution.py
+++ b/solution.py
@@ -424,7 +424,7 @@
 
 def layer_kernel(
     sizes, hd,
-    seg_ref, pad_ref, ga_ref, gm_ref,
+    seg_hbm, pad_hbm, ga_hbm, gm_hbm,
     hidden_hbm, wq_hbm, wk_hbm, wv_hbm, wo_hbm, wd_hbm, cot_hbm, wg_hbm, wu_hbm,
     out_ref, hid_ref, gg_ref, sum_down, sum_gate, sum_up, sum_out, sum_qkv, all_down, all_gate, all_up,
     w_v, wo_v, gate_v, up_v, down_v, h_s, n1_s, n2_s, gall, gm, xt_a, xt_b, inner, g_gate, g_up,
@@ -433,14 +433,14 @@
     padc, part_b, part2_b, slots, slots2, middle_a, middle_b, mid_s,
     twin_down, twin_gate, twin_up, twin_out, twin_qkv,
     relay_down, relay_gate, relay_up, relay_out, relay_qkv,
-    gains_s, gz, gz_slots, gx, gx_slots, hidden_ref, kvw_ref, wo_ref, wd_ref, cot_ref, sends, recvs, local, many,
+    gains_s, gz, gz_slots, gx, gx_slots, hidden_ref, kvw_ref, wo_ref, wd_ref, cot_ref, seg_ref, pad_ref, ga_ref, gm_ref, sends, recvs, local, many,
 ):
     k = Links(sizes, sends, recvs)
     T, F, C, H = k.T, k.F, k.C, k.H
     rows, D = hidden_ref.shape
     R, QW = wq_hbm.shape
     FB = wg_hbm.shape[1]
-    span, length = gall.shape[0], seg_ref.shape[1]
+    span, length = gall.shape[0], seg_hbm.shape[1]
     nh = QW // hd
     QKV = QW + 2 * hd
     pair = 2 * hd
@@ -460,11 +460,14 @@
         for n, (src, dst) in enumerate((
             (wk_hbm, kvw_ref.at[:hd]), (wv_hbm, kvw_ref.at[hd:]), (wo_hbm, wo_ref),
             (wq_hbm, own_w.at[:, :QW]), (hidden_hbm, hidden_ref), (hidden_hbm, h_s.at[at_t]),
-            (wd_hbm, wd_ref), (cot_hbm, cot_ref), (wg_hbm, gw.part()), (wu_hbm, uw.part()),
+            (wd_hbm, wd_ref), (cot_hbm, cot_ref), (seg_hbm, seg_ref), (pad_hbm, pad_ref),
+            (ga_hbm, ga_ref), (gm_hbm, gm_ref), (wg_hbm, gw.part()), (wu_hbm, uw.part()),
         ))
     ]
     for copy in loads:
         copy.start()
+    for copy in loads[10:12]:
+        copy.wait()
     gains_s[mine, :, :R] = ga_ref[...].astype(F32).reshape(1, R)
     gains_s[mine, :, R:] = gm_ref[...].astype(F32).reshape(1, R)
     for copy in loads[:4]:
@@ -483,7 +486,7 @@
             [gains_s[b][:, which * R:(which + 1) * R] for b in range(F * C)], axis=1
         )
 
-    for copy in loads[4:8]:
+    for copy in loads[4:10]:
         copy.wait()
     down_v[ds(mine * R, R)] = wd_ref[...].astype(F32).T.astype(BF)
 
@@ -534,7 +537,7 @@
     aw.second()
     ow.second()
     gw.some(wg_hbm, "f", 0, 4)
-    gw.some(wg_hbm, "c", 0, 1)
+    gw.some(wg_hbm, "c", 0, 2)
     gw.sibling(wg_hbm)
     aw.third()
     for copy in gain_copies:
@@ -568,7 +571,7 @@
     for i in range(1, back + 1):
         kv_copies[i], _ = k.new(own_kv, own_kv, k.cpeer(i))
         k.start(kv_copies[i], k.c + i < C)
-    gw.some(wg_hbm, "c", 1, 3)
+    gw.some(wg_hbm, "c", 2, 2)
     turned = []
     for at, n in chunks(QW, 256):
         pre = dot(n1_s[...], w_v[:, at:at + n])
@@ -584,6 +587,7 @@
     kvt = kv_s[at_w].astype(F32).T.astype(BF)
     kt_s[...] = kvt[:hd]
     vt_s[...] = kvt[hd:]
+    uw.first(wu_hbm)
     g_gather.relay()
     wide = nh * rows
     group = min(256, wide)
@@ -601,7 +605,6 @@
             lse_s[b, :, a:a + group] = top + jnp.log(total)
         attn_s[ds(b * rows, rows)] = across(jnp.concatenate(outs, axis=1)).astype(BF)
 
-    uw.first(wu_hbm)
     ow.done()
 
     @pl.loop(0, D // 256)
@@ -622,19 +625,19 @@
 
     g_gather.wait()
     turn_over(gall, xt_a)
+    uw.second()
+    dw.first_split(dw.part())
     mid = hidden_ref[...].astype(F32) + one.total()
     mid_s[...] = mid
     scale_two = lax.rsqrt(jnp.mean(mid * mid, axis=-1, keepdims=True) + EPS)
     n2_s[at_t] = (mid * scale_two * gain_row(1)).astype(BF)
     n2_gather = ZGather(k, n2_s, rows)
-    uw.second()
-    dw.first_split(dw.part())
     n2_gather.relay()
     gw.third()
     uw.third()
     gw.done()
     uw.done()
-    for copy in loads[8:]:
+    for copy in loads[12:]:
         copy.wait()
     n2_gather.wait()
 
@@ -771,10 +774,10 @@
     last = ZScatter(k, part_b, slots, middle_a, rows)
     qkv_g = Grad(k, xt_b, g_qkv, QKV, spare(w_v, 0, QKV), twin_qkv, relay_qkv, sum_qkv)
     qkv_g.first()
-    out_g.second(local.at[13])
+    out_g.second(local.at[17])
     out_g.direct("f", 0)
     out_g.direct("c", 1)
-    qkv_g.second(local.at[14])
+    qkv_g.second(local.at[18])
     qkv_g.direct("f", 0)
     qkv_g.direct("c", 1)
     last.relay()
@@ -793,7 +796,7 @@
     for n, (grad, room, _) in enumerate(adding):
         grad.collect(room, many.at[n])
     for n, (grad, _, result) in enumerate(adding):
-        grad.add_up(result, local.at[10 + n])
+        grad.add_up(result, local.at[14 + n])
     d_hid, _ = norm_back(last.total(), hidden_ref[...].astype(F32), gain_one_row)
     hid_ref[...] = hid_ref[...] + d_hid
     both = gx[mine]
@@ -830,7 +833,7 @@
             S((rows, D), BF), S((rows, D), F32), S((1, 2 * R), F32),
             *[S((lines, R, n), BF) for n in widths], *[S((R, FB), BF)] * 3,
         ),
-        in_specs=[vm] * 4 + [hbm] * 9,
+        in_specs=[hbm] * 13,
         out_specs=[vm] * 3 + [hbm] * 8,
         scratch_shapes=[
             V((D, QKV), BF), V((D, QW), BF), V((D, FB), BF), V((D, FB), BF), V((D, FB), BF),
@@ -849,8 +852,9 @@
             V((F * C, 1, 2 * R), F32), V((F * C, 1, 2 * R), F32), V((T - 1, F * C, 1, 2 * R), F32),
             V((F * C, 1, 2 * R), F32), V((F * C - 1, 1, 2 * R), F32),
             V((rows, D), BF), V((2 * hd, R), BF), V((QW, R), BF), V((FB, R), BF), V((rows, D), BF),
+            V((1, length), jnp.int32), V((1, length), jnp.int32), V((R,), BF), V((R,), BF),
             pltpu.SemaphoreType.DMA((n_sems,)), pltpu.SemaphoreType.DMA((n_sems,)),
-            pltpu.SemaphoreType.DMA((15,)), pltpu.SemaphoreType.DMA((3, lines - 1)),
+            pltpu.SemaphoreType.DMA((19,)), pltpu.SemaphoreType.DMA((3, lines - 1)),
         ],
         compiler_params=pltpu.CompilerParams(
             collective_id=0, has_side_effects=True, vmem_limit_bytes=62 * 2**20

time: 200 us -> 196 us (0.980)
  Pallas kernels: 199 us -> 195 us
    pallas_call x1, Pallas kernels: 195 us -> 191 us  [layer(): pl.pallas_call(functools.partial(layer_kernel, sizes, hd), out_shape=(S((...]
where the time goes in v8:
time: 196 us
  Pallas kernels  195 us (99%)
    pallas_call x1, Pallas kernels, layer(): pl.pallas_call(functools.partial(layer_kernel, sizes, hd), out_shape=(S((...  191 us
    pallas_call x1, Pallas kernels, final(): pl.pallas_call(functools.partial(final_kernel, hd), grid=(steps,), out_sh...  4.53 us

profile of v8, /device:TPU:0, one launch (start us, length us, event | category | flops | bytes accessed | tf_op | source)
XLA Modules:
  0.0 196.3 jit_solution(2181642337285753073)
XLA Ops:
  0.6 190.9 %layer.1 = (bf16[64,2048]{1,0:T(8,128)(2,1)}, f32[64,2048]{1,0:T(8,128)}, f32[1,512]{1,0:T(1,128)}, bf16[3,256,1408]{2,1,0:T(8,128)(2,1)}, bf16[3,256,1408]{2,1,...) custom-call(s32[1,1024]{1,0:T(1,128)} %seg_hbm.1, ...), custom_call_target="tpu_custom_call" | custom-call | tf_op jit(solution)/shard_map/layer/pallas_call | solution.py:830
  191.6 4.5 %final.1 = (bf16[64,2048]{1,0:T(8,128)(2,1)}, f32[64,2048]{1,0:T(8,128)}, f32[256]{0:T(256)}, f32[256]{0:T(256)}, f32[256,512]{1,0:T(8,128)}, /*index=5*/f32[64,...) custom-call(bf16[64,2048]{1,0:T(8,128)(2,1)} %get-tuple-element.30.o, ...), custom_call_target="tpu_custom_call" | custom-call | tf_op jit(solution)/shard_map/final/pallas_call | solution.py:908

commit v9 on v8

--- a/solution.py
+++ b/solution.py
@@ -126,6 +126,14 @@
             self.line.setdefault((df, 0), []).append(k.send(src, to, k.chip(df, 0)))
         for dh in range(1, k.H) if "c" in along else ():
             self.line.setdefault((0, dh), []).append(k.send(src, to, k.chip(0, dh)))
+
+    def lanes(self, own, lanes):
+        k = self.k
+        to = self.part().at[:, lanes]
+        for df in range(1, k.F):
+            self.line.setdefault((df, 0), []).append(k.send(own, to, k.chip(df, 0)))
+        for dh in range(1, k.H):
+            self.line.setdefault((0, dh), []).append(k.send(own, to, k.chip(0, dh)))
 
     def sibling(self, own):
         self.twin.append(self.k.send(own, self.part(), self.k.sib))
@@ -466,6 +474,9 @@
     ]
     for copy in loads:
         copy.start()
+    k.meet()
+    h_gather = ZGather(k, h_s, rows, hidden_hbm)
+    aw.lanes(wq_hbm, slice(0, QW))
     for copy in loads[10:12]:
         copy.wait()
     gains_s[mine, :, :R] = ga_ref[...].astype(F32).reshape(1, R)
@@ -474,11 +485,10 @@
         copy.wait()
     own_w[:, QW:] = kvw_ref[...].astype(F32).T.astype(BF)
     own_o[...] = wo_ref[...].astype(F32).T.astype(BF)
-    k.meet()
-    h_gather = ZGather(k, h_s, rows, hidden_hbm)
     own_gain = gains_s.at[mine]
     gain_copies = [k.send(own_gain, own_gain, dev) for dev in k.plane_peers()]
-    aw.first(own_w)
+    aw.lanes(own_w.at[:, QW:], slice(QW, QKV))
+    aw.sibling(own_w)
     ow.first(own_o)
 
     def gain_row(which):

time: 196 us -> 197 us (level)
  no operation moved by 1% of the time
where the time goes in v9:
time: 197 us; the launch traced here: 196 us
  Pallas kernels  196 us (99%)
    pallas_call x1, Pallas kernels, layer(): pl.pallas_call(functools.partial(layer_kernel, sizes, hd), out_shape=(S((...  191 us
    pallas_call x1, Pallas kernels, final(): pl.pallas_call(functools.partial(final_kernel, hd), grid=(steps,), out_sh...  4.53 us

profile of v9, /device:TPU:0, one launch (start us, length us, event | category | flops | bytes accessed | tf_op | source)
XLA Modules:
  0.0 196.4 jit_solution(9101688631016309984)
XLA Ops:
  0.6 191.1 %layer.1 = (bf16[64,2048]{1,0:T(8,128)(2,1)}, f32[64,2048]{1,0:T(8,128)}, f32[1,512]{1,0:T(1,128)}, bf16[3,256,1408]{2,1,0:T(8,128)(2,1)}, bf16[3,256,1408]{2,1,...) custom-call(s32[1,1024]{1,0:T(1,128)} %seg_hbm.1, ...), custom_call_target="tpu_custom_call" | custom-call | tf_op jit(solution)/shard_map/layer/pallas_call | solution.py:840
  191.8 4.5 %final.1 = (bf16[64,2048]{1,0:T(8,128)(2,1)}, f32[64,2048]{1,0:T(8,128)}, f32[256]{0:T(256)}, f32[256]{0:T(256)}, f32[256,512]{1,0:T(8,128)}, /*index=5*/f32[64,...) custom-call(bf16[64,2048]{1,0:T(8,128)(2,1)} %get-tuple-element.30.o, ...), custom_call_target="tpu_custom_call" | custom-call | tf_op jit(solution)/shard_map/final/pallas_call | solution.py:918
